TPU v7x, 32 devices: a whole 2x2x4 slice. The times are simulated.
32 devices in a mesh: group: 1, expert: 32 (over z, y, x, core).
Axes of the slice: x: 2, y: 2, z: 4, core: 2. Of those that a mesh axis runs over, the one named last changes fastest.
Arguments:
- hidden_state: bfloat16 [256, 2048], P(('group', 'expert')), may hold values from -6 to 6
- cross_query: bfloat16 [256, 2048], P(('group', 'expert')), may hold values from -62 to 62
- source_keys: bfloat16 [256, 64, 2048], P(('group', 'expert')), may hold values from -3 to 3
- source_values: bfloat16 [256, 64, 2048], P(('group', 'expert')), may hold values from -6 to 6
- src_lengths: int32 [256], P(('group', 'expert')), may hold values from 2 to 64
- norm_gain: float32 [2048], replicated, may hold values from 0.5 to 1.5
- w_in: bfloat16 [2048, 16384], P(None, 'expert'), may hold values from -0.125 to 0.125
- w_out: bfloat16 [16384, 2048], P('expert'), may hold values from -0.09375 to 0.09375
- expert_ids: int32 [256, 2], P(('group', 'expert')), may hold values from 0 to 3, all different within a row; in each aligned block of 8 rows (0 to 7, 8 to 15, ...) at most 8 rows name the same one
- route_weights: float32 [256, 2], P(('group', 'expert')), may hold values from 0.2 to 1
Outputs:
- layer_out: bfloat16 [256, 2048], P(('group', 'expert'))
Inputs may be any that keep to these rules, and one draw needn't show every extreme that they name: `expert_ids`: each row names two different experts. Among the rows of one device (aligned blocks of 8 streams) no expert is named by more than 8 rows, and in every draw some expert is named by exactly 8 rows of some device.
All inputs are finite; a program needn't handle non-finite values.
Results may differ from a plain program's by a relative error of at most 0.0042.
Values may be sent and summed in bfloat16 or wider, within the bound.
No kernel may reach another device: no remote copies, remote signals or barrier semaphores. Data moves between devices by JAX's collectives and lax.ppermute only.
A program may use at most 64 MiB of HBM per device.

v0:
```python
import jax
import jax.numpy as jnp
from jax import lax
from jax.experimental import pallas as pl
from jax.experimental.pallas import tpu as pltpu
from jax.sharding import PartitionSpec as P

HEADS = 16
SPLIT = 8
CORES = 2
PIECES = 4
VMEM_LIMIT = 16 * 1024 * 1024


def swap(value, distance, devices):
    pairs = [(source, source ^ distance) for source in range(devices)]
    return lax.ppermute(value, "expert", pairs)


def outer_exchange(blocks, devices):
    moved = lax.all_to_all(
        jnp.stack(blocks),
        "expert",
        split_axis=0,
        concat_axis=0,
        tiled=True,
        axis_index_groups=[list(range(inner, devices, SPLIT)) for inner in range(SPLIT)],
    )
    return [moved[index] for index in range(len(blocks))]


def far_first(count):
    return list(range(count - 1, 0, -1))


def attend_kernel(lengths_in, hidden_in, query_in, keys, values, gain_in, mixed, normed, lengths, hidden, query, gain, key_buf, value_buf, score_buf, small_sem, key_sem, value_sem):
    streams, width = hidden.shape
    span = key_buf.shape[1]
    head_size = width // HEADS
    group = key_buf.shape[0] // PIECES
    small = [
        pltpu.make_async_copy(query_in, query, small_sem.at[0]),
        pltpu.make_async_copy(lengths_in, lengths, small_sem.at[1]),
        pltpu.make_async_copy(hidden_in, hidden, small_sem.at[2]),
        pltpu.make_async_copy(gain_in, gain, small_sem.at[3]),
    ]
    pieces = [pl.ds(piece * group, group) for piece in range(PIECES)]
    key_copies = [pltpu.make_async_copy(keys.at[p], key_buf.at[p], key_sem.at[i]) for i, p in enumerate(pieces)]
    value_copies = [pltpu.make_async_copy(values.at[p], value_buf.at[p], value_sem.at[i]) for i, p in enumerate(pieces)]
    for copy in small + key_copies + value_copies:
        copy.start()
    owner = lax.broadcasted_iota(jnp.int32, (HEADS, width), 1) // head_size
    own = owner == lax.broadcasted_iota(jnp.int32, (HEADS, width), 0)
    position = lax.broadcasted_iota(jnp.int32, (HEADS, span), 1)
    small[0].wait()
    small[1].wait()
    for b in range(streams):
        if b % group == 0:
            key_copies[b // group].wait()
        spread = jnp.where(own, query[b : b + 1, :].astype(jnp.float32), 0.0).astype(jnp.bfloat16)
        scores = lax.dot_general(spread, key_buf[b], (((1,), (1,)), ((), ())), preferred_element_type=jnp.float32)
        scores = scores / jnp.sqrt(jnp.float32(head_size))
        score_buf[b * HEADS : (b + 1) * HEADS, :] = jnp.where(position < lengths[b], scores, -1e30)
    scores = score_buf[...]
    expo = jnp.exp(scores - jnp.max(scores, axis=-1, keepdims=True))
    score_buf[...] = expo / jnp.sum(expo, axis=-1, keepdims=True)
    for b in range(streams):
        if b % group == 0:
            value_copies[b // group].wait()
        probabilities = score_buf[b * HEADS : (b + 1) * HEADS, :].astype(jnp.bfloat16)
        every = jnp.dot(probabilities, value_buf[b], preferred_element_type=jnp.float32)
        for h in range(HEADS):
            lanes = slice(h * head_size, (h + 1) * head_size)
            mixed[b : b + 1, lanes] = every[h : h + 1, lanes]
    small[2].wait()
    small[3].wait()
    total = hidden[...].astype(jnp.float32) + mixed[...]
    mixed[...] = total
    centered = total - jnp.mean(total, axis=-1, keepdims=True)
    variance = jnp.mean(centered * centered, axis=-1, keepdims=True)
    normed[...] = (centered * lax.rsqrt(variance + 1e-05) * gain[...]).astype(jnp.bfloat16)


def attend(hidden_state, cross_query, source_keys, source_values, src_lengths, norm_gain):
    streams, width = hidden_state.shape
    span = source_keys.shape[1]
    arrays = (
        src_lengths,
        hidden_state,
        cross_query,
        source_keys,
        source_values,
        norm_gain.reshape(1, width),
    )
    vmem = pl.BlockSpec(memory_space=pltpu.VMEM)
    hbm = pl.BlockSpec(memory_space=pltpu.HBM)
    return pl.pallas_call(
        attend_kernel,
        out_shape=(jax.ShapeDtypeStruct((streams, width), jnp.float32), jax.ShapeDtypeStruct((streams, width), jnp.bfloat16)),
        in_specs=[hbm]*6,
        out_specs=(vmem, vmem),
        scratch_shapes=[
            pltpu.SMEM((streams,), jnp.int32),
            pltpu.VMEM((streams, width), hidden_state.dtype),
            pltpu.VMEM((streams, width), cross_query.dtype),
            pltpu.VMEM((1, width), norm_gain.dtype),
            pltpu.VMEM((streams, span, width), source_keys.dtype),
            pltpu.VMEM((streams, span, width), source_values.dtype),
            pltpu.VMEM((streams * HEADS, span), jnp.float32),
            pltpu.SemaphoreType.DMA((4,)),
            pltpu.SemaphoreType.DMA((PIECES,)),
            pltpu.SemaphoreType.DMA((PIECES,)),
        ],
        compiler_params=pltpu.CompilerParams(vmem_limit_bytes=VMEM_LIMIT),
    )(*[pltpu.with_memory_space_constraint(array, pltpu.HBM) for array in arrays])


def step_on_device(
    hidden_state,
    cross_query,
    source_keys,
    source_values,
    src_lengths,
    norm_gain,
    w_in,
    w_out,
    expert_ids,
    route_weights,
):
    streams, width = hidden_state.shape
    devices = lax.axis_size("expert")
    experts_count = devices // SPLIT
    capacity = max(2, min(streams, 4 * streams * SPLIT // devices))
    direct = experts_count <= 4
    mixed, normed = attend(
        hidden_state, cross_query, source_keys, source_values, src_lengths, norm_gain
    )
    group = lax.axis_index("expert") // SPLIT
    order = jnp.arange(experts_count, dtype=jnp.int32)
    if direct:
        order = order ^ group
    chosen = expert_ids[:, :, None] == order[None, None, :]
    weights = jnp.sum(jnp.where(chosen, route_weights[:, :, None], 0.0), axis=1)
    if capacity >= streams:
        blocks = [normed] * experts_count
    else:
        named = jnp.any(chosen, axis=1).astype(jnp.int32)
        rank = jnp.cumsum(named, axis=0) - named
        slots = jnp.arange(capacity, dtype=jnp.int32)
        placed = (named == 1)[None, :, :] & (rank[None, :, :] == slots[:, None, None])
        packed = jnp.einsum(
            "ctk,td->kcd",
            placed.astype(jnp.bfloat16),
            normed,
            preferred_element_type=jnp.float32,
        ).astype(jnp.bfloat16)
        blocks = [packed[index] for index in range(experts_count)]
    chips = SPLIT // CORES
    steps = far_first(chips)
    distances = far_first(experts_count)
    if direct:
        planes = {k: swap(blocks[k], k * SPLIT, devices) for k in distances}
        first = [blocks[0]]
        rest = [planes[k] for k in range(1, experts_count)]
    else:
        first = outer_exchange(blocks, devices)
        rest = []
    first, *others = [jnp.concatenate(part, axis=0) for part in (first, rest) if part]
    near = {0: [first] + others}
    early = {step: swap(first, CORES * step, devices) for step in steps}
    late = {step: [swap(part, CORES * step, devices) for part in others] for step in steps}
    for step in steps:
        near[step] = [early[step]] + late[step]
    far = {step: [swap(part, 1, devices) for part in near[step]] for step in range(chips)}
    order = [(step, place) for step in range(chips) for place in range(1 + len(others))]

    spans = {}
    count = 0
    for step, place in order:
        spans[step, place] = (count, near[step][place].shape[0])
        count += near[step][place].shape[0]
    rows = [near[step][place] for step, place in order] + [far[step][place] for step, place in order]
    units = jnp.dot(jnp.concatenate(rows, axis=0), w_in, preferred_element_type=jnp.float32)
    act = lax.optimization_barrier(jnp.maximum(units, 0.0).astype(jnp.bfloat16))
    far_sent = jnp.dot(act[count:], w_out, preferred_element_type=jnp.float32).astype(jnp.bfloat16)
    near_every = jnp.dot(act[:count], w_out, preferred_element_type=jnp.float32)
    near_every = lax.optimization_barrier(near_every)

    def of(every, step, place):
        start, length = spans[step, place]
        return every[start : start + length]

    pair = {
        (step, place): of(near_every, step, place)
        + swap(of(far_sent, step, place), 1, devices).astype(jnp.float32)
        for step, place in order
    }

    def chip_sum(place):
        total = pair[0, place]
        for step in steps:
            sent = pair[step, place].astype(jnp.bfloat16)
            total = total + swap(sent, CORES * step, devices).astype(jnp.float32)
        return total

    result = mixed
    if direct:
        away = chip_sum(1).reshape(experts_count - 1, capacity, width)
        back = {k: swap(away[k - 1].astype(jnp.bfloat16), k * SPLIT, devices) for k in distances}
        own = chip_sum(0)
        parts = [own] + [back[k].astype(jnp.float32) for k in range(1, experts_count)]
    else:
        total = chip_sum(0).astype(jnp.bfloat16)
        total = total.reshape(experts_count, capacity, width)
        back = outer_exchange([total[k] for k in range(experts_count)], devices)
        parts = [part.astype(jnp.float32) for part in back]
    for k, part in enumerate(parts):
        if capacity < streams:
            part = jnp.einsum(
                "ct,cd->td",
                placed[:, :, k].astype(jnp.float32),
                part,
                precision=lax.Precision.HIGHEST,
                preferred_element_type=jnp.float32,
            )
        result = result + weights[:, k : k + 1] * part
    return result.astype(jnp.bfloat16)


def solution(mesh):
    placed = (
        P(("group", "expert"), None),
        P(("group", "expert"), None),
        P(("group", "expert"), None, None),
        P(("group", "expert"), None, None),
        P(("group", "expert")),
        P(),
        P(None, "expert"),
        P("expert", None),
        P(("group", "expert"), None),
        P(("group", "expert"), None),
    )
    return jax.shard_map(
        step_on_device,
        mesh=mesh,
        in_specs=placed,
        out_specs=P(("group", "expert"), None),
        check_vma=False,
    )
```

profile of v0, /device:TPU:0, one launch (start us, length us, event | category | flops | bytes accessed | tf_op | source)
XLA Modules:
  0.0 49.7 jit_solution(4059031560409837118)
XLA Ops:
  0.0 3.7 %shard_map.100 = (f32[8,2048]{1,0:T(8,128)S(1)}, bf16[8,2048]{1,0:T(8,128)(2,1)S(1)}) custom-call(s32[8]{0:T(128)} %lengths_in.1, bf16[8,2048]{1,0:T(8,128)(2,1)} %hidden_in.1, bf16[8,2048]{1,0:T(8,128)(2,1)} %query_in.1, bf16[8,64,2048]{2,1,0:T(8,128)(2,1)} %keys.1, bf16[8,64,2048]{2,1,0:T(8,128)(2,1)} %values.1, f32[1,2048]{1,0:T(1,128)} %bitcast.13), custom_call_target="tpu_custom_call" | custom-call | tf_op jit(solution)/shard_map/pallas_call | solution.py:97
  3.7 3.1 %collective-permute-start = (bf16[8,2048]{1,0:T(8,128)(2,1)S(1)}, bf16[8,2048]{1,0:T(8,128)(2,1)S(1)}, u32[]{:S(2)}, u32[]{:S(2)}) collective-permute-start(bf16[8,2048]{1,0:T(8,128)(2,1)S(1)} %get-tuple-element.8), channel_id=1, source_target_pairs={{0,8},{1,9},{2,10},{3,11},{4,12},{5,13},{6,14},{7,15},{8,0},{9,1},... | collective-permute-start | bytes 98312 | tf_op jit(solution)/shard_map/ppermute | solution.py:17
  6.8 2.6 %collective-permute-start.1 = (bf16[8,2048]{1,0:T(8,128)(2,1)S(1)}, bf16[8,2048]{1,0:T(8,128)(2,1)S(1)}, u32[]{:S(2)}, u32[]{:S(2)}) collective-permute-start(bf16[8,2048]{1,0:T(8,128)(2,1)S(1)} %get-tuple-element.8), channel_id=1, source_target_pairs={{0,16},{1,17},{2,18},{3,19},{4,20},{5,21},{6,22},{7,23},{8,24},{9,... | collective-permute-start | bytes 98312 | tf_op jit(solution)/shard_map/ppermute | solution.py:17
  9.4 1.7 %collective-permute-start.3 = (bf16[8,2048]{1,0:T(8,128)(2,1)S(1)}, bf16[8,2048]{1,0:T(8,128)(2,1)S(1)}, u32[]{:S(2)}, u32[]{:S(2)}) collective-permute-start(bf16[8,2048]{1,0:T(8,128)(2,1)S(1)} %get-tuple-element.8), channel_id=1, source_target_pairs={{0,2},{1,3},{2,0},{3,1},{4,6},{5,7},{6,4},{7,5},{8,10},{9,11},{10,... | collective-permute-start | bytes 98312 | tf_op jit(solution)/shard_map/ppermute | solution.py:17
  11.1 1.5 %collective-permute-start.5 = (bf16[8,2048]{1,0:T(8,128)(2,1)S(1)}, bf16[8,2048]{1,0:T(8,128)(2,1)S(1)}, u32[]{:S(2)}, u32[]{:S(2)}) collective-permute-start(bf16[8,2048]{1,0:T(8,128)(2,1)S(1)} %get-tuple-element.8), channel_id=1, source_target_pairs={{0,4},{1,5},{2,6},{3,7},{4,0},{5,1},{6,2},{7,3},{8,12},{9,13},{10,... | collective-permute-start | bytes 98312 | tf_op jit(solution)/shard_map/ppermute | solution.py:17
  13.1 2.0 %collective-permute-done.2 = bf16[8,2048]{1,0:T(8,128)(2,1)S(1)} collective-permute-done((bf16[8,2048]{1,0:T(8,128)(2,1)S(1)}, bf16[8,2048]{1,0:T(8,128)(2,1)S(1)}, u32[]{:S(2)}, u32[]{:S(2)}) %collective-permute-start.2) | collective-permute-done | bytes 32800 | tf_op jit(solution)/shard_map/ppermute | solution.py:17
  15.1 1.5 %collective-permute-start.4 = (bf16[24,2048]{1,0:T(8,128)(2,1)S(1)}, bf16[24,2048]{1,0:T(8,128)(2,1)S(1)}, u32[]{:S(2)}, u32[]{:S(2)}) collective-permute-start(bf16[24,2048]{1,0:T(8,128)(2,1)S(1)} %get-tuple-element.26), channel_id=1, source_target_pairs={{0,2},{1,3},{2,0},{3,1},{4,6},{5,7},{6,4},{7,5},{8,10},{9,11},{10,... | collective-permute-start | bytes 294920 | tf_op jit(solution)/shard_map/ppermute | solution.py:17
  16.6 1.5 %collective-permute-start.6 = (bf16[24,2048]{1,0:T(8,128)(2,1)S(1)}, bf16[24,2048]{1,0:T(8,128)(2,1)S(1)}, u32[]{:S(2)}, u32[]{:S(2)}) collective-permute-start(bf16[24,2048]{1,0:T(8,128)(2,1)S(1)} %get-tuple-element.26), channel_id=1, source_target_pairs={{0,4},{1,5},{2,6},{3,7},{4,0},{5,1},{6,2},{7,3},{8,12},{9,13},{10,... | collective-permute-start | bytes 294920 | tf_op jit(solution)/shard_map/ppermute | solution.py:17
  18.1 1.6 %collective-permute-done.4 = bf16[24,2048]{1,0:T(8,128)(2,1)S(1)} collective-permute-done((bf16[24,2048]{1,0:T(8,128)(2,1)S(1)}, bf16[24,2048]{1,0:T(8,128)(2,1)S(1)}, u32[]{:S(2)}, u32[]{:S(2)}) %collective-permute-start.4) | collective-permute-done | bytes 98336 | tf_op jit(solution)/shard_map/ppermute | solution.py:17
  19.7 2.4 %collective-permute-start.8 = (bf16[24,2048]{1,0:T(8,128)(2,1)S(1)}, bf16[24,2048]{1,0:T(8,128)(2,1)S(1)}, u32[]{:S(2)}, u32[]{:S(2)}) collective-permute-start(bf16[24,2048]{1,0:T(8,128)(2,1)S(1)} %get-tuple-element.26), channel_id=1, source_target_pairs={{0,6},{1,7},{2,4},{3,5},{4,2},{5,3},{6,0},{7,1},{8,14},{9,15},{10,... | collective-permute-start | bytes 294920 | tf_op jit(solution)/shard_map/ppermute | solution.py:17
  22.3 0.5 collective-permute-start.11
  23.0 2.3 %collective-permute-done.8 = bf16[24,2048]{1,0:T(8,128)(2,1)S(1)} collective-permute-done((bf16[24,2048]{1,0:T(8,128)(2,1)S(1)}, bf16[24,2048]{1,0:T(8,128)(2,1)S(1)}, u32[]{:S(2)}, u32[]{:S(2)}) %collective-permute-start.8) | collective-permute-done | bytes 98336 | tf_op jit(solution)/shard_map/ppermute | solution.py:17
  25.3 0.6 %collective-permute-start.12 = (bf16[24,2048]{1,0:T(8,128)(2,1)S(1)}, bf16[24,2048]{1,0:T(8,128)(2,1)S(1)}, u32[]{:S(2)}, u32[]{:S(2)}) collective-permute-start(bf16[24,2048]{1,0:T(8,128)(2,1)S(1)} %collective-permute-done.4), channel_id=1, source_target_pairs={{0,1},{1,0},{2,3},{3,2},{4,5},{5,4},{6,7},{7,6},{8,9},{9,8},{10,11... | collective-permute-start | bytes 294920 | tf_op jit(solution)/shard_map/ppermute | solution.py:17
  26.0 0.5 collective-permute-start.16
  27.4 0.7 %fusion = bf16[256,512]{1,0:T(8,128)(2,1)S(1)} fusion(bf16[256,2048]{1,0:T(8,128)(2,1)S(1)} %constant_dynamic-update-slice_fusion.3, bf16[2048,512]{1,0:T(8,128)(2,1)S(1)} %copy-done.3), kind=kOutput, calls=%fused_computation.2 | convolution fusion | flops 537133056 | bytes 3407872 | tf_op jit(solution)/shard_map/dot_general | solution.py:183
  28.2 0.4 convolution_convert_fusion
  28.7 0.4 collective-permute-start.25
  29.2 0.4 collective-permute-start.27
  29.6 0.4 fusion.9
  30.8 0.4 collective-permute-start.20
  31.5 1.5 %collective-permute-start.30 = (bf16[24,2048]{1,0:T(8,128)(2,1)S(1)}, bf16[24,2048]{1,0:T(8,128)(2,1)S(1)}, u32[]{:S(2)}, u32[]{:S(2)}) collective-permute-start(bf16[24,2048]{1,0:T(8,128)(2,1)S(1)} %get-tuple-element.13), channel_id=1, source_target_pairs={{0,2},{1,3},{2,0},{3,1},{4,6},{5,7},{6,4},{7,5},{8,10},{9,11},{10,... | collective-permute-start | bytes 294920 | tf_op jit(solution)/shard_map/ppermute | solution.py:17
  33.0 1.5 %collective-permute-start.28 = (bf16[24,2048]{1,0:T(8,128)(2,1)S(1)}, bf16[24,2048]{1,0:T(8,128)(2,1)S(1)}, u32[]{:S(2)}, u32[]{:S(2)}) collective-permute-start(bf16[24,2048]{1,0:T(8,128)(2,1)S(1)} %get-tuple-element.14), channel_id=1, source_target_pairs={{0,4},{1,5},{2,6},{3,7},{4,0},{5,1},{6,2},{7,3},{8,12},{9,13},{10,... | collective-permute-start | bytes 294920 | tf_op jit(solution)/shard_map/ppermute | solution.py:17
  34.5 0.5 collective-permute-start.26
  35.0 1.6 %collective-permute-start.23 = (bf16[8,2048]{1,0:T(8,128)(2,1)S(1)}, bf16[8,2048]{1,0:T(8,128)(2,1)S(1)}, u32[]{:S(2)}, u32[]{:S(2)}) collective-permute-start(bf16[8,2048]{1,0:T(8,128)(2,1)S(1)} %get-tuple-element.10), channel_id=1, source_target_pairs={{0,2},{1,3},{2,0},{3,1},{4,6},{5,7},{6,4},{7,5},{8,10},{9,11},{10,... | collective-permute-start | bytes 98312 | tf_op jit(solution)/shard_map/ppermute | solution.py:17
  36.6 1.5 %collective-permute-start.21 = (bf16[8,2048]{1,0:T(8,128)(2,1)S(1)}, bf16[8,2048]{1,0:T(8,128)(2,1)S(1)}, u32[]{:S(2)}, u32[]{:S(2)}) collective-permute-start(bf16[8,2048]{1,0:T(8,128)(2,1)S(1)} %get-tuple-element.11), channel_id=1, source_target_pairs={{0,4},{1,5},{2,6},{3,7},{4,0},{5,1},{6,2},{7,3},{8,12},{9,13},{10,... | collective-permute-start | bytes 98312 | tf_op jit(solution)/shard_map/ppermute | solution.py:17
  38.1 1.1 %collective-permute-done.28 = bf16[24,2048]{1,0:T(8,128)(2,1)S(1)} collective-permute-done((bf16[24,2048]{1,0:T(8,128)(2,1)S(1)}, bf16[24,2048]{1,0:T(8,128)(2,1)S(1)}, u32[]{:S(2)}, u32[]{:S(2)}) %collective-permute-start.28) | collective-permute-done | bytes 98336 | tf_op jit(solution)/shard_map/ppermute | solution.py:17
  39.3 1.8 %collective-permute-start.19 = (bf16[8,2048]{1,0:T(8,128)(2,1)S(1)}, bf16[8,2048]{1,0:T(8,128)(2,1)S(1)}, u32[]{:S(2)}, u32[]{:S(2)}) collective-permute-start(bf16[8,2048]{1,0:T(8,128)(2,1)S(1)} %get-tuple-element.9), channel_id=1, source_target_pairs={{0,6},{1,7},{2,4},{3,5},{4,2},{5,3},{6,0},{7,1},{8,14},{9,15},{10,... | collective-permute-start | bytes 98312 | tf_op jit(solution)/shard_map/ppermute | solution.py:17
  41.1 3.1 %collective-permute-start.33 = (bf16[8,2048]{1,0:T(8,128)(2,1)S(1)}, bf16[8,2048]{1,0:T(8,128)(2,1)S(1)}, u32[]{:S(2)}, u32[]{:S(2)}) collective-permute-start(bf16[8,2048]{1,0:T(8,128)(2,1)S(1)} %get-tuple-element.24), channel_id=1, source_target_pairs={{0,24},{1,25},{2,26},{3,27},{4,28},{5,29},{6,30},{7,31},{8,16},{9,... | collective-permute-start | bytes 98312 | tf_op jit(solution)/shard_map/ppermute | solution.py:17
  44.2 1.4 %collective-permute-start.31 = (bf16[8,2048]{1,0:T(8,128)(2,1)S(1)}, bf16[8,2048]{1,0:T(8,128)(2,1)S(1)}, u32[]{:S(2)}, u32[]{:S(2)}) collective-permute-start(bf16[8,2048]{1,0:T(8,128)(2,1)S(1)} %get-tuple-element.23), channel_id=1, source_target_pairs={{0,8},{1,9},{2,10},{3,11},{4,12},{5,13},{6,14},{7,15},{8,0},{9,1},... | collective-permute-start | bytes 98312 | tf_op jit(solution)/shard_map/ppermute | solution.py:17
  45.6 1.3 %collective-permute-done.33 = bf16[8,2048]{1,0:T(8,128)(2,1)S(1)} collective-permute-done((bf16[8,2048]{1,0:T(8,128)(2,1)S(1)}, bf16[8,2048]{1,0:T(8,128)(2,1)S(1)}, u32[]{:S(2)}, u32[]{:S(2)}) %collective-permute-start.33) | collective-permute-done | bytes 32800 | tf_op jit(solution)/shard_map/ppermute | solution.py:17
  46.9 2.1 %collective-permute-done.32 = bf16[8,2048]{1,0:T(8,128)(2,1)S(1)} collective-permute-done((bf16[8,2048]{1,0:T(8,128)(2,1)S(1)}, bf16[8,2048]{1,0:T(8,128)(2,1)S(1)}, u32[]{:S(2)}, u32[]{:S(2)}) %collective-permute-start.32) | collective-permute-done | bytes 32800 | tf_op jit(solution)/shard_map/ppermute | solution.py:17
  49.0 0.7 %fusion.22 = bf16[8,2048]{1,0:T(8,128)(2,1)} fusion(f32[8,2048]{1,0:T(8,128)S(1)} %get-tuple-element.7, f32[128,2048]{1,0:T(8,128)S(1)} %fusion.9, bf16[8,2048]{1,0:T(8,128)(2,1)S(1)} %collective-permute-done.33, bf16[8,2048]{1,0:T(8,128)(2,1)S(1)} %collective-permute-done.32, bf16[8,2048]{1,0:T(8,128)(2,1)S(1)} %collective-permute-done.31, ...), kind=kLoop, calls=%fused_computation.32 | loop fusion | flops 327680 | bytes 393344 | tf_op jit(solution)/shard_map/convert_element_type | solution.py:227
  (76 shorter events, 3.2 us)
Async XLA Ops:
  3.7 9.1 %collective-permute-start = (bf16[8,2048]{1,0:T(8,128)(2,1)S(1)}, bf16[8,2048]{1,0:T(8,128)(2,1)S(1)}, u32[]{:S(2)}, u32[]{:S(2)}) collective-permute-start(bf16[8,2048]{1,0:T(8,128)(2,1)S(1)} %get-tuple-element.8), channel_id=1, source_target_pairs={{0,8},{1,9},{2,10},{3,11},{4,12},{5,13},{6,14},{7,15},{8,0},{9,1},... | collective-permute-start | bytes 98312 | tf_op jit(solution)/shard_map/ppermute | solution.py:17
  6.8 6.2 %collective-permute-start.1 = (bf16[8,2048]{1,0:T(8,128)(2,1)S(1)}, bf16[8,2048]{1,0:T(8,128)(2,1)S(1)}, u32[]{:S(2)}, u32[]{:S(2)}) collective-permute-start(bf16[8,2048]{1,0:T(8,128)(2,1)S(1)} %get-tuple-element.8), channel_id=1, source_target_pairs={{0,16},{1,17},{2,18},{3,19},{4,20},{5,21},{6,22},{7,23},{8,24},{9,... | collective-permute-start | bytes 98312 | tf_op jit(solution)/shard_map/ppermute | solution.py:17
  9.4 5.7 %collective-permute-start.2 = (bf16[8,2048]{1,0:T(8,128)(2,1)S(1)}, bf16[8,2048]{1,0:T(8,128)(2,1)S(1)}, u32[]{:S(2)}, u32[]{:S(2)}) collective-permute-start(bf16[8,2048]{1,0:T(8,128)(2,1)S(1)} %get-tuple-element.8), channel_id=1, source_target_pairs={{0,24},{1,25},{2,26},{3,27},{4,28},{5,29},{6,30},{7,31},{8,16},{9,... | collective-permute-start | bytes 98312 | tf_op jit(solution)/shard_map/ppermute | solution.py:17
  9.4 7.2 %collective-permute-start.3 = (bf16[8,2048]{1,0:T(8,128)(2,1)S(1)}, bf16[8,2048]{1,0:T(8,128)(2,1)S(1)}, u32[]{:S(2)}, u32[]{:S(2)}) collective-permute-start(bf16[8,2048]{1,0:T(8,128)(2,1)S(1)} %get-tuple-element.8), channel_id=1, source_target_pairs={{0,2},{1,3},{2,0},{3,1},{4,6},{5,7},{6,4},{7,5},{8,10},{9,11},{10,... | collective-permute-start | bytes 98312 | tf_op jit(solution)/shard_map/ppermute | solution.py:17
  11.1 11.1 %collective-permute-start.5 = (bf16[8,2048]{1,0:T(8,128)(2,1)S(1)}, bf16[8,2048]{1,0:T(8,128)(2,1)S(1)}, u32[]{:S(2)}, u32[]{:S(2)}) collective-permute-start(bf16[8,2048]{1,0:T(8,128)(2,1)S(1)} %get-tuple-element.8), channel_id=1, source_target_pairs={{0,4},{1,5},{2,6},{3,7},{4,0},{5,1},{6,2},{7,3},{8,12},{9,13},{10,... | collective-permute-start | bytes 98312 | tf_op jit(solution)/shard_map/ppermute | solution.py:17
  12.8 10.0 %collective-permute-start.7 = (bf16[8,2048]{1,0:T(8,128)(2,1)S(1)}, bf16[8,2048]{1,0:T(8,128)(2,1)S(1)}, u32[]{:S(2)}, u32[]{:S(2)}) collective-permute-start(bf16[8,2048]{1,0:T(8,128)(2,1)S(1)} %get-tuple-element.8), channel_id=1, source_target_pairs={{0,6},{1,7},{2,4},{3,5},{4,2},{5,3},{6,0},{7,1},{8,14},{9,15},{10,... | collective-permute-start | bytes 98312 | tf_op jit(solution)/shard_map/ppermute | solution.py:17
  13.0 12.2 %collective-permute-start.9 = (bf16[8,2048]{1,0:T(8,128)(2,1)S(1)}, bf16[8,2048]{1,0:T(8,128)(2,1)S(1)}, u32[]{:S(2)}, u32[]{:S(2)}) collective-permute-start(bf16[8,2048]{1,0:T(8,128)(2,1)S(1)} %get-tuple-element.8), channel_id=1, source_target_pairs={{0,1},{1,0},{2,3},{3,2},{4,5},{5,4},{6,7},{7,6},{8,9},{9,8},{10,11... | collective-permute-start | bytes 98312 | tf_op jit(solution)/shard_map/ppermute | solution.py:17
  15.1 4.6 %collective-permute-start.4 = (bf16[24,2048]{1,0:T(8,128)(2,1)S(1)}, bf16[24,2048]{1,0:T(8,128)(2,1)S(1)}, u32[]{:S(2)}, u32[]{:S(2)}) collective-permute-start(bf16[24,2048]{1,0:T(8,128)(2,1)S(1)} %get-tuple-element.26), channel_id=1, source_target_pairs={{0,2},{1,3},{2,0},{3,1},{4,6},{5,7},{6,4},{7,5},{8,10},{9,11},{10,... | collective-permute-start | bytes 294920 | tf_op jit(solution)/shard_map/ppermute | solution.py:17
  16.6 5.7 %collective-permute-start.6 = (bf16[24,2048]{1,0:T(8,128)(2,1)S(1)}, bf16[24,2048]{1,0:T(8,128)(2,1)S(1)}, u32[]{:S(2)}, u32[]{:S(2)}) collective-permute-start(bf16[24,2048]{1,0:T(8,128)(2,1)S(1)} %get-tuple-element.26), channel_id=1, source_target_pairs={{0,4},{1,5},{2,6},{3,7},{4,0},{5,1},{6,2},{7,3},{8,12},{9,13},{10,... | collective-permute-start | bytes 294920 | tf_op jit(solution)/shard_map/ppermute | solution.py:17
  19.7 5.5 %collective-permute-start.8 = (bf16[24,2048]{1,0:T(8,128)(2,1)S(1)}, bf16[24,2048]{1,0:T(8,128)(2,1)S(1)}, u32[]{:S(2)}, u32[]{:S(2)}) collective-permute-start(bf16[24,2048]{1,0:T(8,128)(2,1)S(1)} %get-tuple-element.26), channel_id=1, source_target_pairs={{0,6},{1,7},{2,4},{3,5},{4,2},{5,3},{6,0},{7,1},{8,14},{9,15},{10,... | collective-permute-start | bytes 294920 | tf_op jit(solution)/shard_map/ppermute | solution.py:17
  22.2 3.7 %collective-permute-start.10 = (bf16[24,2048]{1,0:T(8,128)(2,1)S(1)}, bf16[24,2048]{1,0:T(8,128)(2,1)S(1)}, u32[]{:S(2)}, u32[]{:S(2)}) collective-permute-start(bf16[24,2048]{1,0:T(8,128)(2,1)S(1)} %get-tuple-element.26), channel_id=1, source_target_pairs={{0,1},{1,0},{2,3},{3,2},{4,5},{5,4},{6,7},{7,6},{8,9},{9,8},{10,11... | collective-permute-start | bytes 294920 | tf_op jit(solution)/shard_map/ppermute | solution.py:17
  22.3 3.7 %collective-permute-start.11 = (bf16[8,2048]{1,0:T(8,128)(2,1)S(1)}, bf16[8,2048]{1,0:T(8,128)(2,1)S(1)}, u32[]{:S(2)}, u32[]{:S(2)}) collective-permute-start(bf16[8,2048]{1,0:T(8,128)(2,1)S(1)} %collective-permute-done.3), channel_id=1, source_target_pairs={{0,1},{1,0},{2,3},{3,2},{4,5},{5,4},{6,7},{7,6},{8,9},{9,8},{10,11... | collective-permute-start | bytes 98312 | tf_op jit(solution)/shard_map/ppermute | solution.py:17
  22.8 4.0 %collective-permute-start.13 = (bf16[8,2048]{1,0:T(8,128)(2,1)S(1)}, bf16[8,2048]{1,0:T(8,128)(2,1)S(1)}, u32[]{:S(2)}, u32[]{:S(2)}) collective-permute-start(bf16[8,2048]{1,0:T(8,128)(2,1)S(1)} %collective-permute-done.5), channel_id=1, source_target_pairs={{0,1},{1,0},{2,3},{3,2},{4,5},{5,4},{6,7},{7,6},{8,9},{9,8},{10,11... | collective-permute-start | bytes 98312 | tf_op jit(solution)/shard_map/ppermute | solution.py:17
  25.3 1.9 %collective-permute-start.15 = (bf16[8,2048]{1,0:T(8,128)(2,1)S(1)}, bf16[8,2048]{1,0:T(8,128)(2,1)S(1)}, u32[]{:S(2)}, u32[]{:S(2)}) collective-permute-start(bf16[8,2048]{1,0:T(8,128)(2,1)S(1)} %collective-permute-done.7), channel_id=1, source_target_pairs={{0,1},{1,0},{2,3},{3,2},{4,5},{5,4},{6,7},{7,6},{8,9},{9,8},{10,11... | collective-permute-start | bytes 98312 | tf_op jit(solution)/shard_map/ppermute | solution.py:17
  25.3 1.5 %collective-permute-start.12 = (bf16[24,2048]{1,0:T(8,128)(2,1)S(1)}, bf16[24,2048]{1,0:T(8,128)(2,1)S(1)}, u32[]{:S(2)}, u32[]{:S(2)}) collective-permute-start(bf16[24,2048]{1,0:T(8,128)(2,1)S(1)} %collective-permute-done.4), channel_id=1, source_target_pairs={{0,1},{1,0},{2,3},{3,2},{4,5},{5,4},{6,7},{7,6},{8,9},{9,8},{10,11... | collective-permute-start | bytes 294920 | tf_op jit(solution)/shard_map/ppermute | solution.py:17
  26.0 1.4 %collective-permute-start.16 = (bf16[24,2048]{1,0:T(8,128)(2,1)S(1)}, bf16[24,2048]{1,0:T(8,128)(2,1)S(1)}, u32[]{:S(2)}, u32[]{:S(2)}) collective-permute-start(bf16[24,2048]{1,0:T(8,128)(2,1)S(1)} %collective-permute-done.8), channel_id=1, source_target_pairs={{0,1},{1,0},{2,3},{3,2},{4,5},{5,4},{6,7},{7,6},{8,9},{9,8},{10,11... | collective-permute-start | bytes 294920 | tf_op jit(solution)/shard_map/ppermute | solution.py:17
  28.7 2.0 %collective-permute-start.25 = (bf16[24,2048]{1,0:T(8,128)(2,1)S(1)}, bf16[24,2048]{1,0:T(8,128)(2,1)S(1)}, u32[]{:S(2)}, u32[]{:S(2)}) collective-permute-start(bf16[24,2048]{1,0:T(8,128)(2,1)S(1)} %get-tuple-element.22), channel_id=1, source_target_pairs={{0,1},{1,0},{2,3},{3,2},{4,5},{5,4},{6,7},{7,6},{8,9},{9,8},{10,11... | collective-permute-start | bytes 294920 | tf_op jit(solution)/shard_map/ppermute | solution.py:17
  29.1 1.7 %collective-permute-start.29 = (bf16[24,2048]{1,0:T(8,128)(2,1)S(1)}, bf16[24,2048]{1,0:T(8,128)(2,1)S(1)}, u32[]{:S(2)}, u32[]{:S(2)}) collective-permute-start(bf16[24,2048]{1,0:T(8,128)(2,1)S(1)} %get-tuple-element.20), channel_id=1, source_target_pairs={{0,1},{1,0},{2,3},{3,2},{4,5},{5,4},{6,7},{7,6},{8,9},{9,8},{10,11... | collective-permute-start | bytes 294920 | tf_op jit(solution)/shard_map/ppermute | solution.py:17
  29.2 1.9 %collective-permute-start.27 = (bf16[24,2048]{1,0:T(8,128)(2,1)S(1)}, bf16[24,2048]{1,0:T(8,128)(2,1)S(1)}, u32[]{:S(2)}, u32[]{:S(2)}) collective-permute-start(bf16[24,2048]{1,0:T(8,128)(2,1)S(1)} %get-tuple-element.21), channel_id=1, source_target_pairs={{0,1},{1,0},{2,3},{3,2},{4,5},{5,4},{6,7},{7,6},{8,9},{9,8},{10,11... | collective-permute-start | bytes 294920 | tf_op jit(solution)/shard_map/ppermute | solution.py:17
  30.1 5.0 %collective-permute-start.24 = (bf16[24,2048]{1,0:T(8,128)(2,1)S(1)}, bf16[24,2048]{1,0:T(8,128)(2,1)S(1)}, u32[]{:S(2)}, u32[]{:S(2)}) collective-permute-start(bf16[24,2048]{1,0:T(8,128)(2,1)S(1)} %get-tuple-element.19), channel_id=1, source_target_pairs={{0,1},{1,0},{2,3},{3,2},{4,5},{5,4},{6,7},{7,6},{8,9},{9,8},{10,11... | collective-permute-start | bytes 294920 | tf_op jit(solution)/shard_map/ppermute | solution.py:17
  30.6 2.4 %collective-permute-start.22 = (bf16[8,2048]{1,0:T(8,128)(2,1)S(1)}, bf16[8,2048]{1,0:T(8,128)(2,1)S(1)}, u32[]{:S(2)}, u32[]{:S(2)}) collective-permute-start(bf16[8,2048]{1,0:T(8,128)(2,1)S(1)} %get-tuple-element.16), channel_id=1, source_target_pairs={{0,1},{1,0},{2,3},{3,2},{4,5},{5,4},{6,7},{7,6},{8,9},{9,8},{10,11... | collective-permute-start | bytes 98312 | tf_op jit(solution)/shard_map/ppermute | solution.py:17
  30.8 3.7 %collective-permute-start.20 = (bf16[8,2048]{1,0:T(8,128)(2,1)S(1)}, bf16[8,2048]{1,0:T(8,128)(2,1)S(1)}, u32[]{:S(2)}, u32[]{:S(2)}) collective-permute-start(bf16[8,2048]{1,0:T(8,128)(2,1)S(1)} %get-tuple-element.17), channel_id=1, source_target_pairs={{0,1},{1,0},{2,3},{3,2},{4,5},{5,4},{6,7},{7,6},{8,9},{9,8},{10,11... | collective-permute-start | bytes 98312 | tf_op jit(solution)/shard_map/ppermute | solution.py:17
  31.1 13.0 %collective-permute-start.17 = (bf16[8,2048]{1,0:T(8,128)(2,1)S(1)}, bf16[8,2048]{1,0:T(8,128)(2,1)S(1)}, u32[]{:S(2)}, u32[]{:S(2)}) collective-permute-start(bf16[8,2048]{1,0:T(8,128)(2,1)S(1)} %get-tuple-element.15), channel_id=1, source_target_pairs={{0,1},{1,0},{2,3},{3,2},{4,5},{5,4},{6,7},{7,6},{8,9},{9,8},{10,11... | collective-permute-start | bytes 98312 | tf_op jit(solution)/shard_map/ppermute | solution.py:17
  31.5 5.1 %collective-permute-start.30 = (bf16[24,2048]{1,0:T(8,128)(2,1)S(1)}, bf16[24,2048]{1,0:T(8,128)(2,1)S(1)}, u32[]{:S(2)}, u32[]{:S(2)}) collective-permute-start(bf16[24,2048]{1,0:T(8,128)(2,1)S(1)} %get-tuple-element.13), channel_id=1, source_target_pairs={{0,2},{1,3},{2,0},{3,1},{4,6},{5,7},{6,4},{7,5},{8,10},{9,11},{10,... | collective-permute-start | bytes 294920 | tf_op jit(solution)/shard_map/ppermute | solution.py:17
  33.0 6.3 %collective-permute-start.28 = (bf16[24,2048]{1,0:T(8,128)(2,1)S(1)}, bf16[24,2048]{1,0:T(8,128)(2,1)S(1)}, u32[]{:S(2)}, u32[]{:S(2)}) collective-permute-start(bf16[24,2048]{1,0:T(8,128)(2,1)S(1)} %get-tuple-element.14), channel_id=1, source_target_pairs={{0,4},{1,5},{2,6},{3,7},{4,0},{5,1},{6,2},{7,3},{8,12},{9,13},{10,... | collective-permute-start | bytes 294920 | tf_op jit(solution)/shard_map/ppermute | solution.py:17
  34.5 6.5 %collective-permute-start.26 = (bf16[24,2048]{1,0:T(8,128)(2,1)S(1)}, bf16[24,2048]{1,0:T(8,128)(2,1)S(1)}, u32[]{:S(2)}, u32[]{:S(2)}) collective-permute-start(bf16[24,2048]{1,0:T(8,128)(2,1)S(1)} %get-tuple-element.12), channel_id=1, source_target_pairs={{0,6},{1,7},{2,4},{3,5},{4,2},{5,3},{6,0},{7,1},{8,14},{9,15},{10,... | collective-permute-start | bytes 294920 | tf_op jit(solution)/shard_map/ppermute | solution.py:17
  35.0 9.2 %collective-permute-start.23 = (bf16[8,2048]{1,0:T(8,128)(2,1)S(1)}, bf16[8,2048]{1,0:T(8,128)(2,1)S(1)}, u32[]{:S(2)}, u32[]{:S(2)}) collective-permute-start(bf16[8,2048]{1,0:T(8,128)(2,1)S(1)} %get-tuple-element.10), channel_id=1, source_target_pairs={{0,2},{1,3},{2,0},{3,1},{4,6},{5,7},{6,4},{7,5},{8,10},{9,11},{10,... | collective-permute-start | bytes 98312 | tf_op jit(solution)/shard_map/ppermute | solution.py:17
  36.6 9.0 %collective-permute-start.21 = (bf16[8,2048]{1,0:T(8,128)(2,1)S(1)}, bf16[8,2048]{1,0:T(8,128)(2,1)S(1)}, u32[]{:S(2)}, u32[]{:S(2)}) collective-permute-start(bf16[8,2048]{1,0:T(8,128)(2,1)S(1)} %get-tuple-element.11), channel_id=1, source_target_pairs={{0,4},{1,5},{2,6},{3,7},{4,0},{5,1},{6,2},{7,3},{8,12},{9,13},{10,... | collective-permute-start | bytes 98312 | tf_op jit(solution)/shard_map/ppermute | solution.py:17
  39.3 6.3 %collective-permute-start.19 = (bf16[8,2048]{1,0:T(8,128)(2,1)S(1)}, bf16[8,2048]{1,0:T(8,128)(2,1)S(1)}, u32[]{:S(2)}, u32[]{:S(2)}) collective-permute-start(bf16[8,2048]{1,0:T(8,128)(2,1)S(1)} %get-tuple-element.9), channel_id=1, source_target_pairs={{0,6},{1,7},{2,4},{3,5},{4,2},{5,3},{6,0},{7,1},{8,14},{9,15},{10,... | collective-permute-start | bytes 98312 | tf_op jit(solution)/shard_map/ppermute | solution.py:17
  41.1 5.8 %collective-permute-start.33 = (bf16[8,2048]{1,0:T(8,128)(2,1)S(1)}, bf16[8,2048]{1,0:T(8,128)(2,1)S(1)}, u32[]{:S(2)}, u32[]{:S(2)}) collective-permute-start(bf16[8,2048]{1,0:T(8,128)(2,1)S(1)} %get-tuple-element.24), channel_id=1, source_target_pairs={{0,24},{1,25},{2,26},{3,27},{4,28},{5,29},{6,30},{7,31},{8,16},{9,... | collective-permute-start | bytes 98312 | tf_op jit(solution)/shard_map/ppermute | solution.py:17
  44.2 4.8 %collective-permute-start.32 = (bf16[8,2048]{1,0:T(8,128)(2,1)S(1)}, bf16[8,2048]{1,0:T(8,128)(2,1)S(1)}, u32[]{:S(2)}, u32[]{:S(2)}) collective-permute-start(bf16[8,2048]{1,0:T(8,128)(2,1)S(1)} %get-tuple-element.25), channel_id=1, source_target_pairs={{0,16},{1,17},{2,18},{3,19},{4,20},{5,21},{6,22},{7,23},{8,24},{9,... | collective-permute-start | bytes 98312 | tf_op jit(solution)/shard_map/ppermute | solution.py:17
  44.2 4.8 %collective-permute-start.31 = (bf16[8,2048]{1,0:T(8,128)(2,1)S(1)}, bf16[8,2048]{1,0:T(8,128)(2,1)S(1)}, u32[]{:S(2)}, u32[]{:S(2)}) collective-permute-start(bf16[8,2048]{1,0:T(8,128)(2,1)S(1)} %get-tuple-element.23), channel_id=1, source_target_pairs={{0,8},{1,9},{2,10},{3,11},{4,12},{5,13},{6,14},{7,15},{8,0},{9,1},... | collective-permute-start | bytes 98312 | tf_op jit(solution)/shard_map/ppermute | solution.py:17
  (6 other events, 70.7 us)
where the time goes:
time: 49.9 us; the launch traced here: 49.7 us
  starting transfers between devices  31.6 us (63%)
  waiting for transfers between devices  11.5 us (23%)
  Pallas kernels  3.68 us (7%)
  matrix products  1.62 us (3%)
  other arithmetic  0.94 us (2%)
    ppermute x34, starting transfers between devices, swap(): return lax.ppermute(value, 'expert', pairs)  31.6 us
    ppermute x34, waiting for transfers between devices, swap(): return lax.ppermute(value, 'expert', pairs)  11.5 us
    pallas_call x1, Pallas kernels, attend(): pl.pallas_call(attend_kernel, out_shape=(jax.ShapeDtypeStruct((streams, w...  3.68 us
  transfers between devices with their start and end apart: 34, of which 10 were waited for; matrix products, arithmetic and copies ran while one was open for 2% of the time, Pallas kernels for 0%

commit v1 on v0

--- a/solution.py
+++ b/solution.py
@@ -160,59 +160,38 @@
     distances = far_first(experts_count)
     if direct:
         planes = {k: swap(blocks[k], k * SPLIT, devices) for k in distances}
-        first = [blocks[0]]
-        rest = [planes[k] for k in range(1, experts_count)]
+        column = [blocks[0]] + [planes[k] for k in range(1, experts_count)]
     else:
-        first = outer_exchange(blocks, devices)
-        rest = []
-    first, *others = [jnp.concatenate(part, axis=0) for part in (first, rest) if part]
-    near = {0: [first] + others}
-    early = {step: swap(first, CORES * step, devices) for step in steps}
-    late = {step: [swap(part, CORES * step, devices) for part in others] for step in steps}
-    for step in steps:
-        near[step] = [early[step]] + late[step]
-    far = {step: [swap(part, 1, devices) for part in near[step]] for step in range(chips)}
-    order = [(step, place) for step in range(chips) for place in range(1 + len(others))]
-
-    spans = {}
-    count = 0
-    for step, place in order:
-        spans[step, place] = (count, near[step][place].shape[0])
-        count += near[step][place].shape[0]
-    rows = [near[step][place] for step, place in order] + [far[step][place] for step, place in order]
+        column = outer_exchange(blocks, devices)
+    near = {0: jnp.concatenate(column, axis=0)}
+    count = near[0].shape[0]
+    for step in range(1, chips):
+        near[step] = swap(near[0], CORES * step, devices)
+    far = {step: swap(near[step], 1, devices) for step in range(chips)}
+    rows = [near[step] for step in range(chips)] + [far[step] for step in range(chips)]
+    half = chips * count
     units = jnp.dot(jnp.concatenate(rows, axis=0), w_in, preferred_element_type=jnp.float32)
     act = lax.optimization_barrier(jnp.maximum(units, 0.0).astype(jnp.bfloat16))
-    far_sent = jnp.dot(act[count:], w_out, preferred_element_type=jnp.float32).astype(jnp.bfloat16)
-    near_every = jnp.dot(act[:count], w_out, preferred_element_type=jnp.float32)
+    far_sent = jnp.dot(act[half:], w_out, preferred_element_type=jnp.float32).astype(jnp.bfloat16)
+    near_every = jnp.dot(act[:half], w_out, preferred_element_type=jnp.float32)
     near_every = lax.optimization_barrier(near_every)
-
-    def of(every, step, place):
-        start, length = spans[step, place]
-        return every[start : start + length]
-
-    pair = {
-        (step, place): of(near_every, step, place)
-        + swap(of(far_sent, step, place), 1, devices).astype(jnp.float32)
-        for step, place in order
-    }
-
-    def chip_sum(place):
-        total = pair[0, place]
-        for step in steps:
-            sent = pair[step, place].astype(jnp.bfloat16)
-            total = total + swap(sent, CORES * step, devices).astype(jnp.float32)
-        return total
-
+    pair = {}
+    for step in steps + [0]:
+        place = slice(step * count, (step + 1) * count)
+        given = swap(far_sent[place], 1, devices)
+        pair[step] = near_every[place] + given.astype(jnp.float32)
+    total = pair[0]
+    for step in steps:
+        sent = pair[step].astype(jnp.bfloat16)
+        total = total + swap(sent, CORES * step, devices).astype(jnp.float32)
+    total = total.reshape(experts_count, capacity, width)
     result = mixed
+    sent = total.astype(jnp.bfloat16)
     if direct:
-        away = chip_sum(1).reshape(experts_count - 1, capacity, width)
-        back = {k: swap(away[k - 1].astype(jnp.bfloat16), k * SPLIT, devices) for k in distances}
-        own = chip_sum(0)
-        parts = [own] + [back[k].astype(jnp.float32) for k in range(1, experts_count)]
+        back = {k: swap(sent[k], k * SPLIT, devices) for k in distances}
+        parts = [total[0]] + [back[k].astype(jnp.float32) for k in range(1, experts_count)]
     else:
-        total = chip_sum(0).astype(jnp.bfloat16)
-        total = total.reshape(experts_count, capacity, width)
-        back = outer_exchange([total[k] for k in range(experts_count)], devices)
+        back = outer_exchange([sent[k] for k in range(experts_count)], devices)
         parts = [part.astype(jnp.float32) for part in back]
     for k, part in enumerate(parts):
         if capacity < streams:

time: 49.9 us -> 46.6 us (0.934)
  starting transfers between devices: 31.6 us -> 18.4 us
  waiting for transfers between devices: 11.5 us -> 19.9 us
  matrix products: 1.62 us -> 3.18 us
    ppermute x34 -> x20, starting transfers between devices: 31.6 us -> 18.4 us  [swap(): return lax.ppermute(value, 'expert', pairs)]
    ppermute x34 -> x20, waiting for transfers between devices: 11.5 us -> 19.9 us  [swap(): return lax.ppermute(value, 'expert', pairs)]
    dot_general x1, matrix products: 0.73 us -> 2.29 us  [step_on_device(): jnp.dot(jnp.concatenate(rows, axis=0), w_in, preferred_element_type=jnp.f...]
  transfers between devices with their start and end apart: 34 -> 20, of which waited for: 10 -> 11; matrix products, arithmetic and copies ran while one was open for 2% -> 2% of each run, Pallas kernels for 0% -> 0%
where the time goes in v1:
time: 46.6 us; the launch traced here: 46.5 us
  waiting for transfers between devices  19.9 us (43%)
  starting transfers between devices  18.4 us (39%)
  Pallas kernels  3.69 us (8%)
  matrix products  3.18 us (7%)
  other arithmetic  0.97 us (2%)
    ppermute x20, waiting for transfers between devices, swap(): return lax.ppermute(value, 'expert', pairs)  19.9 us
    ppermute x20, starting transfers between devices, swap(): return lax.ppermute(value, 'expert', pairs)  18.4 us
    pallas_call x1, Pallas kernels, attend(): pl.pallas_call(attend_kernel, out_shape=(jax.ShapeDtypeStruct((streams, w...  3.69 us
    dot_general x1, matrix products, step_on_device(): jnp.dot(jnp.concatenate(rows, axis=0), w_in, preferred_element_type=jnp.f...  2.29 us
  transfers between devices with their start and end apart: 20, of which 11 were waited for; matrix products, arithmetic and copies ran while one was open for 2% of the time, Pallas kernels for 0%

profile of v1, /device:TPU:0, one launch (start us, length us, event | category | flops | bytes accessed | tf_op | source)
XLA Modules:
  0.0 46.5 jit_solution(9795513593741453757)
XLA Ops:
  0.0 3.7 %shard_map.100 = (f32[8,2048]{1,0:T(8,128)S(1)}, bf16[8,2048]{1,0:T(8,128)(2,1)S(1)}) custom-call(s32[8]{0:T(128)} %lengths_in.1, bf16[8,2048]{1,0:T(8,128)(2,1)} %hidden_in.1, bf16[8,2048]{1,0:T(8,128)(2,1)} %query_in.1, bf16[8,64,2048]{2,1,0:T(8,128)(2,1)} %keys.1, bf16[8,64,2048]{2,1,0:T(8,128)(2,1)} %values.1, f32[1,2048]{1,0:T(1,128)} %bitcast.13), custom_call_target="tpu_custom_call" | custom-call | tf_op jit(solution)/shard_map/pallas_call | solution.py:97
  3.7 3.1 %collective-permute-start = (bf16[8,2048]{1,0:T(8,128)(2,1)S(1)}, bf16[8,2048]{1,0:T(8,128)(2,1)S(1)}, u32[]{:S(2)}, u32[]{:S(2)}) collective-permute-start(bf16[8,2048]{1,0:T(8,128)(2,1)S(1)} %get-tuple-element.8), channel_id=1, source_target_pairs={{0,8},{1,9},{2,10},{3,11},{4,12},{5,13},{6,14},{7,15},{8,0},{9,1},... | collective-permute-start | bytes 98312 | tf_op jit(solution)/shard_map/ppermute | solution.py:17
  6.8 2.6 %collective-permute-start.1 = (bf16[8,2048]{1,0:T(8,128)(2,1)S(1)}, bf16[8,2048]{1,0:T(8,128)(2,1)S(1)}, u32[]{:S(2)}, u32[]{:S(2)}) collective-permute-start(bf16[8,2048]{1,0:T(8,128)(2,1)S(1)} %get-tuple-element.8), channel_id=1, source_target_pairs={{0,16},{1,17},{2,18},{3,19},{4,20},{5,21},{6,22},{7,23},{8,24},{9,... | collective-permute-start | bytes 98312 | tf_op jit(solution)/shard_map/ppermute | solution.py:17
  9.4 2.8 %collective-permute-done.1 = bf16[8,2048]{1,0:T(8,128)(2,1)S(1)} collective-permute-done((bf16[8,2048]{1,0:T(8,128)(2,1)S(1)}, bf16[8,2048]{1,0:T(8,128)(2,1)S(1)}, u32[]{:S(2)}, u32[]{:S(2)}) %collective-permute-start.1) | collective-permute-done | bytes 32800 | tf_op jit(solution)/shard_map/ppermute | solution.py:17
  12.2 2.9 %collective-permute-done.2 = bf16[8,2048]{1,0:T(8,128)(2,1)S(1)} collective-permute-done((bf16[8,2048]{1,0:T(8,128)(2,1)S(1)}, bf16[8,2048]{1,0:T(8,128)(2,1)S(1)}, u32[]{:S(2)}, u32[]{:S(2)}) %collective-permute-start.2) | collective-permute-done | bytes 32800 | tf_op jit(solution)/shard_map/ppermute | solution.py:17
  15.1 1.5 %collective-permute-start.3 = (bf16[32,2048]{1,0:T(8,128)(2,1)S(1)}, bf16[32,2048]{1,0:T(8,128)(2,1)S(1)}, u32[]{:S(2)}, u32[]{:S(2)}) collective-permute-start(bf16[32,2048]{1,0:T(8,128)(2,1)S(1)} %get-tuple-element.21), channel_id=1, source_target_pairs={{0,2},{1,3},{2,0},{3,1},{4,6},{5,7},{6,4},{7,5},{8,10},{9,11},{10,... | collective-permute-start | bytes 393224 | tf_op jit(solution)/shard_map/ppermute | solution.py:17
  16.6 1.5 %collective-permute-start.4 = (bf16[32,2048]{1,0:T(8,128)(2,1)S(1)}, bf16[32,2048]{1,0:T(8,128)(2,1)S(1)}, u32[]{:S(2)}, u32[]{:S(2)}) collective-permute-start(bf16[32,2048]{1,0:T(8,128)(2,1)S(1)} %get-tuple-element.21), channel_id=1, source_target_pairs={{0,4},{1,5},{2,6},{3,7},{4,0},{5,1},{6,2},{7,3},{8,12},{9,13},{10,... | collective-permute-start | bytes 393224 | tf_op jit(solution)/shard_map/ppermute | solution.py:17
  18.1 0.5 %collective-permute-start.5 = (bf16[32,2048]{1,0:T(8,128)(2,1)S(1)}, bf16[32,2048]{1,0:T(8,128)(2,1)S(1)}, u32[]{:S(2)}, u32[]{:S(2)}) collective-permute-start(bf16[32,2048]{1,0:T(8,128)(2,1)S(1)} %get-tuple-element.21), channel_id=1, source_target_pairs={{0,6},{1,7},{2,4},{3,5},{4,2},{5,3},{6,0},{7,1},{8,14},{9,15},{10,... | collective-permute-start | bytes 393224 | tf_op jit(solution)/shard_map/ppermute | solution.py:17
  18.6 2.5 %collective-permute-done.3 = bf16[32,2048]{1,0:T(8,128)(2,1)S(1)} collective-permute-done((bf16[32,2048]{1,0:T(8,128)(2,1)S(1)}, bf16[32,2048]{1,0:T(8,128)(2,1)S(1)}, u32[]{:S(2)}, u32[]{:S(2)}) %collective-permute-start.3) | collective-permute-done | bytes 131104 | tf_op jit(solution)/shard_map/ppermute | solution.py:17
  21.2 1.2 %collective-permute-done.4 = bf16[32,2048]{1,0:T(8,128)(2,1)S(1)} collective-permute-done((bf16[32,2048]{1,0:T(8,128)(2,1)S(1)}, bf16[32,2048]{1,0:T(8,128)(2,1)S(1)}, u32[]{:S(2)}, u32[]{:S(2)}) %collective-permute-start.4) | collective-permute-done | bytes 131104 | tf_op jit(solution)/shard_map/ppermute | solution.py:17
  22.4 1.6 %collective-permute-done.5 = bf16[32,2048]{1,0:T(8,128)(2,1)S(1)} collective-permute-done((bf16[32,2048]{1,0:T(8,128)(2,1)S(1)}, bf16[32,2048]{1,0:T(8,128)(2,1)S(1)}, u32[]{:S(2)}, u32[]{:S(2)}) %collective-permute-start.5) | collective-permute-done | bytes 131104 | tf_op jit(solution)/shard_map/ppermute | solution.py:17
  24.1 1.2 %collective-permute-done.9 = bf16[32,2048]{1,0:T(8,128)(2,1)S(1)} collective-permute-done((bf16[32,2048]{1,0:T(8,128)(2,1)S(1)}, bf16[32,2048]{1,0:T(8,128)(2,1)S(1)}, u32[]{:S(2)}, u32[]{:S(2)}) %collective-permute-start.9) | collective-permute-done | bytes 131104 | tf_op jit(solution)/shard_map/ppermute | solution.py:17
  25.4 2.3 %fusion = bf16[256,512]{1,0:T(8,128)(2,1)S(1)} fusion(bf16[256,2048]{1,0:T(8,128)(2,1)S(1)} %constant_dynamic-update-slice_fusion.4, bf16[2048,512]{1,0:T(8,128)(2,1)} %param.16), kind=kOutput, calls=%fused_computation.2 | convolution fusion | flops 537133056 | bytes 3407872 | tf_op jit(solution)/shard_map/dot_general | solution.py:173
  27.7 0.4 convolution_convert_fusion
  28.2 0.2 collective-permute-start.11
  28.4 0.4 collective-permute-start.15
  28.8 0.1 collective-permute-start.13
  28.9 0.4 fusion.8
  29.4 0.4 collective-permute-start.10
  29.8 0.3 collective-permute-done.13
  30.1 0.1 fusion.3
  30.2 0.6 %collective-permute-start.16 = (bf16[32,2048]{1,0:T(8,128)(2,1)S(1)}, bf16[32,2048]{1,0:T(8,128)(2,1)S(1)}, u32[]{:S(2)}, u32[]{:S(2)}) collective-permute-start(bf16[32,2048]{1,0:T(8,128)(2,1)S(1)} %get-tuple-element.12), channel_id=1, source_target_pairs={{0,2},{1,3},{2,0},{3,1},{4,6},{5,7},{6,4},{7,5},{8,10},{9,11},{10,... | collective-permute-start | bytes 393224 | tf_op jit(solution)/shard_map/ppermute | solution.py:17
  30.8 0.6 %collective-permute-start.14 = (bf16[32,2048]{1,0:T(8,128)(2,1)S(1)}, bf16[32,2048]{1,0:T(8,128)(2,1)S(1)}, u32[]{:S(2)}, u32[]{:S(2)}) collective-permute-start(bf16[32,2048]{1,0:T(8,128)(2,1)S(1)} %get-tuple-element.13), channel_id=1, source_target_pairs={{0,4},{1,5},{2,6},{3,7},{4,0},{5,1},{6,2},{7,3},{8,12},{9,13},{10,... | collective-permute-start | bytes 393224 | tf_op jit(solution)/shard_map/ppermute | solution.py:17
  31.4 2.4 %collective-permute-start.12 = (bf16[32,2048]{1,0:T(8,128)(2,1)S(1)}, bf16[32,2048]{1,0:T(8,128)(2,1)S(1)}, u32[]{:S(2)}, u32[]{:S(2)}) collective-permute-start(bf16[32,2048]{1,0:T(8,128)(2,1)S(1)} %get-tuple-element.11), channel_id=1, source_target_pairs={{0,6},{1,7},{2,4},{3,5},{4,2},{5,3},{6,0},{7,1},{8,14},{9,15},{10,... | collective-permute-start | bytes 393224 | tf_op jit(solution)/shard_map/ppermute | solution.py:17
  33.9 2.8 %collective-permute-done.16 = bf16[32,2048]{1,0:T(8,128)(2,1)S(1)} collective-permute-done((bf16[32,2048]{1,0:T(8,128)(2,1)S(1)}, bf16[32,2048]{1,0:T(8,128)(2,1)S(1)}, u32[]{:S(2)}, u32[]{:S(2)}) %collective-permute-start.16) | collective-permute-done | bytes 131104 | tf_op jit(solution)/shard_map/ppermute | solution.py:17
  36.6 2.7 %collective-permute-done.12 = bf16[32,2048]{1,0:T(8,128)(2,1)S(1)} collective-permute-done((bf16[32,2048]{1,0:T(8,128)(2,1)S(1)}, bf16[32,2048]{1,0:T(8,128)(2,1)S(1)}, u32[]{:S(2)}, u32[]{:S(2)}) %collective-permute-start.12) | collective-permute-done | bytes 131104 | tf_op jit(solution)/shard_map/ppermute | solution.py:17
  39.3 0.1 fusion.15
  39.4 0.6 %collective-permute-start.19 = (bf16[8,2048]{1,0:T(8,128)(2,1)S(1)}, bf16[8,2048]{1,0:T(8,128)(2,1)S(1)}, u32[]{:S(2)}, u32[]{:S(2)}) collective-permute-start(bf16[8,2048]{1,0:T(8,128)(2,1)S(1)} %get-tuple-element.19), channel_id=1, source_target_pairs={{0,24},{1,25},{2,26},{3,27},{4,28},{5,29},{6,30},{7,31},{8,16},{9,... | collective-permute-start | bytes 98312 | tf_op jit(solution)/shard_map/ppermute | solution.py:17
  40.1 3.8 %collective-permute-start.17 = (bf16[8,2048]{1,0:T(8,128)(2,1)S(1)}, bf16[8,2048]{1,0:T(8,128)(2,1)S(1)}, u32[]{:S(2)}, u32[]{:S(2)}) collective-permute-start(bf16[8,2048]{1,0:T(8,128)(2,1)S(1)} %get-tuple-element.18), channel_id=1, source_target_pairs={{0,8},{1,9},{2,10},{3,11},{4,12},{5,13},{6,14},{7,15},{8,0},{9,1},... | collective-permute-start | bytes 98312 | tf_op jit(solution)/shard_map/ppermute | solution.py:17
  43.9 1.3 %collective-permute-done.19 = bf16[8,2048]{1,0:T(8,128)(2,1)S(1)} collective-permute-done((bf16[8,2048]{1,0:T(8,128)(2,1)S(1)}, bf16[8,2048]{1,0:T(8,128)(2,1)S(1)}, u32[]{:S(2)}, u32[]{:S(2)}) %collective-permute-start.19) | collective-permute-done | bytes 32800 | tf_op jit(solution)/shard_map/ppermute | solution.py:17
  45.2 0.6 %collective-permute-done.17 = bf16[8,2048]{1,0:T(8,128)(2,1)S(1)} collective-permute-done((bf16[8,2048]{1,0:T(8,128)(2,1)S(1)}, bf16[8,2048]{1,0:T(8,128)(2,1)S(1)}, u32[]{:S(2)}, u32[]{:S(2)}) %collective-permute-start.17) | collective-permute-done | bytes 32800 | tf_op jit(solution)/shard_map/ppermute | solution.py:17
  45.8 0.7 %fusion.14 = bf16[8,2048]{1,0:T(8,128)(2,1)} fusion(f32[8,2048]{1,0:T(8,128)S(1)} %get-tuple-element.7, f32[32,2048]{1,0:T(8,128)S(1)} %get-tuple-element.10, bf16[8,2048]{1,0:T(8,128)(2,1)S(1)} %collective-permute-done.19, bf16[8,2048]{1,0:T(8,128)(2,1)S(1)} %collective-permute-done.18, bf16[8,2048]{1,0:T(8,128)(2,1)S(1)} %collective-permute-done.17, ...), kind=kLoop, calls=%fused_computation.21 | loop fusion | flops 196608 | bytes 262272 | tf_op jit(solution)/shard_map/convert_element_type | solution.py:206
  (37 shorter events, 0.3 us)
Async XLA Ops:
  0.0 27.7 %copy-start = (bf16[512,2048]{1,0:T(8,128)(2,1)S(1)}, bf16[512,2048]{1,0:T(8,128)(2,1)}, u32[]{:S(2)}) copy-start(bf16[512,2048]{1,0:T(8,128)(2,1)} %param.17) | copy-start | bytes 6291460
  3.7 5.7 %collective-permute-start = (bf16[8,2048]{1,0:T(8,128)(2,1)S(1)}, bf16[8,2048]{1,0:T(8,128)(2,1)S(1)}, u32[]{:S(2)}, u32[]{:S(2)}) collective-permute-start(bf16[8,2048]{1,0:T(8,128)(2,1)S(1)} %get-tuple-element.8), channel_id=1, source_target_pairs={{0,8},{1,9},{2,10},{3,11},{4,12},{5,13},{6,14},{7,15},{8,0},{9,1},... | collective-permute-start | bytes 98312 | tf_op jit(solution)/shard_map/ppermute | solution.py:17
  6.8 5.4 %collective-permute-start.1 = (bf16[8,2048]{1,0:T(8,128)(2,1)S(1)}, bf16[8,2048]{1,0:T(8,128)(2,1)S(1)}, u32[]{:S(2)}, u32[]{:S(2)}) collective-permute-start(bf16[8,2048]{1,0:T(8,128)(2,1)S(1)} %get-tuple-element.8), channel_id=1, source_target_pairs={{0,16},{1,17},{2,18},{3,19},{4,20},{5,21},{6,22},{7,23},{8,24},{9,... | collective-permute-start | bytes 98312 | tf_op jit(solution)/shard_map/ppermute | solution.py:17
  9.4 5.7 %collective-permute-start.2 = (bf16[8,2048]{1,0:T(8,128)(2,1)S(1)}, bf16[8,2048]{1,0:T(8,128)(2,1)S(1)}, u32[]{:S(2)}, u32[]{:S(2)}) collective-permute-start(bf16[8,2048]{1,0:T(8,128)(2,1)S(1)} %get-tuple-element.8), channel_id=1, source_target_pairs={{0,24},{1,25},{2,26},{3,27},{4,28},{5,29},{6,30},{7,31},{8,16},{9,... | collective-permute-start | bytes 98312 | tf_op jit(solution)/shard_map/ppermute | solution.py:17
  15.1 6.0 %collective-permute-start.3 = (bf16[32,2048]{1,0:T(8,128)(2,1)S(1)}, bf16[32,2048]{1,0:T(8,128)(2,1)S(1)}, u32[]{:S(2)}, u32[]{:S(2)}) collective-permute-start(bf16[32,2048]{1,0:T(8,128)(2,1)S(1)} %get-tuple-element.21), channel_id=1, source_target_pairs={{0,2},{1,3},{2,0},{3,1},{4,6},{5,7},{6,4},{7,5},{8,10},{9,11},{10,... | collective-permute-start | bytes 393224 | tf_op jit(solution)/shard_map/ppermute | solution.py:17
  16.6 5.8 %collective-permute-start.4 = (bf16[32,2048]{1,0:T(8,128)(2,1)S(1)}, bf16[32,2048]{1,0:T(8,128)(2,1)S(1)}, u32[]{:S(2)}, u32[]{:S(2)}) collective-permute-start(bf16[32,2048]{1,0:T(8,128)(2,1)S(1)} %get-tuple-element.21), channel_id=1, source_target_pairs={{0,4},{1,5},{2,6},{3,7},{4,0},{5,1},{6,2},{7,3},{8,12},{9,13},{10,... | collective-permute-start | bytes 393224 | tf_op jit(solution)/shard_map/ppermute | solution.py:17
  18.1 5.9 %collective-permute-start.5 = (bf16[32,2048]{1,0:T(8,128)(2,1)S(1)}, bf16[32,2048]{1,0:T(8,128)(2,1)S(1)}, u32[]{:S(2)}, u32[]{:S(2)}) collective-permute-start(bf16[32,2048]{1,0:T(8,128)(2,1)S(1)} %get-tuple-element.21), channel_id=1, source_target_pairs={{0,6},{1,7},{2,4},{3,5},{4,2},{5,3},{6,0},{7,1},{8,14},{9,15},{10,... | collective-permute-start | bytes 393224 | tf_op jit(solution)/shard_map/ppermute | solution.py:17
  18.6 5.4 %collective-permute-start.6 = (bf16[32,2048]{1,0:T(8,128)(2,1)S(1)}, bf16[32,2048]{1,0:T(8,128)(2,1)S(1)}, u32[]{:S(2)}, u32[]{:S(2)}) collective-permute-start(bf16[32,2048]{1,0:T(8,128)(2,1)S(1)} %get-tuple-element.21), channel_id=1, source_target_pairs={{0,1},{1,0},{2,3},{3,2},{4,5},{5,4},{6,7},{7,6},{8,9},{9,8},{10,11... | collective-permute-start | bytes 393224 | tf_op jit(solution)/shard_map/ppermute | solution.py:17
  21.1 2.9 %collective-permute-start.7 = (bf16[32,2048]{1,0:T(8,128)(2,1)S(1)}, bf16[32,2048]{1,0:T(8,128)(2,1)S(1)}, u32[]{:S(2)}, u32[]{:S(2)}) collective-permute-start(bf16[32,2048]{1,0:T(8,128)(2,1)S(1)} %collective-permute-done.3), channel_id=1, source_target_pairs={{0,1},{1,0},{2,3},{3,2},{4,5},{5,4},{6,7},{7,6},{8,9},{9,8},{10,11... | collective-permute-start | bytes 393224 | tf_op jit(solution)/shard_map/ppermute | solution.py:17
  22.4 1.7 %collective-permute-start.8 = (bf16[32,2048]{1,0:T(8,128)(2,1)S(1)}, bf16[32,2048]{1,0:T(8,128)(2,1)S(1)}, u32[]{:S(2)}, u32[]{:S(2)}) collective-permute-start(bf16[32,2048]{1,0:T(8,128)(2,1)S(1)} %collective-permute-done.4), channel_id=1, source_target_pairs={{0,1},{1,0},{2,3},{3,2},{4,5},{5,4},{6,7},{7,6},{8,9},{9,8},{10,11... | collective-permute-start | bytes 393224 | tf_op jit(solution)/shard_map/ppermute | solution.py:17
  24.0 1.3 %collective-permute-start.9 = (bf16[32,2048]{1,0:T(8,128)(2,1)S(1)}, bf16[32,2048]{1,0:T(8,128)(2,1)S(1)}, u32[]{:S(2)}, u32[]{:S(2)}) collective-permute-start(bf16[32,2048]{1,0:T(8,128)(2,1)S(1)} %collective-permute-done.5), channel_id=1, source_target_pairs={{0,1},{1,0},{2,3},{3,2},{4,5},{5,4},{6,7},{7,6},{8,9},{9,8},{10,11... | collective-permute-start | bytes 393224 | tf_op jit(solution)/shard_map/ppermute | solution.py:17
  28.2 1.6 %collective-permute-start.11 = (bf16[32,2048]{1,0:T(8,128)(2,1)S(1)}, bf16[32,2048]{1,0:T(8,128)(2,1)S(1)}, u32[]{:S(2)}, u32[]{:S(2)}) collective-permute-start(bf16[32,2048]{1,0:T(8,128)(2,1)S(1)} %get-tuple-element.17), channel_id=1, source_target_pairs={{0,1},{1,0},{2,3},{3,2},{4,5},{5,4},{6,7},{7,6},{8,9},{9,8},{10,11... | collective-permute-start | bytes 393224 | tf_op jit(solution)/shard_map/ppermute | solution.py:17
  28.4 1.4 %collective-permute-start.15 = (bf16[32,2048]{1,0:T(8,128)(2,1)S(1)}, bf16[32,2048]{1,0:T(8,128)(2,1)S(1)}, u32[]{:S(2)}, u32[]{:S(2)}) collective-permute-start(bf16[32,2048]{1,0:T(8,128)(2,1)S(1)} %get-tuple-element.15), channel_id=1, source_target_pairs={{0,1},{1,0},{2,3},{3,2},{4,5},{5,4},{6,7},{7,6},{8,9},{9,8},{10,11... | collective-permute-start | bytes 393224 | tf_op jit(solution)/shard_map/ppermute | solution.py:17
  28.8 5.0 %copy-start.1 = (f32[8,2]{0,1:T(2,128)S(1)}, f32[8,2]{0,1:T(2,128)}, u32[]{:S(2)}) copy-start(f32[8,2]{0,1:T(2,128)} %param.19) | copy-start | bytes 196
  28.8 5.0 %copy-start.2 = (s32[8,2]{0,1:T(2,128)S(1)}, s32[8,2]{0,1:T(2,128)}, u32[]{:S(2)}) copy-start(s32[8,2]{0,1:T(2,128)} %param.18) | copy-start | bytes 196
  28.8 1.3 %collective-permute-start.13 = (bf16[32,2048]{1,0:T(8,128)(2,1)S(1)}, bf16[32,2048]{1,0:T(8,128)(2,1)S(1)}, u32[]{:S(2)}, u32[]{:S(2)}) collective-permute-start(bf16[32,2048]{1,0:T(8,128)(2,1)S(1)} %get-tuple-element.16), channel_id=1, source_target_pairs={{0,1},{1,0},{2,3},{3,2},{4,5},{5,4},{6,7},{7,6},{8,9},{9,8},{10,11... | collective-permute-start | bytes 393224 | tf_op jit(solution)/shard_map/ppermute | solution.py:17
  29.4 4.5 %collective-permute-start.10 = (bf16[32,2048]{1,0:T(8,128)(2,1)S(1)}, bf16[32,2048]{1,0:T(8,128)(2,1)S(1)}, u32[]{:S(2)}, u32[]{:S(2)}) collective-permute-start(bf16[32,2048]{1,0:T(8,128)(2,1)S(1)} %get-tuple-element.14), channel_id=1, source_target_pairs={{0,1},{1,0},{2,3},{3,2},{4,5},{5,4},{6,7},{7,6},{8,9},{9,8},{10,11... | collective-permute-start | bytes 393224 | tf_op jit(solution)/shard_map/ppermute | solution.py:17
  30.2 6.4 %collective-permute-start.16 = (bf16[32,2048]{1,0:T(8,128)(2,1)S(1)}, bf16[32,2048]{1,0:T(8,128)(2,1)S(1)}, u32[]{:S(2)}, u32[]{:S(2)}) collective-permute-start(bf16[32,2048]{1,0:T(8,128)(2,1)S(1)} %get-tuple-element.12), channel_id=1, source_target_pairs={{0,2},{1,3},{2,0},{3,1},{4,6},{5,7},{6,4},{7,5},{8,10},{9,11},{10,... | collective-permute-start | bytes 393224 | tf_op jit(solution)/shard_map/ppermute | solution.py:17
  30.8 5.8 %collective-permute-start.14 = (bf16[32,2048]{1,0:T(8,128)(2,1)S(1)}, bf16[32,2048]{1,0:T(8,128)(2,1)S(1)}, u32[]{:S(2)}, u32[]{:S(2)}) collective-permute-start(bf16[32,2048]{1,0:T(8,128)(2,1)S(1)} %get-tuple-element.13), channel_id=1, source_target_pairs={{0,4},{1,5},{2,6},{3,7},{4,0},{5,1},{6,2},{7,3},{8,12},{9,13},{10,... | collective-permute-start | bytes 393224 | tf_op jit(solution)/shard_map/ppermute | solution.py:17
  31.4 7.9 %collective-permute-start.12 = (bf16[32,2048]{1,0:T(8,128)(2,1)S(1)}, bf16[32,2048]{1,0:T(8,128)(2,1)S(1)}, u32[]{:S(2)}, u32[]{:S(2)}) collective-permute-start(bf16[32,2048]{1,0:T(8,128)(2,1)S(1)} %get-tuple-element.11), channel_id=1, source_target_pairs={{0,6},{1,7},{2,4},{3,5},{4,2},{5,3},{6,0},{7,1},{8,14},{9,15},{10,... | collective-permute-start | bytes 393224 | tf_op jit(solution)/shard_map/ppermute | solution.py:17
  39.4 5.8 %collective-permute-start.19 = (bf16[8,2048]{1,0:T(8,128)(2,1)S(1)}, bf16[8,2048]{1,0:T(8,128)(2,1)S(1)}, u32[]{:S(2)}, u32[]{:S(2)}) collective-permute-start(bf16[8,2048]{1,0:T(8,128)(2,1)S(1)} %get-tuple-element.19), channel_id=1, source_target_pairs={{0,24},{1,25},{2,26},{3,27},{4,28},{5,29},{6,30},{7,31},{8,16},{9,... | collective-permute-start | bytes 98312 | tf_op jit(solution)/shard_map/ppermute | solution.py:17
  40.0 5.2 %collective-permute-start.18 = (bf16[8,2048]{1,0:T(8,128)(2,1)S(1)}, bf16[8,2048]{1,0:T(8,128)(2,1)S(1)}, u32[]{:S(2)}, u32[]{:S(2)}) collective-permute-start(bf16[8,2048]{1,0:T(8,128)(2,1)S(1)} %get-tuple-element.20), channel_id=1, source_target_pairs={{0,16},{1,17},{2,18},{3,19},{4,20},{5,21},{6,22},{7,23},{8,24},{9,... | collective-permute-start | bytes 98312 | tf_op jit(solution)/shard_map/ppermute | solution.py:17
  40.1 5.7 %collective-permute-start.17 = (bf16[8,2048]{1,0:T(8,128)(2,1)S(1)}, bf16[8,2048]{1,0:T(8,128)(2,1)S(1)}, u32[]{:S(2)}, u32[]{:S(2)}) collective-permute-start(bf16[8,2048]{1,0:T(8,128)(2,1)S(1)} %get-tuple-element.18), channel_id=1, source_target_pairs={{0,8},{1,9},{2,10},{3,11},{4,12},{5,13},{6,14},{7,15},{8,0},{9,1},... | collective-permute-start | bytes 98312 | tf_op jit(solution)/shard_map/ppermute | solution.py:17

commit v2 on v1

--- a/solution.py
+++ b/solution.py
@@ -33,7 +33,7 @@
     return list(range(count - 1, 0, -1))
 
 
-def attend_kernel(lengths_in, hidden_in, query_in, keys, values, gain_in, mixed, normed, lengths, hidden, query, gain, key_buf, value_buf, score_buf, small_sem, key_sem, value_sem):
+def attend_kernel(lengths_in, hidden_in, query_in, keys, values, gain_in, w_in_from, w_out_from, mixed, normed, w_in, w_out, lengths, hidden, query, gain, key_buf, value_buf, score_buf, small_sem, key_sem, value_sem):
     streams, width = hidden.shape
     span = key_buf.shape[1]
     head_size = width // HEADS
@@ -47,7 +47,11 @@
     pieces = [pl.ds(piece * group, group) for piece in range(PIECES)]
     key_copies = [pltpu.make_async_copy(keys.at[p], key_buf.at[p], key_sem.at[i]) for i, p in enumerate(pieces)]
     value_copies = [pltpu.make_async_copy(values.at[p], value_buf.at[p], value_sem.at[i]) for i, p in enumerate(pieces)]
-    for copy in small + key_copies + value_copies:
+    weights = [
+        pltpu.make_async_copy(w_in_from, w_in, small_sem.at[4]),
+        pltpu.make_async_copy(w_out_from, w_out, small_sem.at[5]),
+    ]
+    for copy in small + key_copies + value_copies + weights:
         copy.start()
     owner = lax.broadcasted_iota(jnp.int32, (HEADS, width), 1) // head_size
     own = owner == lax.broadcasted_iota(jnp.int32, (HEADS, width), 0)
@@ -79,9 +83,20 @@
     centered = total - jnp.mean(total, axis=-1, keepdims=True)
     variance = jnp.mean(centered * centered, axis=-1, keepdims=True)
     normed[...] = (centered * lax.rsqrt(variance + 1e-05) * gain[...]).astype(jnp.bfloat16)
-
-
-def attend(hidden_state, cross_query, source_keys, source_values, src_lengths, norm_gain):
+    for copy in weights:
+        copy.wait()
+
+
+def attend(
+    hidden_state,
+    cross_query,
+    source_keys,
+    source_values,
+    src_lengths,
+    norm_gain,
+    w_in,
+    w_out,
+):
     streams, width = hidden_state.shape
     span = source_keys.shape[1]
     arrays = (
@@ -91,14 +106,21 @@
         source_keys,
         source_values,
         norm_gain.reshape(1, width),
+        w_in,
+        w_out,
     )
     vmem = pl.BlockSpec(memory_space=pltpu.VMEM)
     hbm = pl.BlockSpec(memory_space=pltpu.HBM)
     return pl.pallas_call(
         attend_kernel,
-        out_shape=(jax.ShapeDtypeStruct((streams, width), jnp.float32), jax.ShapeDtypeStruct((streams, width), jnp.bfloat16)),
-        in_specs=[hbm]*6,
-        out_specs=(vmem, vmem),
+        out_shape=(
+            pltpu.VMEM((streams, width), jnp.float32),
+            pltpu.VMEM((streams, width), jnp.bfloat16),
+            pltpu.VMEM(w_in.shape, w_in.dtype),
+            pltpu.VMEM(w_out.shape, w_out.dtype),
+        ),
+        in_specs=[hbm] * 8,
+        out_specs=(vmem,) * 4,
         scratch_shapes=[
             pltpu.SMEM((streams,), jnp.int32),
             pltpu.VMEM((streams, width), hidden_state.dtype),
@@ -107,12 +129,41 @@
             pltpu.VMEM((streams, span, width), source_keys.dtype),
             pltpu.VMEM((streams, span, width), source_values.dtype),
             pltpu.VMEM((streams * HEADS, span), jnp.float32),
-            pltpu.SemaphoreType.DMA((4,)),
+            pltpu.SemaphoreType.DMA((6,)),
             pltpu.SemaphoreType.DMA((PIECES,)),
             pltpu.SemaphoreType.DMA((PIECES,)),
         ],
         compiler_params=pltpu.CompilerParams(vmem_limit_bytes=VMEM_LIMIT),
     )(*[pltpu.with_memory_space_constraint(array, pltpu.HBM) for array in arrays])
+
+
+def feed_forward(rows, w_in, w_out, kind):
+    def kernel(*refs):
+        row_refs = refs[: len(rows)]
+        w_in_ref, w_out_ref = refs[len(rows) : len(rows) + 2]
+        stacked = jnp.concatenate([ref[...] for ref in row_refs], axis=0)
+        units = jnp.dot(stacked, w_in_ref[...], preferred_element_type=jnp.float32)
+        act = jnp.maximum(units, 0.0).astype(jnp.bfloat16)
+        every = jnp.dot(act, w_out_ref[...], preferred_element_type=jnp.float32).astype(kind)
+        start = 0
+        for ref in refs[len(rows) + 2 :]:
+            ref[...] = every[start : start + ref.shape[0]]
+            start += ref.shape[0]
+
+    vmem = pl.BlockSpec(memory_space=pltpu.VMEM)
+    count = sum(part.shape[0] for part in rows)
+    return pl.pallas_call(
+        kernel,
+        out_shape=[jax.ShapeDtypeStruct(part.shape, kind) for part in rows],
+        in_specs=[vmem] * (len(rows) + 2),
+        out_specs=[vmem] * len(rows),
+        compiler_params=pltpu.CompilerParams(vmem_limit_bytes=VMEM_LIMIT),
+        cost_estimate=pl.CostEstimate(
+            flops=2 * count * w_in.size + 2 * count * w_out.size,
+            transcendentals=0,
+            bytes_accessed=2 * (w_in.size + w_out.size),
+        ),
+    )(*rows, w_in, w_out)
 
 
 def step_on_device(
@@ -132,8 +183,15 @@
     experts_count = devices // SPLIT
     capacity = max(2, min(streams, 4 * streams * SPLIT // devices))
     direct = experts_count <= 4
-    mixed, normed = attend(
-        hidden_state, cross_query, source_keys, source_values, src_lengths, norm_gain
+    mixed, normed, w_in, w_out = attend(
+        hidden_state,
+        cross_query,
+        source_keys,
+        source_values,
+        src_lengths,
+        norm_gain,
+        w_in,
+        w_out,
     )
     group = lax.axis_index("expert") // SPLIT
     order = jnp.arange(experts_count, dtype=jnp.int32)
@@ -156,7 +214,6 @@
         ).astype(jnp.bfloat16)
         blocks = [packed[index] for index in range(experts_count)]
     chips = SPLIT // CORES
-    steps = far_first(chips)
     distances = far_first(experts_count)
     if direct:
         planes = {k: swap(blocks[k], k * SPLIT, devices) for k in distances}
@@ -164,24 +221,18 @@
     else:
         column = outer_exchange(blocks, devices)
     near = {0: jnp.concatenate(column, axis=0)}
-    count = near[0].shape[0]
     for step in range(1, chips):
         near[step] = swap(near[0], CORES * step, devices)
     far = {step: swap(near[step], 1, devices) for step in range(chips)}
-    rows = [near[step] for step in range(chips)] + [far[step] for step in range(chips)]
-    half = chips * count
-    units = jnp.dot(jnp.concatenate(rows, axis=0), w_in, preferred_element_type=jnp.float32)
-    act = lax.optimization_barrier(jnp.maximum(units, 0.0).astype(jnp.bfloat16))
-    far_sent = jnp.dot(act[half:], w_out, preferred_element_type=jnp.float32).astype(jnp.bfloat16)
-    near_every = jnp.dot(act[:half], w_out, preferred_element_type=jnp.float32)
-    near_every = lax.optimization_barrier(near_every)
+    near_every = feed_forward([near[step] for step in range(chips)], w_in, w_out, jnp.float32)
+    near_every, far = lax.optimization_barrier((near_every, far))
+    far_sent = feed_forward([far[step] for step in range(chips)], w_in, w_out, jnp.bfloat16)
     pair = {}
-    for step in steps + [0]:
-        place = slice(step * count, (step + 1) * count)
-        given = swap(far_sent[place], 1, devices)
-        pair[step] = near_every[place] + given.astype(jnp.float32)
+    for step in range(chips):
+        given = swap(far_sent[step], 1, devices)
+        pair[step] = near_every[step] + given.astype(jnp.float32)
     total = pair[0]
-    for step in steps:
+    for step in range(1, chips):
         sent = pair[step].astype(jnp.bfloat16)
         total = total + swap(sent, CORES * step, devices).astype(jnp.float32)
     total = total.reshape(experts_count, capacity, width)

time: 46.6 us -> 44.5 us (0.955)
  matrix products: 3.18 us -> 0 us
  Pallas kernels: 3.69 us -> 5.86 us
  waiting for transfers between devices: 19.9 us -> 19 us
    dot_general x3 -> x0, matrix products: 3.18 us -> none  [the longest x1 2.29 us: step_on_device(): jnp.dot(jnp.concatenate(rows, axis=0), w_in, preferred_element_type=jnp.f...]
    pallas_call x1 -> x3, Pallas kernels: 3.69 us -> 5.86 us  [the longest x1 4.2 us: attend(): pl.pallas_call(attend_kernel, out_shape=(pltpu.VMEM((streams, width), jnp...]
    ppermute x20, waiting for transfers between devices: 19.9 us -> 19 us  [swap(): return lax.ppermute(value, 'expert', pairs)]
  transfers between devices with their start and end apart: 20 -> 20, of which waited for: 11 -> 12; matrix products, arithmetic and copies ran while one was open for 2% -> 0% of each run, Pallas kernels for 0% -> 2%
where the time goes in v2:
time: 44.5 us; the launch traced here: 44.4 us
  waiting for transfers between devices  19 us (43%)
  starting transfers between devices  18.4 us (41%)
  Pallas kernels  5.86 us (13%)
  other arithmetic  0.96 us (2%)
    ppermute x20, waiting for transfers between devices, swap(): return lax.ppermute(value, 'expert', pairs)  19 us
    ppermute x20, starting transfers between devices, swap(): return lax.ppermute(value, 'expert', pairs)  18.4 us
    pallas_call x1, Pallas kernels, attend(): pl.pallas_call(attend_kernel, out_shape=(pltpu.VMEM((streams, width), jnp...  4.2 us
    pallas_call x2, Pallas kernels, feed_forward(): pl.pallas_call(kernel, out_shape=[jax.ShapeDtypeStruct(part.shape, kind)...  1.67 us
  transfers between devices with their start and end apart: 20, of which 12 were waited for; matrix products, arithmetic and copies ran while one was open for 0% of the time, Pallas kernels for 2%

profile of v2, /device:TPU:0, one launch (start us, length us, event | category | flops | bytes accessed | tf_op | source)
XLA Modules:
  0.0 44.4 jit_solution(16636825045477043537)
XLA Ops:
  0.0 4.2 %shard_map.100 = (f32[8,2048]{1,0:T(8,128)S(1)}, bf16[8,2048]{1,0:T(8,128)(2,1)S(1)}, bf16[2048,512]{1,0:T(8,128)(2,1)S(1)}, bf16[512,2048]{1,0:T(8,128)(2,1)S(1)}) custom-call(s32[8]{0:T(128)} %lengths_in.1, bf16[8,2048]{1,0:T(8,128)(2,1)} %hidden_in.1, bf16[8,2048]{1,0:T(8,128)(2,1)} %query_in.1, bf16[8,64,2048]{2,1,0:T(8,128)(2,1)} %keys.1, ...), custom_call_target="tpu_custom_call" | custom-call | tf_op jit(solution)/shard_map/pallas_call | solution.py:114
  4.2 3.1 %collective-permute-start = (bf16[8,2048]{1,0:T(8,128)(2,1)S(1)}, bf16[8,2048]{1,0:T(8,128)(2,1)S(1)}, u32[]{:S(2)}, u32[]{:S(2)}) collective-permute-start(bf16[8,2048]{1,0:T(8,128)(2,1)S(1)} %get-tuple-element.26), channel_id=1, source_target_pairs={{0,8},{1,9},{2,10},{3,11},{4,12},{5,13},{6,14},{7,15},{8,0},{9,1},... | collective-permute-start | bytes 98312 | tf_op jit(solution)/shard_map/ppermute | solution.py:17
  7.3 2.6 %collective-permute-start.1 = (bf16[8,2048]{1,0:T(8,128)(2,1)S(1)}, bf16[8,2048]{1,0:T(8,128)(2,1)S(1)}, u32[]{:S(2)}, u32[]{:S(2)}) collective-permute-start(bf16[8,2048]{1,0:T(8,128)(2,1)S(1)} %get-tuple-element.26), channel_id=1, source_target_pairs={{0,16},{1,17},{2,18},{3,19},{4,20},{5,21},{6,22},{7,23},{8,24},{9,... | collective-permute-start | bytes 98312 | tf_op jit(solution)/shard_map/ppermute | solution.py:17
  9.9 2.8 %collective-permute-done.1 = bf16[8,2048]{1,0:T(8,128)(2,1)S(1)} collective-permute-done((bf16[8,2048]{1,0:T(8,128)(2,1)S(1)}, bf16[8,2048]{1,0:T(8,128)(2,1)S(1)}, u32[]{:S(2)}, u32[]{:S(2)}) %collective-permute-start.1) | collective-permute-done | bytes 32800 | tf_op jit(solution)/shard_map/ppermute | solution.py:17
  12.7 2.9 %collective-permute-done.2 = bf16[8,2048]{1,0:T(8,128)(2,1)S(1)} collective-permute-done((bf16[8,2048]{1,0:T(8,128)(2,1)S(1)}, bf16[8,2048]{1,0:T(8,128)(2,1)S(1)}, u32[]{:S(2)}, u32[]{:S(2)}) %collective-permute-start.2) | collective-permute-done | bytes 32800 | tf_op jit(solution)/shard_map/ppermute | solution.py:17
  15.6 1.5 %collective-permute-start.3 = (bf16[32,2048]{1,0:T(8,128)(2,1)S(1)}, bf16[32,2048]{1,0:T(8,128)(2,1)S(1)}, u32[]{:S(2)}, u32[]{:S(2)}) collective-permute-start(bf16[32,2048]{1,0:T(8,128)(2,1)S(1)} %constant_dynamic-update-slice_fusion.refs_0_), channel_id=1, source_target_pairs={{0,2},{1,3},{2,0},{3,1},{4,6},{5,7},{6,4},{7,5},{8,10},{9,11},{10,... | collective-permute-start | bytes 393224 | tf_op jit(solution)/shard_map/ppermute | solution.py:17
  17.1 1.5 %collective-permute-start.4 = (bf16[32,2048]{1,0:T(8,128)(2,1)S(1)}, bf16[32,2048]{1,0:T(8,128)(2,1)S(1)}, u32[]{:S(2)}, u32[]{:S(2)}) collective-permute-start(bf16[32,2048]{1,0:T(8,128)(2,1)S(1)} %constant_dynamic-update-slice_fusion.refs_0_), channel_id=1, source_target_pairs={{0,4},{1,5},{2,6},{3,7},{4,0},{5,1},{6,2},{7,3},{8,12},{9,13},{10,... | collective-permute-start | bytes 393224 | tf_op jit(solution)/shard_map/ppermute | solution.py:17
  18.6 0.5 %collective-permute-start.5 = (bf16[32,2048]{1,0:T(8,128)(2,1)S(1)}, bf16[32,2048]{1,0:T(8,128)(2,1)S(1)}, u32[]{:S(2)}, u32[]{:S(2)}) collective-permute-start(bf16[32,2048]{1,0:T(8,128)(2,1)S(1)} %constant_dynamic-update-slice_fusion.refs_0_), channel_id=1, source_target_pairs={{0,6},{1,7},{2,4},{3,5},{4,2},{5,3},{6,0},{7,1},{8,14},{9,15},{10,... | collective-permute-start | bytes 393224 | tf_op jit(solution)/shard_map/ppermute | solution.py:17
  19.1 2.5 %collective-permute-done.3.refs_1_ = bf16[32,2048]{1,0:T(8,128)(2,1)S(1)} collective-permute-done((bf16[32,2048]{1,0:T(8,128)(2,1)S(1)}, bf16[32,2048]{1,0:T(8,128)(2,1)S(1)}, u32[]{:S(2)}, u32[]{:S(2)}) %collective-permute-start.3) | collective-permute-done | bytes 131104 | tf_op jit(solution)/shard_map/ppermute | solution.py:17
  21.7 1.2 %collective-permute-done.4.refs_2_ = bf16[32,2048]{1,0:T(8,128)(2,1)S(1)} collective-permute-done((bf16[32,2048]{1,0:T(8,128)(2,1)S(1)}, bf16[32,2048]{1,0:T(8,128)(2,1)S(1)}, u32[]{:S(2)}, u32[]{:S(2)}) %collective-permute-start.4) | collective-permute-done | bytes 131104 | tf_op jit(solution)/shard_map/ppermute | solution.py:17
  22.9 1.6 %collective-permute-done.5.refs_3_ = bf16[32,2048]{1,0:T(8,128)(2,1)S(1)} collective-permute-done((bf16[32,2048]{1,0:T(8,128)(2,1)S(1)}, bf16[32,2048]{1,0:T(8,128)(2,1)S(1)}, u32[]{:S(2)}, u32[]{:S(2)}) %collective-permute-start.5) | collective-permute-done | bytes 131104 | tf_op jit(solution)/shard_map/ppermute | solution.py:17
  24.5 0.8 %shard_map.101 = (f32[32,2048]{1,0:T(8,128)S(1)}, f32[32,2048]{1,0:T(8,128)S(1)}, f32[32,2048]{1,0:T(8,128)S(1)}, f32[32,2048]{1,0:T(8,128)S(1)}) custom-call(bf16[32,2048]{1,0:T(8,128)(2,1)S(1)} %constant_dynamic-update-slice_fusion.refs_0_, bf16[32,2048]{1,0:T(8,128)(2,1)S(1)} %collective-permute-done.3.refs_1_, ...), custom_call_target="tpu_custom_call" | custom-call | flops 536870912 | bytes 4194304 | tf_op jit(solution)/shard_map/pallas_call | solution.py:155
  25.4 0.5 %collective-permute-done.9.refs_3_ = bf16[32,2048]{1,0:T(8,128)(2,1)S(1)} collective-permute-done((bf16[32,2048]{1,0:T(8,128)(2,1)S(1)}, bf16[32,2048]{1,0:T(8,128)(2,1)S(1)}, u32[]{:S(2)}, u32[]{:S(2)}) %collective-permute-start.9) | collective-permute-done | bytes 131104 | tf_op jit(solution)/shard_map/ppermute | solution.py:17
  25.9 0.8 %shard_map.102 = (bf16[32,2048]{1,0:T(8,128)(2,1)S(1)}, bf16[32,2048]{1,0:T(8,128)(2,1)S(1)}, bf16[32,2048]{1,0:T(8,128)(2,1)S(1)}, bf16[32,2048]{1,0:T(8,128)(2,1)S(1)}) custom-call(bf16[32,2048]{1,0:T(8,128)(2,1)S(1)} %collective-permute-done.6.refs_0_, bf16[32,2048]{1,0:T(8,128)(2,1)S(1)} %collective-permute-done.7.refs_1_, ...), custom_call_target="tpu_custom_call" | custom-call | flops 536870912 | bytes 4194304 | tf_op jit(solution)/shard_map/pallas_call | solution.py:155
  26.7 0.2 collective-permute-start.15
  26.9 0.4 collective-permute-start.13
  27.3 0.1 collective-permute-start.11
  27.4 0.4 collective-permute-start.10
  27.8 0.3 collective-permute-done.15
  28.2 0.5 %collective-permute-start.16 = (bf16[32,2048]{1,0:T(8,128)(2,1)S(1)}, bf16[32,2048]{1,0:T(8,128)(2,1)S(1)}, u32[]{:S(2)}, u32[]{:S(2)}) collective-permute-start(bf16[32,2048]{1,0:T(8,128)(2,1)S(1)} %add_convert_fusion), channel_id=1, source_target_pairs={{0,6},{1,7},{2,4},{3,5},{4,2},{5,3},{6,0},{7,1},{8,14},{9,15},{10,... | collective-permute-start | bytes 393224 | tf_op jit(solution)/shard_map/ppermute | solution.py:17
  28.7 1.6 %collective-permute-start.14 = (bf16[32,2048]{1,0:T(8,128)(2,1)S(1)}, bf16[32,2048]{1,0:T(8,128)(2,1)S(1)}, u32[]{:S(2)}, u32[]{:S(2)}) collective-permute-start(bf16[32,2048]{1,0:T(8,128)(2,1)S(1)} %add_convert_fusion.1), channel_id=1, source_target_pairs={{0,4},{1,5},{2,6},{3,7},{4,0},{5,1},{6,2},{7,3},{8,12},{9,13},{10,... | collective-permute-start | bytes 393224 | tf_op jit(solution)/shard_map/ppermute | solution.py:17
  30.4 1.6 %collective-permute-start.12 = (bf16[32,2048]{1,0:T(8,128)(2,1)S(1)}, bf16[32,2048]{1,0:T(8,128)(2,1)S(1)}, u32[]{:S(2)}, u32[]{:S(2)}) collective-permute-start(bf16[32,2048]{1,0:T(8,128)(2,1)S(1)} %add_convert_fusion.2), channel_id=1, source_target_pairs={{0,2},{1,3},{2,0},{3,1},{4,6},{5,7},{6,4},{7,5},{8,10},{9,11},{10,... | collective-permute-start | bytes 393224 | tf_op jit(solution)/shard_map/ppermute | solution.py:17
  31.9 0.1 select_reduce_fusion
  32.0 3.5 %collective-permute-done.16 = bf16[32,2048]{1,0:T(8,128)(2,1)S(1)} collective-permute-done((bf16[32,2048]{1,0:T(8,128)(2,1)S(1)}, bf16[32,2048]{1,0:T(8,128)(2,1)S(1)}, u32[]{:S(2)}, u32[]{:S(2)}) %collective-permute-start.16) | collective-permute-done | bytes 131104 | tf_op jit(solution)/shard_map/ppermute | solution.py:17
  35.5 1.4 %collective-permute-done.14 = bf16[32,2048]{1,0:T(8,128)(2,1)S(1)} collective-permute-done((bf16[32,2048]{1,0:T(8,128)(2,1)S(1)}, bf16[32,2048]{1,0:T(8,128)(2,1)S(1)}, u32[]{:S(2)}, u32[]{:S(2)}) %collective-permute-start.14) | collective-permute-done | bytes 131104 | tf_op jit(solution)/shard_map/ppermute | solution.py:17
  36.9 0.3 collective-permute-done.12
  37.2 0.1 fusion.5
  37.3 0.6 %collective-permute-start.19 = (bf16[8,2048]{1,0:T(8,128)(2,1)S(1)}, bf16[8,2048]{1,0:T(8,128)(2,1)S(1)}, u32[]{:S(2)}, u32[]{:S(2)}) collective-permute-start(bf16[8,2048]{1,0:T(8,128)(2,1)S(1)} %get-tuple-element.48), channel_id=1, source_target_pairs={{0,24},{1,25},{2,26},{3,27},{4,28},{5,29},{6,30},{7,31},{8,16},{9,... | collective-permute-start | bytes 98312 | tf_op jit(solution)/shard_map/ppermute | solution.py:17
  38.0 3.8 %collective-permute-start.17 = (bf16[8,2048]{1,0:T(8,128)(2,1)S(1)}, bf16[8,2048]{1,0:T(8,128)(2,1)S(1)}, u32[]{:S(2)}, u32[]{:S(2)}) collective-permute-start(bf16[8,2048]{1,0:T(8,128)(2,1)S(1)} %get-tuple-element.47), channel_id=1, source_target_pairs={{0,8},{1,9},{2,10},{3,11},{4,12},{5,13},{6,14},{7,15},{8,0},{9,1},... | collective-permute-start | bytes 98312 | tf_op jit(solution)/shard_map/ppermute | solution.py:17
  41.8 1.3 %collective-permute-done.19 = bf16[8,2048]{1,0:T(8,128)(2,1)S(1)} collective-permute-done((bf16[8,2048]{1,0:T(8,128)(2,1)S(1)}, bf16[8,2048]{1,0:T(8,128)(2,1)S(1)}, u32[]{:S(2)}, u32[]{:S(2)}) %collective-permute-start.19) | collective-permute-done | bytes 32800 | tf_op jit(solution)/shard_map/ppermute | solution.py:17
  43.1 0.6 %collective-permute-done.17 = bf16[8,2048]{1,0:T(8,128)(2,1)S(1)} collective-permute-done((bf16[8,2048]{1,0:T(8,128)(2,1)S(1)}, bf16[8,2048]{1,0:T(8,128)(2,1)S(1)}, u32[]{:S(2)}, u32[]{:S(2)}) %collective-permute-start.17) | collective-permute-done | bytes 32800 | tf_op jit(solution)/shard_map/ppermute | solution.py:17
  43.7 0.7 %fusion.4 = bf16[8,2048]{1,0:T(8,128)(2,1)} fusion(f32[8,2048]{1,0:T(8,128)S(1)} %get-tuple-element.25, f32[32,2048]{1,0:T(8,128)S(1)} %get-tuple-element.46, bf16[8,2048]{1,0:T(8,128)(2,1)S(1)} %collective-permute-done.19, bf16[8,2048]{1,0:T(8,128)(2,1)S(1)} %collective-permute-done.18, bf16[8,2048]{1,0:T(8,128)(2,1)S(1)} %collective-permute-done.17, ...), kind=kLoop, calls=%fused_computation.9 | loop fusion | flops 196608 | bytes 262272 | tf_op jit(solution)/shard_map/convert_element_type | solution.py:257
  (28 shorter events, 0.2 us)
Async XLA Ops:
  4.2 5.7 %collective-permute-start = (bf16[8,2048]{1,0:T(8,128)(2,1)S(1)}, bf16[8,2048]{1,0:T(8,128)(2,1)S(1)}, u32[]{:S(2)}, u32[]{:S(2)}) collective-permute-start(bf16[8,2048]{1,0:T(8,128)(2,1)S(1)} %get-tuple-element.26), channel_id=1, source_target_pairs={{0,8},{1,9},{2,10},{3,11},{4,12},{5,13},{6,14},{7,15},{8,0},{9,1},... | collective-permute-start | bytes 98312 | tf_op jit(solution)/shard_map/ppermute | solution.py:17
  7.3 5.4 %collective-permute-start.1 = (bf16[8,2048]{1,0:T(8,128)(2,1)S(1)}, bf16[8,2048]{1,0:T(8,128)(2,1)S(1)}, u32[]{:S(2)}, u32[]{:S(2)}) collective-permute-start(bf16[8,2048]{1,0:T(8,128)(2,1)S(1)} %get-tuple-element.26), channel_id=1, source_target_pairs={{0,16},{1,17},{2,18},{3,19},{4,20},{5,21},{6,22},{7,23},{8,24},{9,... | collective-permute-start | bytes 98312 | tf_op jit(solution)/shard_map/ppermute | solution.py:17
  9.9 5.7 %collective-permute-start.2 = (bf16[8,2048]{1,0:T(8,128)(2,1)S(1)}, bf16[8,2048]{1,0:T(8,128)(2,1)S(1)}, u32[]{:S(2)}, u32[]{:S(2)}) collective-permute-start(bf16[8,2048]{1,0:T(8,128)(2,1)S(1)} %get-tuple-element.26), channel_id=1, source_target_pairs={{0,24},{1,25},{2,26},{3,27},{4,28},{5,29},{6,30},{7,31},{8,16},{9,... | collective-permute-start | bytes 98312 | tf_op jit(solution)/shard_map/ppermute | solution.py:17
  15.6 6.0 %collective-permute-start.3 = (bf16[32,2048]{1,0:T(8,128)(2,1)S(1)}, bf16[32,2048]{1,0:T(8,128)(2,1)S(1)}, u32[]{:S(2)}, u32[]{:S(2)}) collective-permute-start(bf16[32,2048]{1,0:T(8,128)(2,1)S(1)} %constant_dynamic-update-slice_fusion.refs_0_), channel_id=1, source_target_pairs={{0,2},{1,3},{2,0},{3,1},{4,6},{5,7},{6,4},{7,5},{8,10},{9,11},{10,... | collective-permute-start | bytes 393224 | tf_op jit(solution)/shard_map/ppermute | solution.py:17
  17.1 5.8 %collective-permute-start.4 = (bf16[32,2048]{1,0:T(8,128)(2,1)S(1)}, bf16[32,2048]{1,0:T(8,128)(2,1)S(1)}, u32[]{:S(2)}, u32[]{:S(2)}) collective-permute-start(bf16[32,2048]{1,0:T(8,128)(2,1)S(1)} %constant_dynamic-update-slice_fusion.refs_0_), channel_id=1, source_target_pairs={{0,4},{1,5},{2,6},{3,7},{4,0},{5,1},{6,2},{7,3},{8,12},{9,13},{10,... | collective-permute-start | bytes 393224 | tf_op jit(solution)/shard_map/ppermute | solution.py:17
  18.6 5.9 %collective-permute-start.5 = (bf16[32,2048]{1,0:T(8,128)(2,1)S(1)}, bf16[32,2048]{1,0:T(8,128)(2,1)S(1)}, u32[]{:S(2)}, u32[]{:S(2)}) collective-permute-start(bf16[32,2048]{1,0:T(8,128)(2,1)S(1)} %constant_dynamic-update-slice_fusion.refs_0_), channel_id=1, source_target_pairs={{0,6},{1,7},{2,4},{3,5},{4,2},{5,3},{6,0},{7,1},{8,14},{9,15},{10,... | collective-permute-start | bytes 393224 | tf_op jit(solution)/shard_map/ppermute | solution.py:17
  19.1 6.2 %collective-permute-start.6 = (bf16[32,2048]{1,0:T(8,128)(2,1)S(1)}, bf16[32,2048]{1,0:T(8,128)(2,1)S(1)}, u32[]{:S(2)}, u32[]{:S(2)}) collective-permute-start(bf16[32,2048]{1,0:T(8,128)(2,1)S(1)} %constant_dynamic-update-slice_fusion.refs_0_), channel_id=1, source_target_pairs={{0,1},{1,0},{2,3},{3,2},{4,5},{5,4},{6,7},{7,6},{8,9},{9,8},{10,11... | collective-permute-start | bytes 393224 | tf_op jit(solution)/shard_map/ppermute | solution.py:17
  21.7 3.7 %collective-permute-start.7 = (bf16[32,2048]{1,0:T(8,128)(2,1)S(1)}, bf16[32,2048]{1,0:T(8,128)(2,1)S(1)}, u32[]{:S(2)}, u32[]{:S(2)}) collective-permute-start(bf16[32,2048]{1,0:T(8,128)(2,1)S(1)} %collective-permute-done.3.refs_1_), channel_id=1, source_target_pairs={{0,1},{1,0},{2,3},{3,2},{4,5},{5,4},{6,7},{7,6},{8,9},{9,8},{10,11... | collective-permute-start | bytes 393224 | tf_op jit(solution)/shard_map/ppermute | solution.py:17
  22.9 2.5 %collective-permute-start.8 = (bf16[32,2048]{1,0:T(8,128)(2,1)S(1)}, bf16[32,2048]{1,0:T(8,128)(2,1)S(1)}, u32[]{:S(2)}, u32[]{:S(2)}) collective-permute-start(bf16[32,2048]{1,0:T(8,128)(2,1)S(1)} %collective-permute-done.4.refs_2_), channel_id=1, source_target_pairs={{0,1},{1,0},{2,3},{3,2},{4,5},{5,4},{6,7},{7,6},{8,9},{9,8},{10,11... | collective-permute-start | bytes 393224 | tf_op jit(solution)/shard_map/ppermute | solution.py:17
  24.5 1.3 %collective-permute-start.9 = (bf16[32,2048]{1,0:T(8,128)(2,1)S(1)}, bf16[32,2048]{1,0:T(8,128)(2,1)S(1)}, u32[]{:S(2)}, u32[]{:S(2)}) collective-permute-start(bf16[32,2048]{1,0:T(8,128)(2,1)S(1)} %collective-permute-done.5.refs_3_), channel_id=1, source_target_pairs={{0,1},{1,0},{2,3},{3,2},{4,5},{5,4},{6,7},{7,6},{8,9},{9,8},{10,11... | collective-permute-start | bytes 393224 | tf_op jit(solution)/shard_map/ppermute | solution.py:17
  25.9 6.1 %copy-start = (f32[8,2]{0,1:T(2,128)S(1)}, f32[8,2]{0,1:T(2,128)}, u32[]{:S(2)}) copy-start(f32[8,2]{0,1:T(2,128)} %param.19) | copy-start | bytes 196
  25.9 6.1 %copy-start.1 = (s32[8,2]{0,1:T(2,128)S(1)}, s32[8,2]{0,1:T(2,128)}, u32[]{:S(2)}) copy-start(s32[8,2]{0,1:T(2,128)} %param.18) | copy-start | bytes 196
  26.7 1.4 %collective-permute-start.15 = (bf16[32,2048]{1,0:T(8,128)(2,1)S(1)}, bf16[32,2048]{1,0:T(8,128)(2,1)S(1)}, u32[]{:S(2)}, u32[]{:S(2)}) collective-permute-start(bf16[32,2048]{1,0:T(8,128)(2,1)S(1)} %get-tuple-element.44), channel_id=1, source_target_pairs={{0,1},{1,0},{2,3},{3,2},{4,5},{5,4},{6,7},{7,6},{8,9},{9,8},{10,11... | collective-permute-start | bytes 393224 | tf_op jit(solution)/shard_map/ppermute | solution.py:17
  26.9 1.8 %collective-permute-start.13 = (bf16[32,2048]{1,0:T(8,128)(2,1)S(1)}, bf16[32,2048]{1,0:T(8,128)(2,1)S(1)}, u32[]{:S(2)}, u32[]{:S(2)}) collective-permute-start(bf16[32,2048]{1,0:T(8,128)(2,1)S(1)} %get-tuple-element.42), channel_id=1, source_target_pairs={{0,1},{1,0},{2,3},{3,2},{4,5},{5,4},{6,7},{7,6},{8,9},{9,8},{10,11... | collective-permute-start | bytes 393224 | tf_op jit(solution)/shard_map/ppermute | solution.py:17
  27.3 3.0 %collective-permute-start.11 = (bf16[32,2048]{1,0:T(8,128)(2,1)S(1)}, bf16[32,2048]{1,0:T(8,128)(2,1)S(1)}, u32[]{:S(2)}, u32[]{:S(2)}) collective-permute-start(bf16[32,2048]{1,0:T(8,128)(2,1)S(1)} %get-tuple-element.40), channel_id=1, source_target_pairs={{0,1},{1,0},{2,3},{3,2},{4,5},{5,4},{6,7},{7,6},{8,9},{9,8},{10,11... | collective-permute-start | bytes 393224 | tf_op jit(solution)/shard_map/ppermute | solution.py:17
  27.4 4.6 %collective-permute-start.10 = (bf16[32,2048]{1,0:T(8,128)(2,1)S(1)}, bf16[32,2048]{1,0:T(8,128)(2,1)S(1)}, u32[]{:S(2)}, u32[]{:S(2)}) collective-permute-start(bf16[32,2048]{1,0:T(8,128)(2,1)S(1)} %get-tuple-element.38), channel_id=1, source_target_pairs={{0,1},{1,0},{2,3},{3,2},{4,5},{5,4},{6,7},{7,6},{8,9},{9,8},{10,11... | collective-permute-start | bytes 393224 | tf_op jit(solution)/shard_map/ppermute | solution.py:17
  28.2 7.4 %collective-permute-start.16 = (bf16[32,2048]{1,0:T(8,128)(2,1)S(1)}, bf16[32,2048]{1,0:T(8,128)(2,1)S(1)}, u32[]{:S(2)}, u32[]{:S(2)}) collective-permute-start(bf16[32,2048]{1,0:T(8,128)(2,1)S(1)} %add_convert_fusion), channel_id=1, source_target_pairs={{0,6},{1,7},{2,4},{3,5},{4,2},{5,3},{6,0},{7,1},{8,14},{9,15},{10,... | collective-permute-start | bytes 393224 | tf_op jit(solution)/shard_map/ppermute | solution.py:17
  28.7 8.2 %collective-permute-start.14 = (bf16[32,2048]{1,0:T(8,128)(2,1)S(1)}, bf16[32,2048]{1,0:T(8,128)(2,1)S(1)}, u32[]{:S(2)}, u32[]{:S(2)}) collective-permute-start(bf16[32,2048]{1,0:T(8,128)(2,1)S(1)} %add_convert_fusion.1), channel_id=1, source_target_pairs={{0,4},{1,5},{2,6},{3,7},{4,0},{5,1},{6,2},{7,3},{8,12},{9,13},{10,... | collective-permute-start | bytes 393224 | tf_op jit(solution)/shard_map/ppermute | solution.py:17
  30.4 6.9 %collective-permute-start.12 = (bf16[32,2048]{1,0:T(8,128)(2,1)S(1)}, bf16[32,2048]{1,0:T(8,128)(2,1)S(1)}, u32[]{:S(2)}, u32[]{:S(2)}) collective-permute-start(bf16[32,2048]{1,0:T(8,128)(2,1)S(1)} %add_convert_fusion.2), channel_id=1, source_target_pairs={{0,2},{1,3},{2,0},{3,1},{4,6},{5,7},{6,4},{7,5},{8,10},{9,11},{10,... | collective-permute-start | bytes 393224 | tf_op jit(solution)/shard_map/ppermute | solution.py:17
  37.3 5.8 %collective-permute-start.19 = (bf16[8,2048]{1,0:T(8,128)(2,1)S(1)}, bf16[8,2048]{1,0:T(8,128)(2,1)S(1)}, u32[]{:S(2)}, u32[]{:S(2)}) collective-permute-start(bf16[8,2048]{1,0:T(8,128)(2,1)S(1)} %get-tuple-element.48), channel_id=1, source_target_pairs={{0,24},{1,25},{2,26},{3,27},{4,28},{5,29},{6,30},{7,31},{8,16},{9,... | collective-permute-start | bytes 98312 | tf_op jit(solution)/shard_map/ppermute | solution.py:17
  37.9 5.2 %collective-permute-start.18 = (bf16[8,2048]{1,0:T(8,128)(2,1)S(1)}, bf16[8,2048]{1,0:T(8,128)(2,1)S(1)}, u32[]{:S(2)}, u32[]{:S(2)}) collective-permute-start(bf16[8,2048]{1,0:T(8,128)(2,1)S(1)} %get-tuple-element.49), channel_id=1, source_target_pairs={{0,16},{1,17},{2,18},{3,19},{4,20},{5,21},{6,22},{7,23},{8,24},{9,... | collective-permute-start | bytes 98312 | tf_op jit(solution)/shard_map/ppermute | solution.py:17
  38.0 5.7 %collective-permute-start.17 = (bf16[8,2048]{1,0:T(8,128)(2,1)S(1)}, bf16[8,2048]{1,0:T(8,128)(2,1)S(1)}, u32[]{:S(2)}, u32[]{:S(2)}) collective-permute-start(bf16[8,2048]{1,0:T(8,128)(2,1)S(1)} %get-tuple-element.47), channel_id=1, source_target_pairs={{0,8},{1,9},{2,10},{3,11},{4,12},{5,13},{6,14},{7,15},{8,0},{9,1},... | collective-permute-start | bytes 98312 | tf_op jit(solution)/shard_map/ppermute | solution.py:17

commit v3 on v2

--- a/solution.py
+++ b/solution.py
@@ -33,7 +33,7 @@
     return list(range(count - 1, 0, -1))
 
 
-def attend_kernel(lengths_in, hidden_in, query_in, keys, values, gain_in, w_in_from, w_out_from, mixed, normed, w_in, w_out, lengths, hidden, query, gain, key_buf, value_buf, score_buf, small_sem, key_sem, value_sem):
+def attend_kernel(lengths_in, hidden_in, query_in, keys, values, gain_in, mixed, normed, lengths, hidden, query, gain, key_buf, value_buf, score_buf, small_sem, key_sem, value_sem):
     streams, width = hidden.shape
     span = key_buf.shape[1]
     head_size = width // HEADS
@@ -47,11 +47,7 @@
     pieces = [pl.ds(piece * group, group) for piece in range(PIECES)]
     key_copies = [pltpu.make_async_copy(keys.at[p], key_buf.at[p], key_sem.at[i]) for i, p in enumerate(pieces)]
     value_copies = [pltpu.make_async_copy(values.at[p], value_buf.at[p], value_sem.at[i]) for i, p in enumerate(pieces)]
-    weights = [
-        pltpu.make_async_copy(w_in_from, w_in, small_sem.at[4]),
-        pltpu.make_async_copy(w_out_from, w_out, small_sem.at[5]),
-    ]
-    for copy in small + key_copies + value_copies + weights:
+    for copy in small + key_copies + value_copies:
         copy.start()
     owner = lax.broadcasted_iota(jnp.int32, (HEADS, width), 1) // head_size
     own = owner == lax.broadcasted_iota(jnp.int32, (HEADS, width), 0)
@@ -83,8 +79,6 @@
     centered = total - jnp.mean(total, axis=-1, keepdims=True)
     variance = jnp.mean(centered * centered, axis=-1, keepdims=True)
     normed[...] = (centered * lax.rsqrt(variance + 1e-05) * gain[...]).astype(jnp.bfloat16)
-    for copy in weights:
-        copy.wait()
 
 
 def attend(
@@ -94,8 +88,6 @@
     source_values,
     src_lengths,
     norm_gain,
-    w_in,
-    w_out,
 ):
     streams, width = hidden_state.shape
     span = source_keys.shape[1]
@@ -106,8 +98,6 @@
         source_keys,
         source_values,
         norm_gain.reshape(1, width),
-        w_in,
-        w_out,
     )
     vmem = pl.BlockSpec(memory_space=pltpu.VMEM)
     hbm = pl.BlockSpec(memory_space=pltpu.HBM)
@@ -116,11 +106,9 @@
         out_shape=(
             pltpu.VMEM((streams, width), jnp.float32),
             pltpu.VMEM((streams, width), jnp.bfloat16),
-            pltpu.VMEM(w_in.shape, w_in.dtype),
-            pltpu.VMEM(w_out.shape, w_out.dtype),
         ),
-        in_specs=[hbm] * 8,
-        out_specs=(vmem,) * 4,
+        in_specs=[hbm] * 6,
+        out_specs=(vmem, vmem),
         scratch_shapes=[
             pltpu.SMEM((streams,), jnp.int32),
             pltpu.VMEM((streams, width), hidden_state.dtype),
@@ -129,12 +117,28 @@
             pltpu.VMEM((streams, span, width), source_keys.dtype),
             pltpu.VMEM((streams, span, width), source_values.dtype),
             pltpu.VMEM((streams * HEADS, span), jnp.float32),
-            pltpu.SemaphoreType.DMA((6,)),
+            pltpu.SemaphoreType.DMA((4,)),
             pltpu.SemaphoreType.DMA((PIECES,)),
             pltpu.SemaphoreType.DMA((PIECES,)),
         ],
         compiler_params=pltpu.CompilerParams(vmem_limit_bytes=VMEM_LIMIT),
     )(*[pltpu.with_memory_space_constraint(array, pltpu.HBM) for array in arrays])
+
+
+def bring(array):
+    def kernel(source, target, sem):
+        copy = pltpu.make_async_copy(source, target, sem)
+        copy.start()
+        copy.wait()
+
+    return pl.pallas_call(
+        kernel,
+        out_shape=pltpu.VMEM(array.shape, array.dtype),
+        in_specs=[pl.BlockSpec(memory_space=pltpu.HBM)],
+        out_specs=pl.BlockSpec(memory_space=pltpu.VMEM),
+        scratch_shapes=[pltpu.SemaphoreType.DMA(())],
+        compiler_params=pltpu.CompilerParams(vmem_limit_bytes=VMEM_LIMIT),
+    )(pltpu.with_memory_space_constraint(array, pltpu.HBM))
 
 
 def feed_forward(rows, w_in, w_out, kind):
@@ -183,15 +187,13 @@
     experts_count = devices // SPLIT
     capacity = max(2, min(streams, 4 * streams * SPLIT // devices))
     direct = experts_count <= 4
-    mixed, normed, w_in, w_out = attend(
+    mixed, normed = attend(
         hidden_state,
         cross_query,
         source_keys,
         source_values,
         src_lengths,
         norm_gain,
-        w_in,
-        w_out,
     )
     group = lax.axis_index("expert") // SPLIT
     order = jnp.arange(experts_count, dtype=jnp.int32)
@@ -224,6 +226,8 @@
     for step in range(1, chips):
         near[step] = swap(near[0], CORES * step, devices)
     far = {step: swap(near[step], 1, devices) for step in range(chips)}
+    w_in = bring(w_in)
+    w_out = bring(w_out)
     near_every = feed_forward([near[step] for step in range(chips)], w_in, w_out, jnp.float32)
     near_every, far = lax.optimization_barrier((near_every, far))
     far_sent = feed_forward([far[step] for step in range(chips)], w_in, w_out, jnp.bfloat16)

time: 44.5 us -> 46.8 us (1.052)
  Pallas kernels: 5.86 us -> 8.42 us
    pallas_call x0 -> x2, Pallas kernels: none -> 3.2 us  [bring(): pl.pallas_call(kernel, out_shape=pltpu.VMEM(array.shape, array.dtype), in...]
    pallas_call x1, Pallas kernels: 4.2 us -> 3.54 us  [attend(): pl.pallas_call(attend_kernel, out_shape=(pltpu.VMEM((streams, width), jnp...]
  transfers between devices with their start and end apart: 20 -> 20, of which waited for: 12 -> 11; matrix products, arithmetic and copies ran while one was open for 0% -> 0% of each run, Pallas kernels for 2% -> 9%
where the time goes in v3:
time: 46.8 us; the launch traced here: 46.6 us
  waiting for transfers between devices  18.6 us (40%)
  starting transfers between devices  18.5 us (40%)
  Pallas kernels  8.42 us (18%)
  other arithmetic  0.96 us (2%)
    ppermute x20, waiting for transfers between devices, swap(): return lax.ppermute(value, 'expert', pairs)  18.6 us
    ppermute x20, starting transfers between devices, swap(): return lax.ppermute(value, 'expert', pairs)  18.5 us
    pallas_call x1, Pallas kernels, attend(): pl.pallas_call(attend_kernel, out_shape=(pltpu.VMEM((streams, width), jnp...  3.54 us
    pallas_call x2, Pallas kernels, bring(): pl.pallas_call(kernel, out_shape=pltpu.VMEM(array.shape, array.dtype), in...  3.2 us
    pallas_call x2, Pallas kernels, feed_forward(): pl.pallas_call(kernel, out_shape=[jax.ShapeDtypeStruct(part.shape, kind)...  1.67 us
  transfers between devices with their start and end apart: 20, of which 11 were waited for; matrix products, arithmetic and copies ran while one was open for 0% of the time, Pallas kernels for 9%

profile of v3, /device:TPU:0, one launch (start us, length us, event | category | flops | bytes accessed | tf_op | source)
XLA Modules:
  0.0 46.6 jit_solution(6593533077328438986)
XLA Ops:
  0.0 3.5 %shard_map.100 = (f32[8,2048]{1,0:T(8,128)S(1)}, bf16[8,2048]{1,0:T(8,128)(2,1)S(1)}) custom-call(s32[8]{0:T(128)} %lengths_in.1, bf16[8,2048]{1,0:T(8,128)(2,1)} %hidden_in.1, bf16[8,2048]{1,0:T(8,128)(2,1)} %query_in.1, bf16[8,64,2048]{2,1,0:T(8,128)(2,1)} %keys.1, bf16[8,64,2048]{2,1,0:T(8,128)(2,1)} %values.1, f32[1,2048]{1,0:T(1,128)} %bitcast.9), custom_call_target="tpu_custom_call" | custom-call | tf_op jit(solution)/shard_map/pallas_call | solution.py:104
  3.5 3.1 %collective-permute-start = (bf16[8,2048]{1,0:T(8,128)(2,1)S(1)}, bf16[8,2048]{1,0:T(8,128)(2,1)S(1)}, u32[]{:S(2)}, u32[]{:S(2)}) collective-permute-start(bf16[8,2048]{1,0:T(8,128)(2,1)S(1)} %get-tuple-element.24), channel_id=1, source_target_pairs={{0,8},{1,9},{2,10},{3,11},{4,12},{5,13},{6,14},{7,15},{8,0},{9,1},... | collective-permute-start | bytes 98312 | tf_op jit(solution)/shard_map/ppermute | solution.py:17
  6.7 2.6 %collective-permute-start.1 = (bf16[8,2048]{1,0:T(8,128)(2,1)S(1)}, bf16[8,2048]{1,0:T(8,128)(2,1)S(1)}, u32[]{:S(2)}, u32[]{:S(2)}) collective-permute-start(bf16[8,2048]{1,0:T(8,128)(2,1)S(1)} %get-tuple-element.24), channel_id=1, source_target_pairs={{0,16},{1,17},{2,18},{3,19},{4,20},{5,21},{6,22},{7,23},{8,24},{9,... | collective-permute-start | bytes 98312 | tf_op jit(solution)/shard_map/ppermute | solution.py:17
  9.3 2.8 %collective-permute-done.1 = bf16[8,2048]{1,0:T(8,128)(2,1)S(1)} collective-permute-done((bf16[8,2048]{1,0:T(8,128)(2,1)S(1)}, bf16[8,2048]{1,0:T(8,128)(2,1)S(1)}, u32[]{:S(2)}, u32[]{:S(2)}) %collective-permute-start.1) | collective-permute-done | bytes 32800 | tf_op jit(solution)/shard_map/ppermute | solution.py:17
  12.1 2.9 %collective-permute-done.2 = bf16[8,2048]{1,0:T(8,128)(2,1)S(1)} collective-permute-done((bf16[8,2048]{1,0:T(8,128)(2,1)S(1)}, bf16[8,2048]{1,0:T(8,128)(2,1)S(1)}, u32[]{:S(2)}, u32[]{:S(2)}) %collective-permute-start.2) | collective-permute-done | bytes 32800 | tf_op jit(solution)/shard_map/ppermute | solution.py:17
  15.0 1.5 %collective-permute-start.3 = (bf16[32,2048]{1,0:T(8,128)(2,1)S(1)}, bf16[32,2048]{1,0:T(8,128)(2,1)S(1)}, u32[]{:S(2)}, u32[]{:S(2)}) collective-permute-start(bf16[32,2048]{1,0:T(8,128)(2,1)S(1)} %constant_dynamic-update-slice_fusion.refs_0_), channel_id=1, source_target_pairs={{0,2},{1,3},{2,0},{3,1},{4,6},{5,7},{6,4},{7,5},{8,10},{9,11},{10,... | collective-permute-start | bytes 393224 | tf_op jit(solution)/shard_map/ppermute | solution.py:17
  16.5 1.5 %collective-permute-start.4 = (bf16[32,2048]{1,0:T(8,128)(2,1)S(1)}, bf16[32,2048]{1,0:T(8,128)(2,1)S(1)}, u32[]{:S(2)}, u32[]{:S(2)}) collective-permute-start(bf16[32,2048]{1,0:T(8,128)(2,1)S(1)} %constant_dynamic-update-slice_fusion.refs_0_), channel_id=1, source_target_pairs={{0,4},{1,5},{2,6},{3,7},{4,0},{5,1},{6,2},{7,3},{8,12},{9,13},{10,... | collective-permute-start | bytes 393224 | tf_op jit(solution)/shard_map/ppermute | solution.py:17
  18.0 0.5 %collective-permute-start.5 = (bf16[32,2048]{1,0:T(8,128)(2,1)S(1)}, bf16[32,2048]{1,0:T(8,128)(2,1)S(1)}, u32[]{:S(2)}, u32[]{:S(2)}) collective-permute-start(bf16[32,2048]{1,0:T(8,128)(2,1)S(1)} %constant_dynamic-update-slice_fusion.refs_0_), channel_id=1, source_target_pairs={{0,6},{1,7},{2,4},{3,5},{4,2},{5,3},{6,0},{7,1},{8,14},{9,15},{10,... | collective-permute-start | bytes 393224 | tf_op jit(solution)/shard_map/ppermute | solution.py:17
  18.5 2.5 %collective-permute-done.3.refs_1_ = bf16[32,2048]{1,0:T(8,128)(2,1)S(1)} collective-permute-done((bf16[32,2048]{1,0:T(8,128)(2,1)S(1)}, bf16[32,2048]{1,0:T(8,128)(2,1)S(1)}, u32[]{:S(2)}, u32[]{:S(2)}) %collective-permute-start.3) | collective-permute-done | bytes 131104 | tf_op jit(solution)/shard_map/ppermute | solution.py:17
  21.0 1.2 %collective-permute-done.4.refs_2_ = bf16[32,2048]{1,0:T(8,128)(2,1)S(1)} collective-permute-done((bf16[32,2048]{1,0:T(8,128)(2,1)S(1)}, bf16[32,2048]{1,0:T(8,128)(2,1)S(1)}, u32[]{:S(2)}, u32[]{:S(2)}) %collective-permute-start.4) | collective-permute-done | bytes 131104 | tf_op jit(solution)/shard_map/ppermute | solution.py:17
  22.2 1.6 %collective-permute-done.5.refs_3_ = bf16[32,2048]{1,0:T(8,128)(2,1)S(1)} collective-permute-done((bf16[32,2048]{1,0:T(8,128)(2,1)S(1)}, bf16[32,2048]{1,0:T(8,128)(2,1)S(1)}, u32[]{:S(2)}, u32[]{:S(2)}) %collective-permute-start.5) | collective-permute-done | bytes 131104 | tf_op jit(solution)/shard_map/ppermute | solution.py:17
  23.9 1.6 %shard_map.101.refs_4_ = bf16[2048,512]{1,0:T(8,128)(2,1)S(1)} custom-call(bf16[2048,512]{1,0:T(8,128)(2,1)} %source.2), custom_call_target="tpu_custom_call" | custom-call | tf_op jit(solution)/shard_map/pallas_call | solution.py:134
  25.5 1.6 %shard_map.102.refs_5_ = bf16[512,2048]{1,0:T(8,128)(2,1)S(1)} custom-call(bf16[512,2048]{1,0:T(8,128)(2,1)} %source.3), custom_call_target="tpu_custom_call" | custom-call | tf_op jit(solution)/shard_map/pallas_call | solution.py:134
  27.1 0.8 %shard_map.103 = (f32[32,2048]{1,0:T(8,128)S(1)}, f32[32,2048]{1,0:T(8,128)S(1)}, f32[32,2048]{1,0:T(8,128)S(1)}, f32[32,2048]{1,0:T(8,128)S(1)}) custom-call(bf16[32,2048]{1,0:T(8,128)(2,1)S(1)} %constant_dynamic-update-slice_fusion.refs_0_, bf16[32,2048]{1,0:T(8,128)(2,1)S(1)} %collective-permute-done.3.refs_1_, ...), custom_call_target="tpu_custom_call" | custom-call | flops 536870912 | bytes 4194304 | tf_op jit(solution)/shard_map/pallas_call | solution.py:159
  28.0 0.8 %shard_map.104 = (bf16[32,2048]{1,0:T(8,128)(2,1)S(1)}, bf16[32,2048]{1,0:T(8,128)(2,1)S(1)}, bf16[32,2048]{1,0:T(8,128)(2,1)S(1)}, bf16[32,2048]{1,0:T(8,128)(2,1)S(1)}) custom-call(bf16[32,2048]{1,0:T(8,128)(2,1)S(1)} %collective-permute-done.6.refs_0_, bf16[32,2048]{1,0:T(8,128)(2,1)S(1)} %collective-permute-done.7.refs_1_, ...), custom_call_target="tpu_custom_call" | custom-call | flops 536870912 | bytes 4194304 | tf_op jit(solution)/shard_map/pallas_call | solution.py:159
  28.8 0.6 %collective-permute-start.15 = (bf16[32,2048]{1,0:T(8,128)(2,1)S(1)}, bf16[32,2048]{1,0:T(8,128)(2,1)S(1)}, u32[]{:S(2)}, u32[]{:S(2)}) collective-permute-start(bf16[32,2048]{1,0:T(8,128)(2,1)S(1)} %get-tuple-element.40), channel_id=1, source_target_pairs={{0,1},{1,0},{2,3},{3,2},{4,5},{5,4},{6,7},{7,6},{8,9},{9,8},{10,11... | collective-permute-start | bytes 393224 | tf_op jit(solution)/shard_map/ppermute | solution.py:17
  29.4 0.1 collective-permute-start.13
  29.5 0.4 collective-permute-start.11
  29.9 0.1 collective-permute-start.10
  30.0 0.4 collective-permute-done.15
  30.4 0.5 %collective-permute-start.16 = (bf16[32,2048]{1,0:T(8,128)(2,1)S(1)}, bf16[32,2048]{1,0:T(8,128)(2,1)S(1)}, u32[]{:S(2)}, u32[]{:S(2)}) collective-permute-start(bf16[32,2048]{1,0:T(8,128)(2,1)S(1)} %add_convert_fusion), channel_id=1, source_target_pairs={{0,6},{1,7},{2,4},{3,5},{4,2},{5,3},{6,0},{7,1},{8,14},{9,15},{10,... | collective-permute-start | bytes 393224 | tf_op jit(solution)/shard_map/ppermute | solution.py:17
  31.0 1.6 %collective-permute-start.14 = (bf16[32,2048]{1,0:T(8,128)(2,1)S(1)}, bf16[32,2048]{1,0:T(8,128)(2,1)S(1)}, u32[]{:S(2)}, u32[]{:S(2)}) collective-permute-start(bf16[32,2048]{1,0:T(8,128)(2,1)S(1)} %add_convert_fusion.1), channel_id=1, source_target_pairs={{0,4},{1,5},{2,6},{3,7},{4,0},{5,1},{6,2},{7,3},{8,12},{9,13},{10,... | collective-permute-start | bytes 393224 | tf_op jit(solution)/shard_map/ppermute | solution.py:17
  32.6 1.6 %collective-permute-start.12 = (bf16[32,2048]{1,0:T(8,128)(2,1)S(1)}, bf16[32,2048]{1,0:T(8,128)(2,1)S(1)}, u32[]{:S(2)}, u32[]{:S(2)}) collective-permute-start(bf16[32,2048]{1,0:T(8,128)(2,1)S(1)} %add_convert_fusion.2), channel_id=1, source_target_pairs={{0,2},{1,3},{2,0},{3,1},{4,6},{5,7},{6,4},{7,5},{8,10},{9,11},{10,... | collective-permute-start | bytes 393224 | tf_op jit(solution)/shard_map/ppermute | solution.py:17
  34.3 3.5 %collective-permute-done.16 = bf16[32,2048]{1,0:T(8,128)(2,1)S(1)} collective-permute-done((bf16[32,2048]{1,0:T(8,128)(2,1)S(1)}, bf16[32,2048]{1,0:T(8,128)(2,1)S(1)}, u32[]{:S(2)}, u32[]{:S(2)}) %collective-permute-start.16) | collective-permute-done | bytes 131104 | tf_op jit(solution)/shard_map/ppermute | solution.py:17
  37.8 1.6 %collective-permute-done.14 = bf16[32,2048]{1,0:T(8,128)(2,1)S(1)} collective-permute-done((bf16[32,2048]{1,0:T(8,128)(2,1)S(1)}, bf16[32,2048]{1,0:T(8,128)(2,1)S(1)}, u32[]{:S(2)}, u32[]{:S(2)}) %collective-permute-start.14) | collective-permute-done | bytes 131104 | tf_op jit(solution)/shard_map/ppermute | solution.py:17
  39.4 0.1 collective-permute-done.12
  39.5 0.1 fusion.5
  39.6 0.6 %collective-permute-start.19 = (bf16[8,2048]{1,0:T(8,128)(2,1)S(1)}, bf16[8,2048]{1,0:T(8,128)(2,1)S(1)}, u32[]{:S(2)}, u32[]{:S(2)}) collective-permute-start(bf16[8,2048]{1,0:T(8,128)(2,1)S(1)} %get-tuple-element.44), channel_id=1, source_target_pairs={{0,24},{1,25},{2,26},{3,27},{4,28},{5,29},{6,30},{7,31},{8,16},{9,... | collective-permute-start | bytes 98312 | tf_op jit(solution)/shard_map/ppermute | solution.py:17
  40.3 3.8 %collective-permute-start.17 = (bf16[8,2048]{1,0:T(8,128)(2,1)S(1)}, bf16[8,2048]{1,0:T(8,128)(2,1)S(1)}, u32[]{:S(2)}, u32[]{:S(2)}) collective-permute-start(bf16[8,2048]{1,0:T(8,128)(2,1)S(1)} %get-tuple-element.43), channel_id=1, source_target_pairs={{0,8},{1,9},{2,10},{3,11},{4,12},{5,13},{6,14},{7,15},{8,0},{9,1},... | collective-permute-start | bytes 98312 | tf_op jit(solution)/shard_map/ppermute | solution.py:17
  44.0 1.3 %collective-permute-done.19 = bf16[8,2048]{1,0:T(8,128)(2,1)S(1)} collective-permute-done((bf16[8,2048]{1,0:T(8,128)(2,1)S(1)}, bf16[8,2048]{1,0:T(8,128)(2,1)S(1)}, u32[]{:S(2)}, u32[]{:S(2)}) %collective-permute-start.19) | collective-permute-done | bytes 32800 | tf_op jit(solution)/shard_map/ppermute | solution.py:17
  45.4 0.6 %collective-permute-done.17 = bf16[8,2048]{1,0:T(8,128)(2,1)S(1)} collective-permute-done((bf16[8,2048]{1,0:T(8,128)(2,1)S(1)}, bf16[8,2048]{1,0:T(8,128)(2,1)S(1)}, u32[]{:S(2)}, u32[]{:S(2)}) %collective-permute-start.17) | collective-permute-done | bytes 32800 | tf_op jit(solution)/shard_map/ppermute | solution.py:17
  45.9 0.7 %fusion.4 = bf16[8,2048]{1,0:T(8,128)(2,1)} fusion(f32[8,2048]{1,0:T(8,128)S(1)} %get-tuple-element.23, f32[32,2048]{1,0:T(8,128)S(1)} %get-tuple-element.42, bf16[8,2048]{1,0:T(8,128)(2,1)S(1)} %collective-permute-done.19, bf16[8,2048]{1,0:T(8,128)(2,1)S(1)} %collective-permute-done.18, bf16[8,2048]{1,0:T(8,128)(2,1)S(1)} %collective-permute-done.17, ...), kind=kLoop, calls=%fused_computation.9 | loop fusion | flops 196608 | bytes 262272 | tf_op jit(solution)/shard_map/convert_element_type | solution.py:261
  (30 shorter events, 0.3 us)
Async XLA Ops:
  3.5 5.7 %collective-permute-start = (bf16[8,2048]{1,0:T(8,128)(2,1)S(1)}, bf16[8,2048]{1,0:T(8,128)(2,1)S(1)}, u32[]{:S(2)}, u32[]{:S(2)}) collective-permute-start(bf16[8,2048]{1,0:T(8,128)(2,1)S(1)} %get-tuple-element.24), channel_id=1, source_target_pairs={{0,8},{1,9},{2,10},{3,11},{4,12},{5,13},{6,14},{7,15},{8,0},{9,1},... | collective-permute-start | bytes 98312 | tf_op jit(solution)/shard_map/ppermute | solution.py:17
  6.7 5.4 %collective-permute-start.1 = (bf16[8,2048]{1,0:T(8,128)(2,1)S(1)}, bf16[8,2048]{1,0:T(8,128)(2,1)S(1)}, u32[]{:S(2)}, u32[]{:S(2)}) collective-permute-start(bf16[8,2048]{1,0:T(8,128)(2,1)S(1)} %get-tuple-element.24), channel_id=1, source_target_pairs={{0,16},{1,17},{2,18},{3,19},{4,20},{5,21},{6,22},{7,23},{8,24},{9,... | collective-permute-start | bytes 98312 | tf_op jit(solution)/shard_map/ppermute | solution.py:17
  9.3 5.7 %collective-permute-start.2 = (bf16[8,2048]{1,0:T(8,128)(2,1)S(1)}, bf16[8,2048]{1,0:T(8,128)(2,1)S(1)}, u32[]{:S(2)}, u32[]{:S(2)}) collective-permute-start(bf16[8,2048]{1,0:T(8,128)(2,1)S(1)} %get-tuple-element.24), channel_id=1, source_target_pairs={{0,24},{1,25},{2,26},{3,27},{4,28},{5,29},{6,30},{7,31},{8,16},{9,... | collective-permute-start | bytes 98312 | tf_op jit(solution)/shard_map/ppermute | solution.py:17
  15.0 6.0 %collective-permute-start.3 = (bf16[32,2048]{1,0:T(8,128)(2,1)S(1)}, bf16[32,2048]{1,0:T(8,128)(2,1)S(1)}, u32[]{:S(2)}, u32[]{:S(2)}) collective-permute-start(bf16[32,2048]{1,0:T(8,128)(2,1)S(1)} %constant_dynamic-update-slice_fusion.refs_0_), channel_id=1, source_target_pairs={{0,2},{1,3},{2,0},{3,1},{4,6},{5,7},{6,4},{7,5},{8,10},{9,11},{10,... | collective-permute-start | bytes 393224 | tf_op jit(solution)/shard_map/ppermute | solution.py:17
  16.5 5.8 %collective-permute-start.4 = (bf16[32,2048]{1,0:T(8,128)(2,1)S(1)}, bf16[32,2048]{1,0:T(8,128)(2,1)S(1)}, u32[]{:S(2)}, u32[]{:S(2)}) collective-permute-start(bf16[32,2048]{1,0:T(8,128)(2,1)S(1)} %constant_dynamic-update-slice_fusion.refs_0_), channel_id=1, source_target_pairs={{0,4},{1,5},{2,6},{3,7},{4,0},{5,1},{6,2},{7,3},{8,12},{9,13},{10,... | collective-permute-start | bytes 393224 | tf_op jit(solution)/shard_map/ppermute | solution.py:17
  18.0 5.9 %collective-permute-start.5 = (bf16[32,2048]{1,0:T(8,128)(2,1)S(1)}, bf16[32,2048]{1,0:T(8,128)(2,1)S(1)}, u32[]{:S(2)}, u32[]{:S(2)}) collective-permute-start(bf16[32,2048]{1,0:T(8,128)(2,1)S(1)} %constant_dynamic-update-slice_fusion.refs_0_), channel_id=1, source_target_pairs={{0,6},{1,7},{2,4},{3,5},{4,2},{5,3},{6,0},{7,1},{8,14},{9,15},{10,... | collective-permute-start | bytes 393224 | tf_op jit(solution)/shard_map/ppermute | solution.py:17
  18.5 9.5 %collective-permute-start.6 = (bf16[32,2048]{1,0:T(8,128)(2,1)S(1)}, bf16[32,2048]{1,0:T(8,128)(2,1)S(1)}, u32[]{:S(2)}, u32[]{:S(2)}) collective-permute-start(bf16[32,2048]{1,0:T(8,128)(2,1)S(1)} %constant_dynamic-update-slice_fusion.refs_0_), channel_id=1, source_target_pairs={{0,1},{1,0},{2,3},{3,2},{4,5},{5,4},{6,7},{7,6},{8,9},{9,8},{10,11... | collective-permute-start | bytes 393224 | tf_op jit(solution)/shard_map/ppermute | solution.py:17
  21.0 6.9 %collective-permute-start.7 = (bf16[32,2048]{1,0:T(8,128)(2,1)S(1)}, bf16[32,2048]{1,0:T(8,128)(2,1)S(1)}, u32[]{:S(2)}, u32[]{:S(2)}) collective-permute-start(bf16[32,2048]{1,0:T(8,128)(2,1)S(1)} %collective-permute-done.3.refs_1_), channel_id=1, source_target_pairs={{0,1},{1,0},{2,3},{3,2},{4,5},{5,4},{6,7},{7,6},{8,9},{9,8},{10,11... | collective-permute-start | bytes 393224 | tf_op jit(solution)/shard_map/ppermute | solution.py:17
  22.2 5.7 %collective-permute-start.8 = (bf16[32,2048]{1,0:T(8,128)(2,1)S(1)}, bf16[32,2048]{1,0:T(8,128)(2,1)S(1)}, u32[]{:S(2)}, u32[]{:S(2)}) collective-permute-start(bf16[32,2048]{1,0:T(8,128)(2,1)S(1)} %collective-permute-done.4.refs_2_), channel_id=1, source_target_pairs={{0,1},{1,0},{2,3},{3,2},{4,5},{5,4},{6,7},{7,6},{8,9},{9,8},{10,11... | collective-permute-start | bytes 393224 | tf_op jit(solution)/shard_map/ppermute | solution.py:17
  23.9 4.1 %collective-permute-start.9 = (bf16[32,2048]{1,0:T(8,128)(2,1)S(1)}, bf16[32,2048]{1,0:T(8,128)(2,1)S(1)}, u32[]{:S(2)}, u32[]{:S(2)}) collective-permute-start(bf16[32,2048]{1,0:T(8,128)(2,1)S(1)} %collective-permute-done.5.refs_3_), channel_id=1, source_target_pairs={{0,1},{1,0},{2,3},{3,2},{4,5},{5,4},{6,7},{7,6},{8,9},{9,8},{10,11... | collective-permute-start | bytes 393224 | tf_op jit(solution)/shard_map/ppermute | solution.py:17
  28.0 6.2 %copy-start = (f32[8,2]{0,1:T(2,128)S(1)}, f32[8,2]{0,1:T(2,128)}, u32[]{:S(2)}) copy-start(f32[8,2]{0,1:T(2,128)} %param.19) | copy-start | bytes 196
  28.0 6.2 %copy-start.1 = (s32[8,2]{0,1:T(2,128)S(1)}, s32[8,2]{0,1:T(2,128)}, u32[]{:S(2)}) copy-start(s32[8,2]{0,1:T(2,128)} %param.18) | copy-start | bytes 196
  28.8 1.6 %collective-permute-start.15 = (bf16[32,2048]{1,0:T(8,128)(2,1)S(1)}, bf16[32,2048]{1,0:T(8,128)(2,1)S(1)}, u32[]{:S(2)}, u32[]{:S(2)}) collective-permute-start(bf16[32,2048]{1,0:T(8,128)(2,1)S(1)} %get-tuple-element.40), channel_id=1, source_target_pairs={{0,1},{1,0},{2,3},{3,2},{4,5},{5,4},{6,7},{7,6},{8,9},{9,8},{10,11... | collective-permute-start | bytes 393224 | tf_op jit(solution)/shard_map/ppermute | solution.py:17
  29.4 1.6 %collective-permute-start.13 = (bf16[32,2048]{1,0:T(8,128)(2,1)S(1)}, bf16[32,2048]{1,0:T(8,128)(2,1)S(1)}, u32[]{:S(2)}, u32[]{:S(2)}) collective-permute-start(bf16[32,2048]{1,0:T(8,128)(2,1)S(1)} %get-tuple-element.38), channel_id=1, source_target_pairs={{0,1},{1,0},{2,3},{3,2},{4,5},{5,4},{6,7},{7,6},{8,9},{9,8},{10,11... | collective-permute-start | bytes 393224 | tf_op jit(solution)/shard_map/ppermute | solution.py:17
  29.5 3.1 %collective-permute-start.11 = (bf16[32,2048]{1,0:T(8,128)(2,1)S(1)}, bf16[32,2048]{1,0:T(8,128)(2,1)S(1)}, u32[]{:S(2)}, u32[]{:S(2)}) collective-permute-start(bf16[32,2048]{1,0:T(8,128)(2,1)S(1)} %get-tuple-element.36), channel_id=1, source_target_pairs={{0,1},{1,0},{2,3},{3,2},{4,5},{5,4},{6,7},{7,6},{8,9},{9,8},{10,11... | collective-permute-start | bytes 393224 | tf_op jit(solution)/shard_map/ppermute | solution.py:17
  29.9 4.4 %collective-permute-start.10 = (bf16[32,2048]{1,0:T(8,128)(2,1)S(1)}, bf16[32,2048]{1,0:T(8,128)(2,1)S(1)}, u32[]{:S(2)}, u32[]{:S(2)}) collective-permute-start(bf16[32,2048]{1,0:T(8,128)(2,1)S(1)} %get-tuple-element.34), channel_id=1, source_target_pairs={{0,1},{1,0},{2,3},{3,2},{4,5},{5,4},{6,7},{7,6},{8,9},{9,8},{10,11... | collective-permute-start | bytes 393224 | tf_op jit(solution)/shard_map/ppermute | solution.py:17
  30.4 7.4 %collective-permute-start.16 = (bf16[32,2048]{1,0:T(8,128)(2,1)S(1)}, bf16[32,2048]{1,0:T(8,128)(2,1)S(1)}, u32[]{:S(2)}, u32[]{:S(2)}) collective-permute-start(bf16[32,2048]{1,0:T(8,128)(2,1)S(1)} %add_convert_fusion), channel_id=1, source_target_pairs={{0,6},{1,7},{2,4},{3,5},{4,2},{5,3},{6,0},{7,1},{8,14},{9,15},{10,... | collective-permute-start | bytes 393224 | tf_op jit(solution)/shard_map/ppermute | solution.py:17
  31.0 8.4 %collective-permute-start.14 = (bf16[32,2048]{1,0:T(8,128)(2,1)S(1)}, bf16[32,2048]{1,0:T(8,128)(2,1)S(1)}, u32[]{:S(2)}, u32[]{:S(2)}) collective-permute-start(bf16[32,2048]{1,0:T(8,128)(2,1)S(1)} %add_convert_fusion.1), channel_id=1, source_target_pairs={{0,4},{1,5},{2,6},{3,7},{4,0},{5,1},{6,2},{7,3},{8,12},{9,13},{10,... | collective-permute-start | bytes 393224 | tf_op jit(solution)/shard_map/ppermute | solution.py:17
  32.6 6.9 %collective-permute-start.12 = (bf16[32,2048]{1,0:T(8,128)(2,1)S(1)}, bf16[32,2048]{1,0:T(8,128)(2,1)S(1)}, u32[]{:S(2)}, u32[]{:S(2)}) collective-permute-start(bf16[32,2048]{1,0:T(8,128)(2,1)S(1)} %add_convert_fusion.2), channel_id=1, source_target_pairs={{0,2},{1,3},{2,0},{3,1},{4,6},{5,7},{6,4},{7,5},{8,10},{9,11},{10,... | collective-permute-start | bytes 393224 | tf_op jit(solution)/shard_map/ppermute | solution.py:17
  39.6 5.8 %collective-permute-start.19 = (bf16[8,2048]{1,0:T(8,128)(2,1)S(1)}, bf16[8,2048]{1,0:T(8,128)(2,1)S(1)}, u32[]{:S(2)}, u32[]{:S(2)}) collective-permute-start(bf16[8,2048]{1,0:T(8,128)(2,1)S(1)} %get-tuple-element.44), channel_id=1, source_target_pairs={{0,24},{1,25},{2,26},{3,27},{4,28},{5,29},{6,30},{7,31},{8,16},{9,... | collective-permute-start | bytes 98312 | tf_op jit(solution)/shard_map/ppermute | solution.py:17
  40.2 5.2 %collective-permute-start.18 = (bf16[8,2048]{1,0:T(8,128)(2,1)S(1)}, bf16[8,2048]{1,0:T(8,128)(2,1)S(1)}, u32[]{:S(2)}, u32[]{:S(2)}) collective-permute-start(bf16[8,2048]{1,0:T(8,128)(2,1)S(1)} %get-tuple-element.45), channel_id=1, source_target_pairs={{0,16},{1,17},{2,18},{3,19},{4,20},{5,21},{6,22},{7,23},{8,24},{9,... | collective-permute-start | bytes 98312 | tf_op jit(solution)/shard_map/ppermute | solution.py:17
  40.3 5.7 %collective-permute-start.17 = (bf16[8,2048]{1,0:T(8,128)(2,1)S(1)}, bf16[8,2048]{1,0:T(8,128)(2,1)S(1)}, u32[]{:S(2)}, u32[]{:S(2)}) collective-permute-start(bf16[8,2048]{1,0:T(8,128)(2,1)S(1)} %get-tuple-element.43), channel_id=1, source_target_pairs={{0,8},{1,9},{2,10},{3,11},{4,12},{5,13},{6,14},{7,15},{8,0},{9,1},... | collective-permute-start | bytes 98312 | tf_op jit(solution)/shard_map/ppermute | solution.py:17

commit v4 on v3

--- a/solution.py
+++ b/solution.py
@@ -187,6 +187,8 @@
     experts_count = devices // SPLIT
     capacity = max(2, min(streams, 4 * streams * SPLIT // devices))
     direct = experts_count <= 4
+    group = lax.shift_right_logical(lax.axis_index("expert"), SPLIT.bit_length() - 1)
+    group, src_lengths = lax.optimization_barrier((group, src_lengths))
     mixed, normed = attend(
         hidden_state,
         cross_query,
@@ -195,7 +197,6 @@
         src_lengths,
         norm_gain,
     )
-    group = lax.axis_index("expert") // SPLIT
     order = jnp.arange(experts_count, dtype=jnp.int32)
     if direct:
         order = order ^ group
@@ -231,20 +232,26 @@
     near_every = feed_forward([near[step] for step in range(chips)], w_in, w_out, jnp.float32)
     near_every, far = lax.optimization_barrier((near_every, far))
     far_sent = feed_forward([far[step] for step in range(chips)], w_in, w_out, jnp.bfloat16)
-    pair = {}
+    pair = [None] * chips
     for step in range(chips):
-        given = swap(far_sent[step], 1, devices)
-        pair[step] = near_every[step] + given.astype(jnp.float32)
-    total = pair[0]
-    for step in range(1, chips):
-        sent = pair[step].astype(jnp.bfloat16)
-        total = total + swap(sent, CORES * step, devices).astype(jnp.float32)
-    total = total.reshape(experts_count, capacity, width)
+        pair[step] = (near_every[step], swap(far_sent[step], 1, devices))
+    bounds = [("reduce_chip", slice(capacity, None)), ("reduce_own", slice(0, capacity))]
+    if not direct:
+        bounds = [("reduce_chip", slice(None))]
+    sums = {}
+    for name, place in bounds:
+        joined = [mine[place] + other[place].astype(jnp.float32) for mine, other in pair]
+        sums[name] = joined[0]
+        for step in range(1, chips):
+            given = swap(joined[step].astype(jnp.bfloat16), CORES * step, devices)
+            sums[name] = sums[name] + given.astype(jnp.float32)
+    total = sums["reduce_chip"].reshape(-1, capacity, width)
     result = mixed
     sent = total.astype(jnp.bfloat16)
     if direct:
-        back = {k: swap(sent[k], k * SPLIT, devices) for k in distances}
-        parts = [total[0]] + [back[k].astype(jnp.float32) for k in range(1, experts_count)]
+        back = {k: swap(sent[k - 1], k * SPLIT, devices) for k in distances}
+        parts = [sums["reduce_own"]]
+        parts += [back[k].astype(jnp.float32) for k in range(1, experts_count)]
     else:
         back = outer_exchange([sent[k] for k in range(experts_count)], devices)
         parts = [part.astype(jnp.float32) for part in back]

time: 46.8 us -> 47.8 us (1.021)
  starting transfers between devices: 18.5 us -> 22.1 us
  waiting for transfers between devices: 18.6 us -> 15.9 us
    ppermute x20 -> x23, starting transfers between devices: 18.5 us -> 22.1 us  [swap(): return lax.ppermute(value, 'expert', pairs)]
    ppermute x20 -> x23, waiting for transfers between devices: 18.6 us -> 15.9 us  [swap(): return lax.ppermute(value, 'expert', pairs)]
  transfers between devices with their start and end apart: 20 -> 23, of which waited for: 11 -> 10; matrix products, arithmetic and copies ran while one was open for 0% -> 1% of each run, Pallas kernels for 9% -> 8%
where the time goes in v4:
time: 47.8 us; the launch traced here: 47.6 us
  starting transfers between devices  22.1 us (46%)
  waiting for transfers between devices  15.9 us (33%)
  Pallas kernels  8.42 us (18%)
  other arithmetic  0.94 us (2%)
    ppermute x23, starting transfers between devices, swap(): return lax.ppermute(value, 'expert', pairs)  22.1 us
    ppermute x23, waiting for transfers between devices, swap(): return lax.ppermute(value, 'expert', pairs)  15.9 us
    pallas_call x1, Pallas kernels, attend(): pl.pallas_call(attend_kernel, out_shape=(pltpu.VMEM((streams, width), jnp...  3.54 us
    pallas_call x2, Pallas kernels, bring(): pl.pallas_call(kernel, out_shape=pltpu.VMEM(array.shape, array.dtype), in...  3.2 us
    pallas_call x2, Pallas kernels, feed_forward(): pl.pallas_call(kernel, out_shape=[jax.ShapeDtypeStruct(part.shape, kind)...  1.67 us
  transfers between devices with their start and end apart: 23, of which 10 were waited for; matrix products, arithmetic and copies ran while one was open for 1% of the time, Pallas kernels for 8%

profile of v4, /device:TPU:0, one launch (start us, length us, event | category | flops | bytes accessed | tf_op | source)
XLA Modules:
  0.0 47.6 jit_solution(11558027973405261940)
XLA Ops:
  0.0 3.5 %shard_map.100 = (f32[8,2048]{1,0:T(8,128)S(1)}, bf16[8,2048]{1,0:T(8,128)(2,1)S(1)}) custom-call(s32[8]{0:T(128)} %lengths_in, bf16[8,2048]{1,0:T(8,128)(2,1)} %hidden_in.1, bf16[8,2048]{1,0:T(8,128)(2,1)} %query_in.1, bf16[8,64,2048]{2,1,0:T(8,128)(2,1)} %keys.1, bf16[8,64,2048]{2,1,0:T(8,128)(2,1)} %values.1, f32[1,2048]{1,0:T(1,128)} %bitcast.9), custom_call_target="tpu_custom_call" | custom-call | tf_op jit(solution)/shard_map/pallas_call | solution.py:104
  3.5 3.1 %collective-permute-start = (bf16[8,2048]{1,0:T(8,128)(2,1)S(1)}, bf16[8,2048]{1,0:T(8,128)(2,1)S(1)}, u32[]{:S(2)}, u32[]{:S(2)}) collective-permute-start(bf16[8,2048]{1,0:T(8,128)(2,1)S(1)} %get-tuple-element.28), channel_id=1, source_target_pairs={{0,8},{1,9},{2,10},{3,11},{4,12},{5,13},{6,14},{7,15},{8,0},{9,1},... | collective-permute-start | bytes 98312 | tf_op jit(solution)/shard_map/ppermute | solution.py:17
  6.7 2.6 %collective-permute-start.1 = (bf16[8,2048]{1,0:T(8,128)(2,1)S(1)}, bf16[8,2048]{1,0:T(8,128)(2,1)S(1)}, u32[]{:S(2)}, u32[]{:S(2)}) collective-permute-start(bf16[8,2048]{1,0:T(8,128)(2,1)S(1)} %get-tuple-element.28), channel_id=1, source_target_pairs={{0,16},{1,17},{2,18},{3,19},{4,20},{5,21},{6,22},{7,23},{8,24},{9,... | collective-permute-start | bytes 98312 | tf_op jit(solution)/shard_map/ppermute | solution.py:17
  9.3 2.8 %collective-permute-done.1 = bf16[8,2048]{1,0:T(8,128)(2,1)S(1)} collective-permute-done((bf16[8,2048]{1,0:T(8,128)(2,1)S(1)}, bf16[8,2048]{1,0:T(8,128)(2,1)S(1)}, u32[]{:S(2)}, u32[]{:S(2)}) %collective-permute-start.1) | collective-permute-done | bytes 32800 | tf_op jit(solution)/shard_map/ppermute | solution.py:17
  12.1 2.9 %collective-permute-done.2 = bf16[8,2048]{1,0:T(8,128)(2,1)S(1)} collective-permute-done((bf16[8,2048]{1,0:T(8,128)(2,1)S(1)}, bf16[8,2048]{1,0:T(8,128)(2,1)S(1)}, u32[]{:S(2)}, u32[]{:S(2)}) %collective-permute-start.2) | collective-permute-done | bytes 32800 | tf_op jit(solution)/shard_map/ppermute | solution.py:17
  15.0 1.5 %collective-permute-start.3 = (bf16[32,2048]{1,0:T(8,128)(2,1)S(1)}, bf16[32,2048]{1,0:T(8,128)(2,1)S(1)}, u32[]{:S(2)}, u32[]{:S(2)}) collective-permute-start(bf16[32,2048]{1,0:T(8,128)(2,1)S(1)} %constant_dynamic-update-slice_fusion.refs_0_), channel_id=1, source_target_pairs={{0,2},{1,3},{2,0},{3,1},{4,6},{5,7},{6,4},{7,5},{8,10},{9,11},{10,... | collective-permute-start | bytes 393224 | tf_op jit(solution)/shard_map/ppermute | solution.py:17
  16.5 1.5 %collective-permute-start.4 = (bf16[32,2048]{1,0:T(8,128)(2,1)S(1)}, bf16[32,2048]{1,0:T(8,128)(2,1)S(1)}, u32[]{:S(2)}, u32[]{:S(2)}) collective-permute-start(bf16[32,2048]{1,0:T(8,128)(2,1)S(1)} %constant_dynamic-update-slice_fusion.refs_0_), channel_id=1, source_target_pairs={{0,4},{1,5},{2,6},{3,7},{4,0},{5,1},{6,2},{7,3},{8,12},{9,13},{10,... | collective-permute-start | bytes 393224 | tf_op jit(solution)/shard_map/ppermute | solution.py:17
  18.0 0.5 %collective-permute-start.5 = (bf16[32,2048]{1,0:T(8,128)(2,1)S(1)}, bf16[32,2048]{1,0:T(8,128)(2,1)S(1)}, u32[]{:S(2)}, u32[]{:S(2)}) collective-permute-start(bf16[32,2048]{1,0:T(8,128)(2,1)S(1)} %constant_dynamic-update-slice_fusion.refs_0_), channel_id=1, source_target_pairs={{0,6},{1,7},{2,4},{3,5},{4,2},{5,3},{6,0},{7,1},{8,14},{9,15},{10,... | collective-permute-start | bytes 393224 | tf_op jit(solution)/shard_map/ppermute | solution.py:17
  18.5 2.5 %collective-permute-done.3.refs_1_ = bf16[32,2048]{1,0:T(8,128)(2,1)S(1)} collective-permute-done((bf16[32,2048]{1,0:T(8,128)(2,1)S(1)}, bf16[32,2048]{1,0:T(8,128)(2,1)S(1)}, u32[]{:S(2)}, u32[]{:S(2)}) %collective-permute-start.3) | collective-permute-done | bytes 131104 | tf_op jit(solution)/shard_map/ppermute | solution.py:17
  21.0 1.2 %collective-permute-done.4.refs_2_ = bf16[32,2048]{1,0:T(8,128)(2,1)S(1)} collective-permute-done((bf16[32,2048]{1,0:T(8,128)(2,1)S(1)}, bf16[32,2048]{1,0:T(8,128)(2,1)S(1)}, u32[]{:S(2)}, u32[]{:S(2)}) %collective-permute-start.4) | collective-permute-done | bytes 131104 | tf_op jit(solution)/shard_map/ppermute | solution.py:17
  22.2 1.6 %collective-permute-done.5.refs_3_ = bf16[32,2048]{1,0:T(8,128)(2,1)S(1)} collective-permute-done((bf16[32,2048]{1,0:T(8,128)(2,1)S(1)}, bf16[32,2048]{1,0:T(8,128)(2,1)S(1)}, u32[]{:S(2)}, u32[]{:S(2)}) %collective-permute-start.5) | collective-permute-done | bytes 131104 | tf_op jit(solution)/shard_map/ppermute | solution.py:17
  23.9 1.6 %shard_map.101.refs_4_ = bf16[2048,512]{1,0:T(8,128)(2,1)S(1)} custom-call(bf16[2048,512]{1,0:T(8,128)(2,1)} %source.2), custom_call_target="tpu_custom_call" | custom-call | tf_op jit(solution)/shard_map/pallas_call | solution.py:134
  25.5 1.6 %shard_map.102.refs_5_ = bf16[512,2048]{1,0:T(8,128)(2,1)S(1)} custom-call(bf16[512,2048]{1,0:T(8,128)(2,1)} %source.3), custom_call_target="tpu_custom_call" | custom-call | tf_op jit(solution)/shard_map/pallas_call | solution.py:134
  27.1 0.8 %shard_map.103 = (f32[32,2048]{1,0:T(8,128)S(1)}, f32[32,2048]{1,0:T(8,128)S(1)}, f32[32,2048]{1,0:T(8,128)S(1)}, f32[32,2048]{1,0:T(8,128)S(1)}) custom-call(bf16[32,2048]{1,0:T(8,128)(2,1)S(1)} %constant_dynamic-update-slice_fusion.refs_0_, bf16[32,2048]{1,0:T(8,128)(2,1)S(1)} %collective-permute-done.3.refs_1_, ...), custom_call_target="tpu_custom_call" | custom-call | flops 536870912 | bytes 4194304 | tf_op jit(solution)/shard_map/pallas_call | solution.py:159
  28.0 0.8 %shard_map.104 = (bf16[32,2048]{1,0:T(8,128)(2,1)S(1)}, bf16[32,2048]{1,0:T(8,128)(2,1)S(1)}, bf16[32,2048]{1,0:T(8,128)(2,1)S(1)}, bf16[32,2048]{1,0:T(8,128)(2,1)S(1)}) custom-call(bf16[32,2048]{1,0:T(8,128)(2,1)S(1)} %collective-permute-done.6.refs_0_, bf16[32,2048]{1,0:T(8,128)(2,1)S(1)} %collective-permute-done.7.refs_1_, ...), custom_call_target="tpu_custom_call" | custom-call | flops 536870912 | bytes 4194304 | tf_op jit(solution)/shard_map/pallas_call | solution.py:159
  28.8 0.6 %collective-permute-start.11 = (bf16[32,2048]{1,0:T(8,128)(2,1)S(1)}, bf16[32,2048]{1,0:T(8,128)(2,1)S(1)}, u32[]{:S(2)}, u32[]{:S(2)}) collective-permute-start(bf16[32,2048]{1,0:T(8,128)(2,1)S(1)} %get-tuple-element.40), channel_id=1, source_target_pairs={{0,1},{1,0},{2,3},{3,2},{4,5},{5,4},{6,7},{7,6},{8,9},{9,8},{10,11... | collective-permute-start | bytes 393224 | tf_op jit(solution)/shard_map/ppermute | solution.py:17
  29.4 0.1 select_reduce_fusion
  29.5 0.5 collective-permute-start.15
  30.1 0.3 collective-permute-done.11
  30.4 0.6 %collective-permute-start.12 = (bf16[8,2048]{1,0:T(8,128)(2,1)S(1)}, bf16[8,2048]{1,0:T(8,128)(2,1)S(1)}, u32[]{:S(2)}, u32[]{:S(2)}) collective-permute-start(bf16[8,2048]{1,0:T(8,128)(2,1)S(1)} %add_convert_fusion.7), channel_id=1, source_target_pairs={{0,2},{1,3},{2,0},{3,1},{4,6},{5,7},{6,4},{7,5},{8,10},{9,11},{10,... | collective-permute-start | bytes 98312 | tf_op jit(solution)/shard_map/ppermute | solution.py:17
  31.0 1.6 %collective-permute-start.17 = (bf16[24,2048]{1,0:T(8,128)(2,1)S(1)}, bf16[24,2048]{1,0:T(8,128)(2,1)S(1)}, u32[]{:S(2)}, u32[]{:S(2)}) collective-permute-start(bf16[24,2048]{1,0:T(8,128)(2,1)S(1)} %add_convert_fusion.3), channel_id=1, source_target_pairs={{0,2},{1,3},{2,0},{3,1},{4,6},{5,7},{6,4},{7,5},{8,10},{9,11},{10,... | collective-permute-start | bytes 294920 | tf_op jit(solution)/shard_map/ppermute | solution.py:17
  32.6 1.2 %collective-permute-start.18 = (bf16[24,2048]{1,0:T(8,128)(2,1)S(1)}, bf16[24,2048]{1,0:T(8,128)(2,1)S(1)}, u32[]{:S(2)}, u32[]{:S(2)}) collective-permute-start(bf16[24,2048]{1,0:T(8,128)(2,1)S(1)} %add_convert_fusion.2), channel_id=1, source_target_pairs={{0,4},{1,5},{2,6},{3,7},{4,0},{5,1},{6,2},{7,3},{8,12},{9,13},{10,... | collective-permute-start | bytes 294920 | tf_op jit(solution)/shard_map/ppermute | solution.py:17
  33.9 0.9 %collective-permute-start.19 = (bf16[24,2048]{1,0:T(8,128)(2,1)S(1)}, bf16[24,2048]{1,0:T(8,128)(2,1)S(1)}, u32[]{:S(2)}, u32[]{:S(2)}) collective-permute-start(bf16[24,2048]{1,0:T(8,128)(2,1)S(1)} %add_convert_fusion.1), channel_id=1, source_target_pairs={{0,6},{1,7},{2,4},{3,5},{4,2},{5,3},{6,0},{7,1},{8,14},{9,15},{10,... | collective-permute-start | bytes 294920 | tf_op jit(solution)/shard_map/ppermute | solution.py:17
  34.8 0.7 %collective-permute-start.14 = (bf16[8,2048]{1,0:T(8,128)(2,1)S(1)}, bf16[8,2048]{1,0:T(8,128)(2,1)S(1)}, u32[]{:S(2)}, u32[]{:S(2)}) collective-permute-start(bf16[8,2048]{1,0:T(8,128)(2,1)S(1)} %add_convert_fusion.6), channel_id=1, source_target_pairs={{0,4},{1,5},{2,6},{3,7},{4,0},{5,1},{6,2},{7,3},{8,12},{9,13},{10,... | collective-permute-start | bytes 98312 | tf_op jit(solution)/shard_map/ppermute | solution.py:17
  35.5 0.7 %collective-permute-done.17 = bf16[24,2048]{1,0:T(8,128)(2,1)S(1)} collective-permute-done((bf16[24,2048]{1,0:T(8,128)(2,1)S(1)}, bf16[24,2048]{1,0:T(8,128)(2,1)S(1)}, u32[]{:S(2)}, u32[]{:S(2)}) %collective-permute-start.17) | collective-permute-done | bytes 98336 | tf_op jit(solution)/shard_map/ppermute | solution.py:17
  36.2 2.3 %collective-permute-start.16 = (bf16[8,2048]{1,0:T(8,128)(2,1)S(1)}, bf16[8,2048]{1,0:T(8,128)(2,1)S(1)}, u32[]{:S(2)}, u32[]{:S(2)}) collective-permute-start(bf16[8,2048]{1,0:T(8,128)(2,1)S(1)} %add_convert_fusion.5), channel_id=1, source_target_pairs={{0,6},{1,7},{2,4},{3,5},{4,2},{5,3},{6,0},{7,1},{8,14},{9,15},{10,... | collective-permute-start | bytes 98312 | tf_op jit(solution)/shard_map/ppermute | solution.py:17
  38.5 1.6 %collective-permute-done.18 = bf16[24,2048]{1,0:T(8,128)(2,1)S(1)} collective-permute-done((bf16[24,2048]{1,0:T(8,128)(2,1)S(1)}, bf16[24,2048]{1,0:T(8,128)(2,1)S(1)}, u32[]{:S(2)}, u32[]{:S(2)}) %collective-permute-start.18) | collective-permute-done | bytes 98336 | tf_op jit(solution)/shard_map/ppermute | solution.py:17
  40.3 0.9 %collective-permute-start.21 = (bf16[8,2048]{1,0:T(8,128)(2,1)S(1)}, bf16[8,2048]{1,0:T(8,128)(2,1)S(1)}, u32[]{:S(2)}, u32[]{:S(2)}) collective-permute-start(bf16[8,2048]{1,0:T(8,128)(2,1)S(1)} %get-tuple-element.47), channel_id=1, source_target_pairs={{0,16},{1,17},{2,18},{3,19},{4,20},{5,21},{6,22},{7,23},{8,24},{9,... | collective-permute-start | bytes 98312 | tf_op jit(solution)/shard_map/ppermute | solution.py:17
  41.2 3.5 %collective-permute-start.22 = (bf16[8,2048]{1,0:T(8,128)(2,1)S(1)}, bf16[8,2048]{1,0:T(8,128)(2,1)S(1)}, u32[]{:S(2)}, u32[]{:S(2)}) collective-permute-start(bf16[8,2048]{1,0:T(8,128)(2,1)S(1)} %get-tuple-element.46), channel_id=1, source_target_pairs={{0,24},{1,25},{2,26},{3,27},{4,28},{5,29},{6,30},{7,31},{8,16},{9,... | collective-permute-start | bytes 98312 | tf_op jit(solution)/shard_map/ppermute | solution.py:17
  44.7 0.5 %collective-permute-done.21 = bf16[8,2048]{1,0:T(8,128)(2,1)S(1)} collective-permute-done((bf16[8,2048]{1,0:T(8,128)(2,1)S(1)}, bf16[8,2048]{1,0:T(8,128)(2,1)S(1)}, u32[]{:S(2)}, u32[]{:S(2)}) %collective-permute-start.21) | collective-permute-done | bytes 32800 | tf_op jit(solution)/shard_map/ppermute | solution.py:17
  45.1 1.7 %collective-permute-done.22 = bf16[8,2048]{1,0:T(8,128)(2,1)S(1)} collective-permute-done((bf16[8,2048]{1,0:T(8,128)(2,1)S(1)}, bf16[8,2048]{1,0:T(8,128)(2,1)S(1)}, u32[]{:S(2)}, u32[]{:S(2)}) %collective-permute-start.22) | collective-permute-done | bytes 32800 | tf_op jit(solution)/shard_map/ppermute | solution.py:17
  46.9 0.7 %add_convert_fusion.4 = bf16[8,2048]{1,0:T(8,128)(2,1)} fusion(bf16[8,2048]{1,0:T(8,128)(2,1)S(1)} %collective-permute-done.22, bf16[8,2048]{1,0:T(8,128)(2,1)S(1)} %collective-permute-done.21, bf16[8,2048]{1,0:T(8,128)(2,1)S(1)} %collective-permute-done.20, f32[8,2048]{1,0:T(8,128)S(1)} %get-tuple-element.26, ...), kind=kLoop, calls=%fused_computation.4 | loop fusion | flops 327680 | bytes 393344 | tf_op jit(solution)/shard_map/convert_element_type | solution.py:268
  (39 shorter events, 0.4 us)
Async XLA Ops:
  3.5 5.7 %collective-permute-start = (bf16[8,2048]{1,0:T(8,128)(2,1)S(1)}, bf16[8,2048]{1,0:T(8,128)(2,1)S(1)}, u32[]{:S(2)}, u32[]{:S(2)}) collective-permute-start(bf16[8,2048]{1,0:T(8,128)(2,1)S(1)} %get-tuple-element.28), channel_id=1, source_target_pairs={{0,8},{1,9},{2,10},{3,11},{4,12},{5,13},{6,14},{7,15},{8,0},{9,1},... | collective-permute-start | bytes 98312 | tf_op jit(solution)/shard_map/ppermute | solution.py:17
  6.7 5.4 %collective-permute-start.1 = (bf16[8,2048]{1,0:T(8,128)(2,1)S(1)}, bf16[8,2048]{1,0:T(8,128)(2,1)S(1)}, u32[]{:S(2)}, u32[]{:S(2)}) collective-permute-start(bf16[8,2048]{1,0:T(8,128)(2,1)S(1)} %get-tuple-element.28), channel_id=1, source_target_pairs={{0,16},{1,17},{2,18},{3,19},{4,20},{5,21},{6,22},{7,23},{8,24},{9,... | collective-permute-start | bytes 98312 | tf_op jit(solution)/shard_map/ppermute | solution.py:17
  9.3 5.7 %collective-permute-start.2 = (bf16[8,2048]{1,0:T(8,128)(2,1)S(1)}, bf16[8,2048]{1,0:T(8,128)(2,1)S(1)}, u32[]{:S(2)}, u32[]{:S(2)}) collective-permute-start(bf16[8,2048]{1,0:T(8,128)(2,1)S(1)} %get-tuple-element.28), channel_id=1, source_target_pairs={{0,24},{1,25},{2,26},{3,27},{4,28},{5,29},{6,30},{7,31},{8,16},{9,... | collective-permute-start | bytes 98312 | tf_op jit(solution)/shard_map/ppermute | solution.py:17
  15.0 6.0 %collective-permute-start.3 = (bf16[32,2048]{1,0:T(8,128)(2,1)S(1)}, bf16[32,2048]{1,0:T(8,128)(2,1)S(1)}, u32[]{:S(2)}, u32[]{:S(2)}) collective-permute-start(bf16[32,2048]{1,0:T(8,128)(2,1)S(1)} %constant_dynamic-update-slice_fusion.refs_0_), channel_id=1, source_target_pairs={{0,2},{1,3},{2,0},{3,1},{4,6},{5,7},{6,4},{7,5},{8,10},{9,11},{10,... | collective-permute-start | bytes 393224 | tf_op jit(solution)/shard_map/ppermute | solution.py:17
  16.5 5.8 %collective-permute-start.4 = (bf16[32,2048]{1,0:T(8,128)(2,1)S(1)}, bf16[32,2048]{1,0:T(8,128)(2,1)S(1)}, u32[]{:S(2)}, u32[]{:S(2)}) collective-permute-start(bf16[32,2048]{1,0:T(8,128)(2,1)S(1)} %constant_dynamic-update-slice_fusion.refs_0_), channel_id=1, source_target_pairs={{0,4},{1,5},{2,6},{3,7},{4,0},{5,1},{6,2},{7,3},{8,12},{9,13},{10,... | collective-permute-start | bytes 393224 | tf_op jit(solution)/shard_map/ppermute | solution.py:17
  18.0 5.9 %collective-permute-start.5 = (bf16[32,2048]{1,0:T(8,128)(2,1)S(1)}, bf16[32,2048]{1,0:T(8,128)(2,1)S(1)}, u32[]{:S(2)}, u32[]{:S(2)}) collective-permute-start(bf16[32,2048]{1,0:T(8,128)(2,1)S(1)} %constant_dynamic-update-slice_fusion.refs_0_), channel_id=1, source_target_pairs={{0,6},{1,7},{2,4},{3,5},{4,2},{5,3},{6,0},{7,1},{8,14},{9,15},{10,... | collective-permute-start | bytes 393224 | tf_op jit(solution)/shard_map/ppermute | solution.py:17
  18.5 9.5 %collective-permute-start.6 = (bf16[32,2048]{1,0:T(8,128)(2,1)S(1)}, bf16[32,2048]{1,0:T(8,128)(2,1)S(1)}, u32[]{:S(2)}, u32[]{:S(2)}) collective-permute-start(bf16[32,2048]{1,0:T(8,128)(2,1)S(1)} %constant_dynamic-update-slice_fusion.refs_0_), channel_id=1, source_target_pairs={{0,1},{1,0},{2,3},{3,2},{4,5},{5,4},{6,7},{7,6},{8,9},{9,8},{10,11... | collective-permute-start | bytes 393224 | tf_op jit(solution)/shard_map/ppermute | solution.py:17
  21.0 6.9 %collective-permute-start.7 = (bf16[32,2048]{1,0:T(8,128)(2,1)S(1)}, bf16[32,2048]{1,0:T(8,128)(2,1)S(1)}, u32[]{:S(2)}, u32[]{:S(2)}) collective-permute-start(bf16[32,2048]{1,0:T(8,128)(2,1)S(1)} %collective-permute-done.3.refs_1_), channel_id=1, source_target_pairs={{0,1},{1,0},{2,3},{3,2},{4,5},{5,4},{6,7},{7,6},{8,9},{9,8},{10,11... | collective-permute-start | bytes 393224 | tf_op jit(solution)/shard_map/ppermute | solution.py:17
  22.2 5.7 %collective-permute-start.8 = (bf16[32,2048]{1,0:T(8,128)(2,1)S(1)}, bf16[32,2048]{1,0:T(8,128)(2,1)S(1)}, u32[]{:S(2)}, u32[]{:S(2)}) collective-permute-start(bf16[32,2048]{1,0:T(8,128)(2,1)S(1)} %collective-permute-done.4.refs_2_), channel_id=1, source_target_pairs={{0,1},{1,0},{2,3},{3,2},{4,5},{5,4},{6,7},{7,6},{8,9},{9,8},{10,11... | collective-permute-start | bytes 393224 | tf_op jit(solution)/shard_map/ppermute | solution.py:17
  23.9 4.1 %collective-permute-start.9 = (bf16[32,2048]{1,0:T(8,128)(2,1)S(1)}, bf16[32,2048]{1,0:T(8,128)(2,1)S(1)}, u32[]{:S(2)}, u32[]{:S(2)}) collective-permute-start(bf16[32,2048]{1,0:T(8,128)(2,1)S(1)} %collective-permute-done.5.refs_3_), channel_id=1, source_target_pairs={{0,1},{1,0},{2,3},{3,2},{4,5},{5,4},{6,7},{7,6},{8,9},{9,8},{10,11... | collective-permute-start | bytes 393224 | tf_op jit(solution)/shard_map/ppermute | solution.py:17
  28.0 1.4 %copy-start = (f32[8,2]{0,1:T(2,128)S(1)}, f32[8,2]{0,1:T(2,128)}, u32[]{:S(2)}) copy-start(f32[8,2]{0,1:T(2,128)} %param.19) | copy-start | bytes 196
  28.0 1.4 %copy-start.1 = (s32[8,2]{0,1:T(2,128)S(1)}, s32[8,2]{0,1:T(2,128)}, u32[]{:S(2)}) copy-start(s32[8,2]{0,1:T(2,128)} %param.18) | copy-start | bytes 196
  28.8 1.6 %collective-permute-start.11 = (bf16[32,2048]{1,0:T(8,128)(2,1)S(1)}, bf16[32,2048]{1,0:T(8,128)(2,1)S(1)}, u32[]{:S(2)}, u32[]{:S(2)}) collective-permute-start(bf16[32,2048]{1,0:T(8,128)(2,1)S(1)} %get-tuple-element.40), channel_id=1, source_target_pairs={{0,1},{1,0},{2,3},{3,2},{4,5},{5,4},{6,7},{7,6},{8,9},{9,8},{10,11... | collective-permute-start | bytes 393224 | tf_op jit(solution)/shard_map/ppermute | solution.py:17
  29.5 3.1 %collective-permute-start.13 = (bf16[32,2048]{1,0:T(8,128)(2,1)S(1)}, bf16[32,2048]{1,0:T(8,128)(2,1)S(1)}, u32[]{:S(2)}, u32[]{:S(2)}) collective-permute-start(bf16[32,2048]{1,0:T(8,128)(2,1)S(1)} %get-tuple-element.42), channel_id=1, source_target_pairs={{0,1},{1,0},{2,3},{3,2},{4,5},{5,4},{6,7},{7,6},{8,9},{9,8},{10,11... | collective-permute-start | bytes 393224 | tf_op jit(solution)/shard_map/ppermute | solution.py:17
  29.5 4.3 %collective-permute-start.15 = (bf16[32,2048]{1,0:T(8,128)(2,1)S(1)}, bf16[32,2048]{1,0:T(8,128)(2,1)S(1)}, u32[]{:S(2)}, u32[]{:S(2)}) collective-permute-start(bf16[32,2048]{1,0:T(8,128)(2,1)S(1)} %get-tuple-element.44), channel_id=1, source_target_pairs={{0,1},{1,0},{2,3},{3,2},{4,5},{5,4},{6,7},{7,6},{8,9},{9,8},{10,11... | collective-permute-start | bytes 393224 | tf_op jit(solution)/shard_map/ppermute | solution.py:17
  30.0 4.8 %collective-permute-start.10 = (bf16[32,2048]{1,0:T(8,128)(2,1)S(1)}, bf16[32,2048]{1,0:T(8,128)(2,1)S(1)}, u32[]{:S(2)}, u32[]{:S(2)}) collective-permute-start(bf16[32,2048]{1,0:T(8,128)(2,1)S(1)} %get-tuple-element.38), channel_id=1, source_target_pairs={{0,1},{1,0},{2,3},{3,2},{4,5},{5,4},{6,7},{7,6},{8,9},{9,8},{10,11... | collective-permute-start | bytes 393224 | tf_op jit(solution)/shard_map/ppermute | solution.py:17
  30.4 10.8 %collective-permute-start.12 = (bf16[8,2048]{1,0:T(8,128)(2,1)S(1)}, bf16[8,2048]{1,0:T(8,128)(2,1)S(1)}, u32[]{:S(2)}, u32[]{:S(2)}) collective-permute-start(bf16[8,2048]{1,0:T(8,128)(2,1)S(1)} %add_convert_fusion.7), channel_id=1, source_target_pairs={{0,2},{1,3},{2,0},{3,1},{4,6},{5,7},{6,4},{7,5},{8,10},{9,11},{10,... | collective-permute-start | bytes 98312 | tf_op jit(solution)/shard_map/ppermute | solution.py:17
  31.0 5.2 %collective-permute-start.17 = (bf16[24,2048]{1,0:T(8,128)(2,1)S(1)}, bf16[24,2048]{1,0:T(8,128)(2,1)S(1)}, u32[]{:S(2)}, u32[]{:S(2)}) collective-permute-start(bf16[24,2048]{1,0:T(8,128)(2,1)S(1)} %add_convert_fusion.3), channel_id=1, source_target_pairs={{0,2},{1,3},{2,0},{3,1},{4,6},{5,7},{6,4},{7,5},{8,10},{9,11},{10,... | collective-permute-start | bytes 294920 | tf_op jit(solution)/shard_map/ppermute | solution.py:17
  32.6 7.5 %collective-permute-start.18 = (bf16[24,2048]{1,0:T(8,128)(2,1)S(1)}, bf16[24,2048]{1,0:T(8,128)(2,1)S(1)}, u32[]{:S(2)}, u32[]{:S(2)}) collective-permute-start(bf16[24,2048]{1,0:T(8,128)(2,1)S(1)} %add_convert_fusion.2), channel_id=1, source_target_pairs={{0,4},{1,5},{2,6},{3,7},{4,0},{5,1},{6,2},{7,3},{8,12},{9,13},{10,... | collective-permute-start | bytes 294920 | tf_op jit(solution)/shard_map/ppermute | solution.py:17
  33.9 6.2 %collective-permute-start.19 = (bf16[24,2048]{1,0:T(8,128)(2,1)S(1)}, bf16[24,2048]{1,0:T(8,128)(2,1)S(1)}, u32[]{:S(2)}, u32[]{:S(2)}) collective-permute-start(bf16[24,2048]{1,0:T(8,128)(2,1)S(1)} %add_convert_fusion.1), channel_id=1, source_target_pairs={{0,6},{1,7},{2,4},{3,5},{4,2},{5,3},{6,0},{7,1},{8,14},{9,15},{10,... | collective-permute-start | bytes 294920 | tf_op jit(solution)/shard_map/ppermute | solution.py:17
  34.8 9.8 %collective-permute-start.14 = (bf16[8,2048]{1,0:T(8,128)(2,1)S(1)}, bf16[8,2048]{1,0:T(8,128)(2,1)S(1)}, u32[]{:S(2)}, u32[]{:S(2)}) collective-permute-start(bf16[8,2048]{1,0:T(8,128)(2,1)S(1)} %add_convert_fusion.6), channel_id=1, source_target_pairs={{0,4},{1,5},{2,6},{3,7},{4,0},{5,1},{6,2},{7,3},{8,12},{9,13},{10,... | collective-permute-start | bytes 98312 | tf_op jit(solution)/shard_map/ppermute | solution.py:17
  36.2 8.4 %collective-permute-start.16 = (bf16[8,2048]{1,0:T(8,128)(2,1)S(1)}, bf16[8,2048]{1,0:T(8,128)(2,1)S(1)}, u32[]{:S(2)}, u32[]{:S(2)}) collective-permute-start(bf16[8,2048]{1,0:T(8,128)(2,1)S(1)} %add_convert_fusion.5), channel_id=1, source_target_pairs={{0,6},{1,7},{2,4},{3,5},{4,2},{5,3},{6,0},{7,1},{8,14},{9,15},{10,... | collective-permute-start | bytes 98312 | tf_op jit(solution)/shard_map/ppermute | solution.py:17
  40.2 4.5 %collective-permute-start.20 = (bf16[8,2048]{1,0:T(8,128)(2,1)S(1)}, bf16[8,2048]{1,0:T(8,128)(2,1)S(1)}, u32[]{:S(2)}, u32[]{:S(2)}) collective-permute-start(bf16[8,2048]{1,0:T(8,128)(2,1)S(1)} %get-tuple-element.45), channel_id=1, source_target_pairs={{0,8},{1,9},{2,10},{3,11},{4,12},{5,13},{6,14},{7,15},{8,0},{9,1},... | collective-permute-start | bytes 98312 | tf_op jit(solution)/shard_map/ppermute | solution.py:17
  40.3 4.9 %collective-permute-start.21 = (bf16[8,2048]{1,0:T(8,128)(2,1)S(1)}, bf16[8,2048]{1,0:T(8,128)(2,1)S(1)}, u32[]{:S(2)}, u32[]{:S(2)}) collective-permute-start(bf16[8,2048]{1,0:T(8,128)(2,1)S(1)} %get-tuple-element.47), channel_id=1, source_target_pairs={{0,16},{1,17},{2,18},{3,19},{4,20},{5,21},{6,22},{7,23},{8,24},{9,... | collective-permute-start | bytes 98312 | tf_op jit(solution)/shard_map/ppermute | solution.py:17
  41.2 5.7 %collective-permute-start.22 = (bf16[8,2048]{1,0:T(8,128)(2,1)S(1)}, bf16[8,2048]{1,0:T(8,128)(2,1)S(1)}, u32[]{:S(2)}, u32[]{:S(2)}) collective-permute-start(bf16[8,2048]{1,0:T(8,128)(2,1)S(1)} %get-tuple-element.46), channel_id=1, source_target_pairs={{0,24},{1,25},{2,26},{3,27},{4,28},{5,29},{6,30},{7,31},{8,16},{9,... | collective-permute-start | bytes 98312 | tf_op jit(solution)/shard_map/ppermute | solution.py:17

commit v5 on v4

--- a/solution.py
+++ b/solution.py
@@ -33,7 +33,7 @@
     return list(range(count - 1, 0, -1))
 
 
-def attend_kernel(lengths_in, hidden_in, query_in, keys, values, gain_in, mixed, normed, lengths, hidden, query, gain, key_buf, value_buf, score_buf, small_sem, key_sem, value_sem):
+def attend_kernel(lengths_in, hidden_in, query_in, keys, values, gain_in, w_in_from, mixed, normed, w_in, lengths, hidden, query, gain, key_buf, value_buf, score_buf, small_sem, key_sem, value_sem):
     streams, width = hidden.shape
     span = key_buf.shape[1]
     head_size = width // HEADS
@@ -47,7 +47,8 @@
     pieces = [pl.ds(piece * group, group) for piece in range(PIECES)]
     key_copies = [pltpu.make_async_copy(keys.at[p], key_buf.at[p], key_sem.at[i]) for i, p in enumerate(pieces)]
     value_copies = [pltpu.make_async_copy(values.at[p], value_buf.at[p], value_sem.at[i]) for i, p in enumerate(pieces)]
-    for copy in small + key_copies + value_copies:
+    weight_copy = pltpu.make_async_copy(w_in_from, w_in, small_sem.at[4])
+    for copy in small + key_copies + value_copies + [weight_copy]:
         copy.start()
     owner = lax.broadcasted_iota(jnp.int32, (HEADS, width), 1) // head_size
     own = owner == lax.broadcasted_iota(jnp.int32, (HEADS, width), 0)
@@ -79,6 +80,7 @@
     centered = total - jnp.mean(total, axis=-1, keepdims=True)
     variance = jnp.mean(centered * centered, axis=-1, keepdims=True)
     normed[...] = (centered * lax.rsqrt(variance + 1e-05) * gain[...]).astype(jnp.bfloat16)
+    weight_copy.wait()
 
 
 def attend(
@@ -88,6 +90,7 @@
     source_values,
     src_lengths,
     norm_gain,
+    w_in,
 ):
     streams, width = hidden_state.shape
     span = source_keys.shape[1]
@@ -98,6 +101,7 @@
         source_keys,
         source_values,
         norm_gain.reshape(1, width),
+        w_in,
     )
     vmem = pl.BlockSpec(memory_space=pltpu.VMEM)
     hbm = pl.BlockSpec(memory_space=pltpu.HBM)
@@ -106,9 +110,10 @@
         out_shape=(
             pltpu.VMEM((streams, width), jnp.float32),
             pltpu.VMEM((streams, width), jnp.bfloat16),
+            pltpu.VMEM(w_in.shape, w_in.dtype),
         ),
-        in_specs=[hbm] * 6,
-        out_specs=(vmem, vmem),
+        in_specs=[hbm] * 7,
+        out_specs=(vmem,) * 3,
         scratch_shapes=[
             pltpu.SMEM((streams,), jnp.int32),
             pltpu.VMEM((streams, width), hidden_state.dtype),
@@ -117,7 +122,7 @@
             pltpu.VMEM((streams, span, width), source_keys.dtype),
             pltpu.VMEM((streams, span, width), source_values.dtype),
             pltpu.VMEM((streams * HEADS, span), jnp.float32),
-            pltpu.SemaphoreType.DMA((4,)),
+            pltpu.SemaphoreType.DMA((5,)),
             pltpu.SemaphoreType.DMA((PIECES,)),
             pltpu.SemaphoreType.DMA((PIECES,)),
         ],
@@ -141,33 +146,41 @@
     )(pltpu.with_memory_space_constraint(array, pltpu.HBM))
 
 
-def feed_forward(rows, w_in, w_out, kind):
+def feed_forward(rows, weights, cuts):
+    kinds = [jnp.float32] + [jnp.bfloat16] * (len(rows) - 1)
+    height, width = rows[0].shape
+    parts = [(block, start, end) for block in range(len(rows)) for start, end in cuts]
+
     def kernel(*refs):
         row_refs = refs[: len(rows)]
-        w_in_ref, w_out_ref = refs[len(rows) : len(rows) + 2]
+        weight_refs = refs[len(rows) : len(rows) + 2 * len(weights)]
+        out_refs = refs[len(rows) + 2 * len(weights) :]
         stacked = jnp.concatenate([ref[...] for ref in row_refs], axis=0)
-        units = jnp.dot(stacked, w_in_ref[...], preferred_element_type=jnp.float32)
-        act = jnp.maximum(units, 0.0).astype(jnp.bfloat16)
-        every = jnp.dot(act, w_out_ref[...], preferred_element_type=jnp.float32).astype(kind)
-        start = 0
-        for ref in refs[len(rows) + 2 :]:
-            ref[...] = every[start : start + ref.shape[0]]
-            start += ref.shape[0]
+        every = None
+        for w_in_ref, w_out_ref in zip(weight_refs[::2], weight_refs[1::2]):
+            units = jnp.dot(stacked, w_in_ref[...], preferred_element_type=jnp.float32)
+            act = jnp.maximum(units, 0.0).astype(jnp.bfloat16)
+            some = jnp.dot(act, w_out_ref[...], preferred_element_type=jnp.float32)
+            every = some if every is None else every + some
+        for ref, (block, start, end) in zip(out_refs, parts):
+            ref[...] = every[block * height + start : block * height + end].astype(kinds[block])
 
     vmem = pl.BlockSpec(memory_space=pltpu.VMEM)
-    count = sum(part.shape[0] for part in rows)
-    return pl.pallas_call(
+    flat = [array for pair in weights for array in pair]
+    size = sum(array.size for array in flat)
+    out = pl.pallas_call(
         kernel,
-        out_shape=[jax.ShapeDtypeStruct(part.shape, kind) for part in rows],
-        in_specs=[vmem] * (len(rows) + 2),
-        out_specs=[vmem] * len(rows),
+        out_shape=[
+            jax.ShapeDtypeStruct((end - start, width), kinds[block]) for block, start, end in parts
+        ],
+        in_specs=[vmem] * (len(rows) + len(flat)),
+        out_specs=[vmem] * len(parts),
         compiler_params=pltpu.CompilerParams(vmem_limit_bytes=VMEM_LIMIT),
         cost_estimate=pl.CostEstimate(
-            flops=2 * count * w_in.size + 2 * count * w_out.size,
-            transcendentals=0,
-            bytes_accessed=2 * (w_in.size + w_out.size),
+            flops=2 * len(rows) * height * size, transcendentals=0, bytes_accessed=2 * size
         ),
-    )(*rows, w_in, w_out)
+    )(*rows, *flat)
+    return [out[block * len(cuts) : (block + 1) * len(cuts)] for block in range(len(rows))]
 
 
 def step_on_device(
@@ -189,13 +202,14 @@
     direct = experts_count <= 4
     group = lax.shift_right_logical(lax.axis_index("expert"), SPLIT.bit_length() - 1)
     group, src_lengths = lax.optimization_barrier((group, src_lengths))
-    mixed, normed = attend(
+    mixed, normed, w_in = attend(
         hidden_state,
         cross_query,
         source_keys,
         source_values,
         src_lengths,
         norm_gain,
+        w_in,
     )
     order = jnp.arange(experts_count, dtype=jnp.int32)
     if direct:
@@ -226,24 +240,23 @@
     near = {0: jnp.concatenate(column, axis=0)}
     for step in range(1, chips):
         near[step] = swap(near[0], CORES * step, devices)
-    far = {step: swap(near[step], 1, devices) for step in range(chips)}
-    w_in = bring(w_in)
+    other_in = swap(w_in, 1, devices)
     w_out = bring(w_out)
-    near_every = feed_forward([near[step] for step in range(chips)], w_in, w_out, jnp.float32)
-    near_every, far = lax.optimization_barrier((near_every, far))
-    far_sent = feed_forward([far[step] for step in range(chips)], w_in, w_out, jnp.bfloat16)
-    pair = [None] * chips
-    for step in range(chips):
-        pair[step] = (near_every[step], swap(far_sent[step], 1, devices))
-    bounds = [("reduce_chip", slice(capacity, None)), ("reduce_own", slice(0, capacity))]
-    if not direct:
-        bounds = [("reduce_chip", slice(None))]
+    other_out = swap(w_out, 1, devices)
+    height = near[0].shape[0]
+    cuts = [("reduce_chip", 0, height)]
+    if direct:
+        cuts = [("reduce_chip", capacity, height), ("reduce_own", 0, capacity)]
+    parts = feed_forward(
+        [near[step] for step in range(chips)],
+        [(w_in, w_out), (other_in, other_out)],
+        [(start, end) for _, start, end in cuts],
+    )
     sums = {}
-    for name, place in bounds:
-        joined = [mine[place] + other[place].astype(jnp.float32) for mine, other in pair]
-        sums[name] = joined[0]
+    for place, (name, _, _) in enumerate(cuts):
+        sums[name] = parts[0][place]
         for step in range(1, chips):
-            given = swap(joined[step].astype(jnp.bfloat16), CORES * step, devices)
+            given = swap(parts[step][place], CORES * step, devices)
             sums[name] = sums[name] + given.astype(jnp.float32)
     total = sums["reduce_chip"].reshape(-1, capacity, width)
     result = mixed

time: 47.8 us -> 42.5 us (0.89)
  waiting for transfers between devices: 15.9 us -> 13.6 us
  Pallas kernels: 8.42 us -> 6.54 us
  starting transfers between devices: 22.1 us -> 21.2 us
    ppermute x23 -> x17, waiting for transfers between devices: 15.9 us -> 13.6 us  [swap(): return lax.ppermute(value, 'expert', pairs)]
    pallas_call x2 -> x1, Pallas kernels: 3.2 us -> 1.6 us  [bring(): pl.pallas_call(kernel, out_shape=pltpu.VMEM(array.shape, array.dtype), in...]
    ppermute x23 -> x17, starting transfers between devices: 22.1 us -> 21.2 us  [swap(): return lax.ppermute(value, 'expert', pairs)]
    pallas_call x2 -> x1, Pallas kernels: 1.67 us -> 1.38 us  [feed_forward(): pl.pallas_call(kernel, out_shape=[jax.ShapeDtypeStruct((end - start, widt...]
  transfers between devices with their start and end apart: 23 -> 17, of which waited for: 10 -> 8; matrix products, arithmetic and copies ran while one was open for 1% -> 0% of each run, Pallas kernels for 8% -> 4%
where the time goes in v5:
time: 42.5 us; the launch traced here: 42.3 us
  starting transfers between devices  21.2 us (50%)
  waiting for transfers between devices  13.6 us (32%)
  Pallas kernels  6.54 us (15%)
  other arithmetic  0.84 us (2%)
    ppermute x17, starting transfers between devices, swap(): return lax.ppermute(value, 'expert', pairs)  21.2 us
    ppermute x17, waiting for transfers between devices, swap(): return lax.ppermute(value, 'expert', pairs)  13.6 us
    pallas_call x1, Pallas kernels, attend(): pl.pallas_call(attend_kernel, out_shape=(pltpu.VMEM((streams, width), jnp...  3.56 us
    pallas_call x1, Pallas kernels, bring(): pl.pallas_call(kernel, out_shape=pltpu.VMEM(array.shape, array.dtype), in...  1.6 us
    pallas_call x1, Pallas kernels, feed_forward(): pl.pallas_call(kernel, out_shape=[jax.ShapeDtypeStruct((end - start, widt...  1.38 us
  transfers between devices with their start and end apart: 17, of which 8 were waited for; matrix products, arithmetic and copies ran while one was open for 0% of the time, Pallas kernels for 4%

profile of v5, /device:TPU:0, one launch (start us, length us, event | category | flops | bytes accessed | tf_op | source)
XLA Modules:
  0.0 42.3 jit_solution(5741341447048237470)
XLA Ops:
  0.0 3.6 %shard_map.100 = (f32[8,2048]{1,0:T(8,128)S(1)}, bf16[8,2048]{1,0:T(8,128)(2,1)S(1)}, bf16[2048,512]{1,0:T(8,128)(2,1)S(1)}) custom-call(s32[8]{0:T(128)} %lengths_in, bf16[8,2048]{1,0:T(8,128)(2,1)} %hidden_in.1, bf16[8,2048]{1,0:T(8,128)(2,1)} %query_in.1, bf16[8,64,2048]{2,1,0:T(8,128)(2,1)} %keys.1, bf16[8,64,2048]{2,1,0:T(8,128)(2,1)} %values.1, ...), custom_call_target="tpu_custom_call" | custom-call | tf_op jit(solution)/shard_map/pallas_call | solution.py:108
  3.6 0.6 %collective-permute-start.6 = (bf16[2048,512]{1,0:T(8,128)(2,1)S(1)}, bf16[2048,512]{1,0:T(8,128)(2,1)S(1)}, u32[]{:S(2)}, u32[]{:S(2)}) collective-permute-start(bf16[2048,512]{1,0:T(8,128)(2,1)S(1)} %get-tuple-element.22.refs_4_), channel_id=1, source_target_pairs={{0,1},{1,0},{2,3},{3,2},{4,5},{5,4},{6,7},{7,6},{8,9},{9,8},{10,11... | collective-permute-start | bytes 6291464 | tf_op jit(solution)/shard_map/ppermute | solution.py:17
  4.1 1.6 %shard_map.101.refs_5_ = bf16[512,2048]{1,0:T(8,128)(2,1)S(1)} custom-call(bf16[512,2048]{1,0:T(8,128)(2,1)} %source.1), custom_call_target="tpu_custom_call" | custom-call | tf_op jit(solution)/shard_map/pallas_call | solution.py:139
  5.7 0.1 collective-permute-start.7
  5.8 3.1 %collective-permute-start = (bf16[8,2048]{1,0:T(8,128)(2,1)S(1)}, bf16[8,2048]{1,0:T(8,128)(2,1)S(1)}, u32[]{:S(2)}, u32[]{:S(2)}) collective-permute-start(bf16[8,2048]{1,0:T(8,128)(2,1)S(1)} %get-tuple-element.21), channel_id=1, source_target_pairs={{0,8},{1,9},{2,10},{3,11},{4,12},{5,13},{6,14},{7,15},{8,0},{9,1},... | collective-permute-start | bytes 98312 | tf_op jit(solution)/shard_map/ppermute | solution.py:17
  8.9 2.6 %collective-permute-start.1 = (bf16[8,2048]{1,0:T(8,128)(2,1)S(1)}, bf16[8,2048]{1,0:T(8,128)(2,1)S(1)}, u32[]{:S(2)}, u32[]{:S(2)}) collective-permute-start(bf16[8,2048]{1,0:T(8,128)(2,1)S(1)} %get-tuple-element.21), channel_id=1, source_target_pairs={{0,16},{1,17},{2,18},{3,19},{4,20},{5,21},{6,22},{7,23},{8,24},{9,... | collective-permute-start | bytes 98312 | tf_op jit(solution)/shard_map/ppermute | solution.py:17
  11.5 2.8 %collective-permute-done.1 = bf16[8,2048]{1,0:T(8,128)(2,1)S(1)} collective-permute-done((bf16[8,2048]{1,0:T(8,128)(2,1)S(1)}, bf16[8,2048]{1,0:T(8,128)(2,1)S(1)}, u32[]{:S(2)}, u32[]{:S(2)}) %collective-permute-start.1) | collective-permute-done | bytes 32800 | tf_op jit(solution)/shard_map/ppermute | solution.py:17
  14.3 2.9 %collective-permute-done.2 = bf16[8,2048]{1,0:T(8,128)(2,1)S(1)} collective-permute-done((bf16[8,2048]{1,0:T(8,128)(2,1)S(1)}, bf16[8,2048]{1,0:T(8,128)(2,1)S(1)}, u32[]{:S(2)}, u32[]{:S(2)}) %collective-permute-start.2) | collective-permute-done | bytes 32800 | tf_op jit(solution)/shard_map/ppermute | solution.py:17
  17.2 1.5 %collective-permute-start.3 = (bf16[32,2048]{1,0:T(8,128)(2,1)S(1)}, bf16[32,2048]{1,0:T(8,128)(2,1)S(1)}, u32[]{:S(2)}, u32[]{:S(2)}) collective-permute-start(bf16[32,2048]{1,0:T(8,128)(2,1)S(1)} %constant_dynamic-update-slice_fusion.refs_0_), channel_id=1, source_target_pairs={{0,2},{1,3},{2,0},{3,1},{4,6},{5,7},{6,4},{7,5},{8,10},{9,11},{10,... | collective-permute-start | bytes 393224 | tf_op jit(solution)/shard_map/ppermute | solution.py:17
  18.7 1.5 %collective-permute-start.4 = (bf16[32,2048]{1,0:T(8,128)(2,1)S(1)}, bf16[32,2048]{1,0:T(8,128)(2,1)S(1)}, u32[]{:S(2)}, u32[]{:S(2)}) collective-permute-start(bf16[32,2048]{1,0:T(8,128)(2,1)S(1)} %constant_dynamic-update-slice_fusion.refs_0_), channel_id=1, source_target_pairs={{0,4},{1,5},{2,6},{3,7},{4,0},{5,1},{6,2},{7,3},{8,12},{9,13},{10,... | collective-permute-start | bytes 393224 | tf_op jit(solution)/shard_map/ppermute | solution.py:17
  20.2 0.5 %collective-permute-start.5 = (bf16[32,2048]{1,0:T(8,128)(2,1)S(1)}, bf16[32,2048]{1,0:T(8,128)(2,1)S(1)}, u32[]{:S(2)}, u32[]{:S(2)}) collective-permute-start(bf16[32,2048]{1,0:T(8,128)(2,1)S(1)} %constant_dynamic-update-slice_fusion.refs_0_), channel_id=1, source_target_pairs={{0,6},{1,7},{2,4},{3,5},{4,2},{5,3},{6,0},{7,1},{8,14},{9,15},{10,... | collective-permute-start | bytes 393224 | tf_op jit(solution)/shard_map/ppermute | solution.py:17
  20.7 2.7 %collective-permute-done.3.refs_1_ = bf16[32,2048]{1,0:T(8,128)(2,1)S(1)} collective-permute-done((bf16[32,2048]{1,0:T(8,128)(2,1)S(1)}, bf16[32,2048]{1,0:T(8,128)(2,1)S(1)}, u32[]{:S(2)}, u32[]{:S(2)}) %collective-permute-start.3) | collective-permute-done | bytes 131104 | tf_op jit(solution)/shard_map/ppermute | solution.py:17
  23.3 1.2 %collective-permute-done.4.refs_2_ = bf16[32,2048]{1,0:T(8,128)(2,1)S(1)} collective-permute-done((bf16[32,2048]{1,0:T(8,128)(2,1)S(1)}, bf16[32,2048]{1,0:T(8,128)(2,1)S(1)}, u32[]{:S(2)}, u32[]{:S(2)}) %collective-permute-start.4) | collective-permute-done | bytes 131104 | tf_op jit(solution)/shard_map/ppermute | solution.py:17
  24.6 1.5 %collective-permute-done.5.refs_3_ = bf16[32,2048]{1,0:T(8,128)(2,1)S(1)} collective-permute-done((bf16[32,2048]{1,0:T(8,128)(2,1)S(1)}, bf16[32,2048]{1,0:T(8,128)(2,1)S(1)}, u32[]{:S(2)}, u32[]{:S(2)}) %collective-permute-start.5) | collective-permute-done | bytes 131104 | tf_op jit(solution)/shard_map/ppermute | solution.py:17
  26.1 0.0 collective-permute-done.7.refs_7_
  26.1 1.4 %shard_map.102 = (f32[24,2048]{1,0:T(8,128)S(1)}, f32[8,2048]{1,0:T(8,128)S(1)}, bf16[24,2048]{1,0:T(8,128)(2,1)S(1)}, bf16[8,2048]{1,0:T(8,128)(2,1)S(1)}, bf16...) custom-call(bf16[32,2048]{1,0:T(8,128)(2,1)S(1)} %constant_dynamic-u, ...), custom_call_target="tpu_custom_call" | custom-call | flops 1073741824 | bytes 8388608 | tf_op jit(solution)/shard_map/pallas_call | solution.py:171
  27.4 0.6 %collective-permute-start.11 = (bf16[24,2048]{1,0:T(8,128)(2,1)S(1)}, bf16[24,2048]{1,0:T(8,128)(2,1)S(1)}, u32[]{:S(2)}, u32[]{:S(2)}) collective-permute-start(bf16[24,2048]{1,0:T(8,128)(2,1)S(1)} %get-tuple-element.28), channel_id=1, source_target_pairs={{0,2},{1,3},{2,0},{3,1},{4,6},{5,7},{6,4},{7,5},{8,10},{9,11},{10,... | collective-permute-start | bytes 294920 | tf_op jit(solution)/shard_map/ppermute | solution.py:17
  28.0 0.5 %collective-permute-start.12 = (bf16[24,2048]{1,0:T(8,128)(2,1)S(1)}, bf16[24,2048]{1,0:T(8,128)(2,1)S(1)}, u32[]{:S(2)}, u32[]{:S(2)}) collective-permute-start(bf16[24,2048]{1,0:T(8,128)(2,1)S(1)} %get-tuple-element.29), channel_id=1, source_target_pairs={{0,4},{1,5},{2,6},{3,7},{4,0},{5,1},{6,2},{7,3},{8,12},{9,13},{10,... | collective-permute-start | bytes 294920 | tf_op jit(solution)/shard_map/ppermute | solution.py:17
  28.6 2.4 %collective-permute-start.13 = (bf16[24,2048]{1,0:T(8,128)(2,1)S(1)}, bf16[24,2048]{1,0:T(8,128)(2,1)S(1)}, u32[]{:S(2)}, u32[]{:S(2)}) collective-permute-start(bf16[24,2048]{1,0:T(8,128)(2,1)S(1)} %get-tuple-element.30), channel_id=1, source_target_pairs={{0,6},{1,7},{2,4},{3,5},{4,2},{5,3},{6,0},{7,1},{8,14},{9,15},{10,... | collective-permute-start | bytes 294920 | tf_op jit(solution)/shard_map/ppermute | solution.py:17
  31.0 0.1 select_reduce_fusion
  31.1 0.5 %collective-permute-start.10 = (bf16[8,2048]{1,0:T(8,128)(2,1)S(1)}, bf16[8,2048]{1,0:T(8,128)(2,1)S(1)}, u32[]{:S(2)}, u32[]{:S(2)}) collective-permute-start(bf16[8,2048]{1,0:T(8,128)(2,1)S(1)} %get-tuple-element.26), channel_id=1, source_target_pairs={{0,6},{1,7},{2,4},{3,5},{4,2},{5,3},{6,0},{7,1},{8,14},{9,15},{10,... | collective-permute-start | bytes 98312 | tf_op jit(solution)/shard_map/ppermute | solution.py:17
  31.6 1.9 %collective-permute-start.8 = (bf16[8,2048]{1,0:T(8,128)(2,1)S(1)}, bf16[8,2048]{1,0:T(8,128)(2,1)S(1)}, u32[]{:S(2)}, u32[]{:S(2)}) collective-permute-start(bf16[8,2048]{1,0:T(8,128)(2,1)S(1)} %get-tuple-element.24), channel_id=1, source_target_pairs={{0,2},{1,3},{2,0},{3,1},{4,6},{5,7},{6,4},{7,5},{8,10},{9,11},{10,... | collective-permute-start | bytes 98312 | tf_op jit(solution)/shard_map/ppermute | solution.py:17
  33.5 1.1 %collective-permute-start.9 = (bf16[8,2048]{1,0:T(8,128)(2,1)S(1)}, bf16[8,2048]{1,0:T(8,128)(2,1)S(1)}, u32[]{:S(2)}, u32[]{:S(2)}) collective-permute-start(bf16[8,2048]{1,0:T(8,128)(2,1)S(1)} %get-tuple-element.25), channel_id=1, source_target_pairs={{0,4},{1,5},{2,6},{3,7},{4,0},{5,1},{6,2},{7,3},{8,12},{9,13},{10,... | collective-permute-start | bytes 98312 | tf_op jit(solution)/shard_map/ppermute | solution.py:17
  34.6 0.0 collective-permute-done.12
  34.6 0.0 collective-permute-done.13
  34.7 0.1 collective-permute-start.14
  34.7 1.1 %collective-permute-start.15 = (bf16[8,2048]{1,0:T(8,128)(2,1)S(1)}, bf16[8,2048]{1,0:T(8,128)(2,1)S(1)}, u32[]{:S(2)}, u32[]{:S(2)}) collective-permute-start(bf16[8,2048]{1,0:T(8,128)(2,1)S(1)} %get-tuple-element.33), channel_id=1, source_target_pairs={{0,16},{1,17},{2,18},{3,19},{4,20},{5,21},{6,22},{7,23},{8,24},{9,... | collective-permute-start | bytes 98312 | tf_op jit(solution)/shard_map/ppermute | solution.py:17
  35.8 0.1 collective-permute-done.10
  35.9 3.2 %collective-permute-start.16 = (bf16[8,2048]{1,0:T(8,128)(2,1)S(1)}, bf16[8,2048]{1,0:T(8,128)(2,1)S(1)}, u32[]{:S(2)}, u32[]{:S(2)}) collective-permute-start(bf16[8,2048]{1,0:T(8,128)(2,1)S(1)} %get-tuple-element.32), channel_id=1, source_target_pairs={{0,24},{1,25},{2,26},{3,27},{4,28},{5,29},{6,30},{7,31},{8,16},{9,... | collective-permute-start | bytes 98312 | tf_op jit(solution)/shard_map/ppermute | solution.py:17
  39.1 0.5 %collective-permute-done.15 = bf16[8,2048]{1,0:T(8,128)(2,1)S(1)} collective-permute-done((bf16[8,2048]{1,0:T(8,128)(2,1)S(1)}, bf16[8,2048]{1,0:T(8,128)(2,1)S(1)}, u32[]{:S(2)}, u32[]{:S(2)}) %collective-permute-start.15) | collective-permute-done | bytes 32800 | tf_op jit(solution)/shard_map/ppermute | solution.py:17
  39.6 2.0 %collective-permute-done.16 = bf16[8,2048]{1,0:T(8,128)(2,1)S(1)} collective-permute-done((bf16[8,2048]{1,0:T(8,128)(2,1)S(1)}, bf16[8,2048]{1,0:T(8,128)(2,1)S(1)}, u32[]{:S(2)}, u32[]{:S(2)}) %collective-permute-start.16) | collective-permute-done | bytes 32800 | tf_op jit(solution)/shard_map/ppermute | solution.py:17
  41.6 0.7 %add_convert_fusion.1 = bf16[8,2048]{1,0:T(8,128)(2,1)} fusion(bf16[8,2048]{1,0:T(8,128)(2,1)S(1)} %collective-permute-done.16, bf16[8,2048]{1,0:T(8,128)(2,1)S(1)} %collective-permute-done.15, bf16[8,2048]{1,0:T(8,128)(2,1)S(1)} %collective-permute-done.14, f32[8,2048]{1,0:T(8,128)S(1)} %get-tuple-element.19, ...), kind=kLoop, calls=%fused_computation.1 | loop fusion | flops 294912 | bytes 360576 | tf_op jit(solution)/shard_map/convert_element_type | solution.py:281
  (19 shorter events, 0.1 us)
Async XLA Ops:
  3.6 22.5 %collective-permute-start.6 = (bf16[2048,512]{1,0:T(8,128)(2,1)S(1)}, bf16[2048,512]{1,0:T(8,128)(2,1)S(1)}, u32[]{:S(2)}, u32[]{:S(2)}) collective-permute-start(bf16[2048,512]{1,0:T(8,128)(2,1)S(1)} %get-tuple-element.22.refs_4_), channel_id=1, source_target_pairs={{0,1},{1,0},{2,3},{3,2},{4,5},{5,4},{6,7},{7,6},{8,9},{9,8},{10,11... | collective-permute-start | bytes 6291464 | tf_op jit(solution)/shard_map/ppermute | solution.py:17
  5.7 20.3 %collective-permute-start.7 = (bf16[512,2048]{1,0:T(8,128)(2,1)S(1)}, bf16[512,2048]{1,0:T(8,128)(2,1)S(1)}, u32[]{:S(2)}, u32[]{:S(2)}) collective-permute-start(bf16[512,2048]{1,0:T(8,128)(2,1)S(1)} %shard_map.101.refs_5_), channel_id=1, source_target_pairs={{0,1},{1,0},{2,3},{3,2},{4,5},{5,4},{6,7},{7,6},{8,9},{9,8},{10,11... | collective-permute-start | bytes 6291464 | tf_op jit(solution)/shard_map/ppermute | solution.py:17
  5.8 5.7 %collective-permute-start = (bf16[8,2048]{1,0:T(8,128)(2,1)S(1)}, bf16[8,2048]{1,0:T(8,128)(2,1)S(1)}, u32[]{:S(2)}, u32[]{:S(2)}) collective-permute-start(bf16[8,2048]{1,0:T(8,128)(2,1)S(1)} %get-tuple-element.21), channel_id=1, source_target_pairs={{0,8},{1,9},{2,10},{3,11},{4,12},{5,13},{6,14},{7,15},{8,0},{9,1},... | collective-permute-start | bytes 98312 | tf_op jit(solution)/shard_map/ppermute | solution.py:17
  8.9 5.4 %collective-permute-start.1 = (bf16[8,2048]{1,0:T(8,128)(2,1)S(1)}, bf16[8,2048]{1,0:T(8,128)(2,1)S(1)}, u32[]{:S(2)}, u32[]{:S(2)}) collective-permute-start(bf16[8,2048]{1,0:T(8,128)(2,1)S(1)} %get-tuple-element.21), channel_id=1, source_target_pairs={{0,16},{1,17},{2,18},{3,19},{4,20},{5,21},{6,22},{7,23},{8,24},{9,... | collective-permute-start | bytes 98312 | tf_op jit(solution)/shard_map/ppermute | solution.py:17
  11.5 5.7 %collective-permute-start.2 = (bf16[8,2048]{1,0:T(8,128)(2,1)S(1)}, bf16[8,2048]{1,0:T(8,128)(2,1)S(1)}, u32[]{:S(2)}, u32[]{:S(2)}) collective-permute-start(bf16[8,2048]{1,0:T(8,128)(2,1)S(1)} %get-tuple-element.21), channel_id=1, source_target_pairs={{0,24},{1,25},{2,26},{3,27},{4,28},{5,29},{6,30},{7,31},{8,16},{9,... | collective-permute-start | bytes 98312 | tf_op jit(solution)/shard_map/ppermute | solution.py:17
  17.2 6.2 %collective-permute-start.3 = (bf16[32,2048]{1,0:T(8,128)(2,1)S(1)}, bf16[32,2048]{1,0:T(8,128)(2,1)S(1)}, u32[]{:S(2)}, u32[]{:S(2)}) collective-permute-start(bf16[32,2048]{1,0:T(8,128)(2,1)S(1)} %constant_dynamic-update-slice_fusion.refs_0_), channel_id=1, source_target_pairs={{0,2},{1,3},{2,0},{3,1},{4,6},{5,7},{6,4},{7,5},{8,10},{9,11},{10,... | collective-permute-start | bytes 393224 | tf_op jit(solution)/shard_map/ppermute | solution.py:17
  18.7 5.9 %collective-permute-start.4 = (bf16[32,2048]{1,0:T(8,128)(2,1)S(1)}, bf16[32,2048]{1,0:T(8,128)(2,1)S(1)}, u32[]{:S(2)}, u32[]{:S(2)}) collective-permute-start(bf16[32,2048]{1,0:T(8,128)(2,1)S(1)} %constant_dynamic-update-slice_fusion.refs_0_), channel_id=1, source_target_pairs={{0,4},{1,5},{2,6},{3,7},{4,0},{5,1},{6,2},{7,3},{8,12},{9,13},{10,... | collective-permute-start | bytes 393224 | tf_op jit(solution)/shard_map/ppermute | solution.py:17
  20.2 5.9 %collective-permute-start.5 = (bf16[32,2048]{1,0:T(8,128)(2,1)S(1)}, bf16[32,2048]{1,0:T(8,128)(2,1)S(1)}, u32[]{:S(2)}, u32[]{:S(2)}) collective-permute-start(bf16[32,2048]{1,0:T(8,128)(2,1)S(1)} %constant_dynamic-update-slice_fusion.refs_0_), channel_id=1, source_target_pairs={{0,6},{1,7},{2,4},{3,5},{4,2},{5,3},{6,0},{7,1},{8,14},{9,15},{10,... | collective-permute-start | bytes 393224 | tf_op jit(solution)/shard_map/ppermute | solution.py:17
  20.7 10.3 %copy-start = (f32[8,2]{0,1:T(2,128)S(1)}, f32[8,2]{0,1:T(2,128)}, u32[]{:S(2)}) copy-start(f32[8,2]{0,1:T(2,128)} %param.19) | copy-start | bytes 196
  20.7 10.3 %copy-start.1 = (s32[8,2]{0,1:T(2,128)S(1)}, s32[8,2]{0,1:T(2,128)}, u32[]{:S(2)}) copy-start(s32[8,2]{0,1:T(2,128)} %param.18) | copy-start | bytes 196
  27.4 6.0 %collective-permute-start.11 = (bf16[24,2048]{1,0:T(8,128)(2,1)S(1)}, bf16[24,2048]{1,0:T(8,128)(2,1)S(1)}, u32[]{:S(2)}, u32[]{:S(2)}) collective-permute-start(bf16[24,2048]{1,0:T(8,128)(2,1)S(1)} %get-tuple-element.28), channel_id=1, source_target_pairs={{0,2},{1,3},{2,0},{3,1},{4,6},{5,7},{6,4},{7,5},{8,10},{9,11},{10,... | collective-permute-start | bytes 294920 | tf_op jit(solution)/shard_map/ppermute | solution.py:17
  28.0 6.5 %collective-permute-start.12 = (bf16[24,2048]{1,0:T(8,128)(2,1)S(1)}, bf16[24,2048]{1,0:T(8,128)(2,1)S(1)}, u32[]{:S(2)}, u32[]{:S(2)}) collective-permute-start(bf16[24,2048]{1,0:T(8,128)(2,1)S(1)} %get-tuple-element.29), channel_id=1, source_target_pairs={{0,4},{1,5},{2,6},{3,7},{4,0},{5,1},{6,2},{7,3},{8,12},{9,13},{10,... | collective-permute-start | bytes 294920 | tf_op jit(solution)/shard_map/ppermute | solution.py:17
  28.6 6.0 %collective-permute-start.13 = (bf16[24,2048]{1,0:T(8,128)(2,1)S(1)}, bf16[24,2048]{1,0:T(8,128)(2,1)S(1)}, u32[]{:S(2)}, u32[]{:S(2)}) collective-permute-start(bf16[24,2048]{1,0:T(8,128)(2,1)S(1)} %get-tuple-element.30), channel_id=1, source_target_pairs={{0,6},{1,7},{2,4},{3,5},{4,2},{5,3},{6,0},{7,1},{8,14},{9,15},{10,... | collective-permute-start | bytes 294920 | tf_op jit(solution)/shard_map/ppermute | solution.py:17
  31.1 4.8 %collective-permute-start.10 = (bf16[8,2048]{1,0:T(8,128)(2,1)S(1)}, bf16[8,2048]{1,0:T(8,128)(2,1)S(1)}, u32[]{:S(2)}, u32[]{:S(2)}) collective-permute-start(bf16[8,2048]{1,0:T(8,128)(2,1)S(1)} %get-tuple-element.26), channel_id=1, source_target_pairs={{0,6},{1,7},{2,4},{3,5},{4,2},{5,3},{6,0},{7,1},{8,14},{9,15},{10,... | collective-permute-start | bytes 98312 | tf_op jit(solution)/shard_map/ppermute | solution.py:17
  31.6 7.6 %collective-permute-start.8 = (bf16[8,2048]{1,0:T(8,128)(2,1)S(1)}, bf16[8,2048]{1,0:T(8,128)(2,1)S(1)}, u32[]{:S(2)}, u32[]{:S(2)}) collective-permute-start(bf16[8,2048]{1,0:T(8,128)(2,1)S(1)} %get-tuple-element.24), channel_id=1, source_target_pairs={{0,2},{1,3},{2,0},{3,1},{4,6},{5,7},{6,4},{7,5},{8,10},{9,11},{10,... | collective-permute-start | bytes 98312 | tf_op jit(solution)/shard_map/ppermute | solution.py:17
  33.5 5.6 %collective-permute-start.9 = (bf16[8,2048]{1,0:T(8,128)(2,1)S(1)}, bf16[8,2048]{1,0:T(8,128)(2,1)S(1)}, u32[]{:S(2)}, u32[]{:S(2)}) collective-permute-start(bf16[8,2048]{1,0:T(8,128)(2,1)S(1)} %get-tuple-element.25), channel_id=1, source_target_pairs={{0,4},{1,5},{2,6},{3,7},{4,0},{5,1},{6,2},{7,3},{8,12},{9,13},{10,... | collective-permute-start | bytes 98312 | tf_op jit(solution)/shard_map/ppermute | solution.py:17
  34.7 4.5 %collective-permute-start.14 = (bf16[8,2048]{1,0:T(8,128)(2,1)S(1)}, bf16[8,2048]{1,0:T(8,128)(2,1)S(1)}, u32[]{:S(2)}, u32[]{:S(2)}) collective-permute-start(bf16[8,2048]{1,0:T(8,128)(2,1)S(1)} %get-tuple-element.31), channel_id=1, source_target_pairs={{0,8},{1,9},{2,10},{3,11},{4,12},{5,13},{6,14},{7,15},{8,0},{9,1},... | collective-permute-start | bytes 98312 | tf_op jit(solution)/shard_map/ppermute | solution.py:17
  34.7 4.9 %collective-permute-start.15 = (bf16[8,2048]{1,0:T(8,128)(2,1)S(1)}, bf16[8,2048]{1,0:T(8,128)(2,1)S(1)}, u32[]{:S(2)}, u32[]{:S(2)}) collective-permute-start(bf16[8,2048]{1,0:T(8,128)(2,1)S(1)} %get-tuple-element.33), channel_id=1, source_target_pairs={{0,16},{1,17},{2,18},{3,19},{4,20},{5,21},{6,22},{7,23},{8,24},{9,... | collective-permute-start | bytes 98312 | tf_op jit(solution)/shard_map/ppermute | solution.py:17
  35.9 5.7 %collective-permute-start.16 = (bf16[8,2048]{1,0:T(8,128)(2,1)S(1)}, bf16[8,2048]{1,0:T(8,128)(2,1)S(1)}, u32[]{:S(2)}, u32[]{:S(2)}) collective-permute-start(bf16[8,2048]{1,0:T(8,128)(2,1)S(1)} %get-tuple-element.32), channel_id=1, source_target_pairs={{0,24},{1,25},{2,26},{3,27},{4,28},{5,29},{6,30},{7,31},{8,16},{9,... | collective-permute-start | bytes 98312 | tf_op jit(solution)/shard_map/ppermute | solution.py:17

commit v6 on v5

--- a/solution.py
+++ b/solution.py
@@ -146,10 +146,9 @@
     )(pltpu.with_memory_space_constraint(array, pltpu.HBM))
 
 
-def feed_forward(rows, weights, cuts):
+def feed_forward(rows, weights):
     kinds = [jnp.float32] + [jnp.bfloat16] * (len(rows) - 1)
     height, width = rows[0].shape
-    parts = [(block, start, end) for block in range(len(rows)) for start, end in cuts]
 
     def kernel(*refs):
         row_refs = refs[: len(rows)]
@@ -162,25 +161,22 @@
             act = jnp.maximum(units, 0.0).astype(jnp.bfloat16)
             some = jnp.dot(act, w_out_ref[...], preferred_element_type=jnp.float32)
             every = some if every is None else every + some
-        for ref, (block, start, end) in zip(out_refs, parts):
-            ref[...] = every[block * height + start : block * height + end].astype(kinds[block])
+        for block, ref in enumerate(out_refs):
+            ref[...] = every[block * height : (block + 1) * height].astype(kinds[block])
 
     vmem = pl.BlockSpec(memory_space=pltpu.VMEM)
     flat = [array for pair in weights for array in pair]
     size = sum(array.size for array in flat)
-    out = pl.pallas_call(
+    return pl.pallas_call(
         kernel,
-        out_shape=[
-            jax.ShapeDtypeStruct((end - start, width), kinds[block]) for block, start, end in parts
-        ],
+        out_shape=[jax.ShapeDtypeStruct((height, width), kind) for kind in kinds],
         in_specs=[vmem] * (len(rows) + len(flat)),
-        out_specs=[vmem] * len(parts),
+        out_specs=[vmem] * len(rows),
         compiler_params=pltpu.CompilerParams(vmem_limit_bytes=VMEM_LIMIT),
         cost_estimate=pl.CostEstimate(
             flops=2 * len(rows) * height * size, transcendentals=0, bytes_accessed=2 * size
         ),
     )(*rows, *flat)
-    return [out[block * len(cuts) : (block + 1) * len(cuts)] for block in range(len(rows))]
 
 
 def step_on_device(
@@ -243,28 +239,19 @@
     other_in = swap(w_in, 1, devices)
     w_out = bring(w_out)
     other_out = swap(w_out, 1, devices)
-    height = near[0].shape[0]
-    cuts = [("reduce_chip", 0, height)]
-    if direct:
-        cuts = [("reduce_chip", capacity, height), ("reduce_own", 0, capacity)]
     parts = feed_forward(
-        [near[step] for step in range(chips)],
-        [(w_in, w_out), (other_in, other_out)],
-        [(start, end) for _, start, end in cuts],
-    )
-    sums = {}
-    for place, (name, _, _) in enumerate(cuts):
-        sums[name] = parts[0][place]
-        for step in range(1, chips):
-            given = swap(parts[step][place], CORES * step, devices)
-            sums[name] = sums[name] + given.astype(jnp.float32)
-    total = sums["reduce_chip"].reshape(-1, capacity, width)
+        [near[step] for step in range(chips)], [(w_in, w_out), (other_in, other_out)]
+    )
+    total = parts[0]
+    for step in range(1, chips):
+        given = swap(parts[step], CORES * step, devices)
+        total = total + given.astype(jnp.float32)
+    total = total.reshape(experts_count, capacity, width)
     result = mixed
     sent = total.astype(jnp.bfloat16)
     if direct:
-        back = {k: swap(sent[k - 1], k * SPLIT, devices) for k in distances}
-        parts = [sums["reduce_own"]]
-        parts += [back[k].astype(jnp.float32) for k in range(1, experts_count)]
+        back = {k: swap(sent[k], k * SPLIT, devices) for k in distances}
+        parts = [total[0]] + [back[k].astype(jnp.float32) for k in range(1, experts_count)]
     else:
         back = outer_exchange([sent[k] for k in range(experts_count)], devices)
         parts = [part.astype(jnp.float32) for part in back]

time: 42.5 us -> 41.8 us (0.984)
  starting transfers between devices: 21.2 us -> 17.8 us
  waiting for transfers between devices: 13.6 us -> 16.4 us
    ppermute x17 -> x14, starting transfers between devices: 21.2 us -> 17.8 us  [swap(): return lax.ppermute(value, 'expert', pairs)]
    ppermute x17 -> x14, waiting for transfers between devices: 13.6 us -> 16.4 us  [swap(): return lax.ppermute(value, 'expert', pairs)]
  transfers between devices with their start and end apart: 17 -> 14, of which waited for: 8 -> 10; matrix products, arithmetic and copies ran while one was open for 0% -> 0% of each run, Pallas kernels for 4% -> 4%
where the time goes in v6:
time: 41.8 us; the launch traced here: 41.7 us
  starting transfers between devices  17.8 us (43%)
  waiting for transfers between devices  16.4 us (39%)
  Pallas kernels  6.54 us (16%)
  other arithmetic  0.85 us (2%)
    ppermute x14, starting transfers between devices, swap(): return lax.ppermute(value, 'expert', pairs)  17.8 us
    ppermute x14, waiting for transfers between devices, swap(): return lax.ppermute(value, 'expert', pairs)  16.4 us
    pallas_call x1, Pallas kernels, attend(): pl.pallas_call(attend_kernel, out_shape=(pltpu.VMEM((streams, width), jnp...  3.56 us
    pallas_call x1, Pallas kernels, bring(): pl.pallas_call(kernel, out_shape=pltpu.VMEM(array.shape, array.dtype), in...  1.6 us
    pallas_call x1, Pallas kernels, feed_forward(): pl.pallas_call(kernel, out_shape=[jax.ShapeDtypeStruct((height, width), k...  1.38 us
  transfers between devices with their start and end apart: 14, of which 10 were waited for; matrix products, arithmetic and copies ran while one was open for 0% of the time, Pallas kernels for 4%

profile of v6, /device:TPU:0, one launch (start us, length us, event | category | flops | bytes accessed | tf_op | source)
XLA Modules:
  0.0 41.7 jit_solution(5243338268429866930)
XLA Ops:
  0.0 3.6 %shard_map.100 = (f32[8,2048]{1,0:T(8,128)S(1)}, bf16[8,2048]{1,0:T(8,128)(2,1)S(1)}, bf16[2048,512]{1,0:T(8,128)(2,1)S(1)}) custom-call(s32[8]{0:T(128)} %lengths_in, bf16[8,2048]{1,0:T(8,128)(2,1)} %hidden_in.1, bf16[8,2048]{1,0:T(8,128)(2,1)} %query_in.1, bf16[8,64,2048]{2,1,0:T(8,128)(2,1)} %keys.1, bf16[8,64,2048]{2,1,0:T(8,128)(2,1)} %values.1, ...), custom_call_target="tpu_custom_call" | custom-call | tf_op jit(solution)/shard_map/pallas_call | solution.py:108
  3.6 0.6 %collective-permute-start.6 = (bf16[2048,512]{1,0:T(8,128)(2,1)S(1)}, bf16[2048,512]{1,0:T(8,128)(2,1)S(1)}, u32[]{:S(2)}, u32[]{:S(2)}) collective-permute-start(bf16[2048,512]{1,0:T(8,128)(2,1)S(1)} %get-tuple-element.18.refs_4_), channel_id=1, source_target_pairs={{0,1},{1,0},{2,3},{3,2},{4,5},{5,4},{6,7},{7,6},{8,9},{9,8},{10,11... | collective-permute-start | bytes 6291464 | tf_op jit(solution)/shard_map/ppermute | solution.py:17
  4.1 1.6 %shard_map.101.refs_5_ = bf16[512,2048]{1,0:T(8,128)(2,1)S(1)} custom-call(bf16[512,2048]{1,0:T(8,128)(2,1)} %source.1), custom_call_target="tpu_custom_call" | custom-call | tf_op jit(solution)/shard_map/pallas_call | solution.py:139
  5.7 0.1 collective-permute-start.7
  5.8 3.1 %collective-permute-start = (bf16[8,2048]{1,0:T(8,128)(2,1)S(1)}, bf16[8,2048]{1,0:T(8,128)(2,1)S(1)}, u32[]{:S(2)}, u32[]{:S(2)}) collective-permute-start(bf16[8,2048]{1,0:T(8,128)(2,1)S(1)} %get-tuple-element.17), channel_id=1, source_target_pairs={{0,8},{1,9},{2,10},{3,11},{4,12},{5,13},{6,14},{7,15},{8,0},{9,1},... | collective-permute-start | bytes 98312 | tf_op jit(solution)/shard_map/ppermute | solution.py:17
  8.9 2.6 %collective-permute-start.1 = (bf16[8,2048]{1,0:T(8,128)(2,1)S(1)}, bf16[8,2048]{1,0:T(8,128)(2,1)S(1)}, u32[]{:S(2)}, u32[]{:S(2)}) collective-permute-start(bf16[8,2048]{1,0:T(8,128)(2,1)S(1)} %get-tuple-element.17), channel_id=1, source_target_pairs={{0,16},{1,17},{2,18},{3,19},{4,20},{5,21},{6,22},{7,23},{8,24},{9,... | collective-permute-start | bytes 98312 | tf_op jit(solution)/shard_map/ppermute | solution.py:17
  11.5 0.0 collective-permute-start.2
  11.5 0.0 collective-permute-done
  11.5 2.8 %collective-permute-done.1 = bf16[8,2048]{1,0:T(8,128)(2,1)S(1)} collective-permute-done((bf16[8,2048]{1,0:T(8,128)(2,1)S(1)}, bf16[8,2048]{1,0:T(8,128)(2,1)S(1)}, u32[]{:S(2)}, u32[]{:S(2)}) %collective-permute-start.1) | collective-permute-done | bytes 32800 | tf_op jit(solution)/shard_map/ppermute | solution.py:17
  14.3 2.9 %collective-permute-done.2 = bf16[8,2048]{1,0:T(8,128)(2,1)S(1)} collective-permute-done((bf16[8,2048]{1,0:T(8,128)(2,1)S(1)}, bf16[8,2048]{1,0:T(8,128)(2,1)S(1)}, u32[]{:S(2)}, u32[]{:S(2)}) %collective-permute-start.2) | collective-permute-done | bytes 32800 | tf_op jit(solution)/shard_map/ppermute | solution.py:17
  17.2 1.6 %collective-permute-start.3 = (bf16[32,2048]{1,0:T(8,128)(2,1)S(1)}, bf16[32,2048]{1,0:T(8,128)(2,1)S(1)}, u32[]{:S(2)}, u32[]{:S(2)}) collective-permute-start(bf16[32,2048]{1,0:T(8,128)(2,1)S(1)} %constant_dynamic-update-slice_fusion.refs_0_), channel_id=1, source_target_pairs={{0,2},{1,3},{2,0},{3,1},{4,6},{5,7},{6,4},{7,5},{8,10},{9,11},{10,... | collective-permute-start | bytes 393224 | tf_op jit(solution)/shard_map/ppermute | solution.py:17
  18.7 1.5 %collective-permute-start.4 = (bf16[32,2048]{1,0:T(8,128)(2,1)S(1)}, bf16[32,2048]{1,0:T(8,128)(2,1)S(1)}, u32[]{:S(2)}, u32[]{:S(2)}) collective-permute-start(bf16[32,2048]{1,0:T(8,128)(2,1)S(1)} %constant_dynamic-update-slice_fusion.refs_0_), channel_id=1, source_target_pairs={{0,4},{1,5},{2,6},{3,7},{4,0},{5,1},{6,2},{7,3},{8,12},{9,13},{10,... | collective-permute-start | bytes 393224 | tf_op jit(solution)/shard_map/ppermute | solution.py:17
  20.3 0.5 %collective-permute-start.5 = (bf16[32,2048]{1,0:T(8,128)(2,1)S(1)}, bf16[32,2048]{1,0:T(8,128)(2,1)S(1)}, u32[]{:S(2)}, u32[]{:S(2)}) collective-permute-start(bf16[32,2048]{1,0:T(8,128)(2,1)S(1)} %constant_dynamic-update-slice_fusion.refs_0_), channel_id=1, source_target_pairs={{0,6},{1,7},{2,4},{3,5},{4,2},{5,3},{6,0},{7,1},{8,14},{9,15},{10,... | collective-permute-start | bytes 393224 | tf_op jit(solution)/shard_map/ppermute | solution.py:17
  20.7 2.7 %collective-permute-done.3.refs_1_ = bf16[32,2048]{1,0:T(8,128)(2,1)S(1)} collective-permute-done((bf16[32,2048]{1,0:T(8,128)(2,1)S(1)}, bf16[32,2048]{1,0:T(8,128)(2,1)S(1)}, u32[]{:S(2)}, u32[]{:S(2)}) %collective-permute-start.3) | collective-permute-done | bytes 131104 | tf_op jit(solution)/shard_map/ppermute | solution.py:17
  23.4 1.2 %collective-permute-done.4.refs_2_ = bf16[32,2048]{1,0:T(8,128)(2,1)S(1)} collective-permute-done((bf16[32,2048]{1,0:T(8,128)(2,1)S(1)}, bf16[32,2048]{1,0:T(8,128)(2,1)S(1)}, u32[]{:S(2)}, u32[]{:S(2)}) %collective-permute-start.4) | collective-permute-done | bytes 131104 | tf_op jit(solution)/shard_map/ppermute | solution.py:17
  24.6 1.5 %collective-permute-done.5.refs_3_ = bf16[32,2048]{1,0:T(8,128)(2,1)S(1)} collective-permute-done((bf16[32,2048]{1,0:T(8,128)(2,1)S(1)}, bf16[32,2048]{1,0:T(8,128)(2,1)S(1)}, u32[]{:S(2)}, u32[]{:S(2)}) %collective-permute-start.5) | collective-permute-done | bytes 131104 | tf_op jit(solution)/shard_map/ppermute | solution.py:17
  26.1 0.0 collective-permute-done.6.refs_6_
  26.1 1.4 %shard_map.102 = (f32[32,2048]{1,0:T(8,128)S(1)}, bf16[32,2048]{1,0:T(8,128)(2,1)S(1)}, bf16[32,2048]{1,0:T(8,128)(2,1)S(1)}, bf16[32,2048]{1,0:T(8,128)(2,1)S(1)}) custom-call(bf16[32,2048]{1,0:T(8,128)(2,1)S(1)} %constant_dynamic-update-slice_fusion.refs_0_, bf16[32,2048]{1,0:T(8,128)(2,1)S(1)} %collective-permute-done.3.refs_1_, ...), custom_call_target="tpu_custom_call" | custom-call | flops 1073741824 | bytes 8388608 | tf_op jit(solution)/shard_map/pallas_call | solution.py:170
  27.5 0.5 %collective-permute-start.10 = (bf16[32,2048]{1,0:T(8,128)(2,1)S(1)}, bf16[32,2048]{1,0:T(8,128)(2,1)S(1)}, u32[]{:S(2)}, u32[]{:S(2)}) collective-permute-start(bf16[32,2048]{1,0:T(8,128)(2,1)S(1)} %get-tuple-element.22), channel_id=1, source_target_pairs={{0,6},{1,7},{2,4},{3,5},{4,2},{5,3},{6,0},{7,1},{8,14},{9,15},{10,... | collective-permute-start | bytes 393224 | tf_op jit(solution)/shard_map/ppermute | solution.py:17
  28.1 1.5 %collective-permute-start.9 = (bf16[32,2048]{1,0:T(8,128)(2,1)S(1)}, bf16[32,2048]{1,0:T(8,128)(2,1)S(1)}, u32[]{:S(2)}, u32[]{:S(2)}) collective-permute-start(bf16[32,2048]{1,0:T(8,128)(2,1)S(1)} %get-tuple-element.21), channel_id=1, source_target_pairs={{0,4},{1,5},{2,6},{3,7},{4,0},{5,1},{6,2},{7,3},{8,12},{9,13},{10,... | collective-permute-start | bytes 393224 | tf_op jit(solution)/shard_map/ppermute | solution.py:17
  29.6 1.5 %collective-permute-start.8 = (bf16[32,2048]{1,0:T(8,128)(2,1)S(1)}, bf16[32,2048]{1,0:T(8,128)(2,1)S(1)}, u32[]{:S(2)}, u32[]{:S(2)}) collective-permute-start(bf16[32,2048]{1,0:T(8,128)(2,1)S(1)} %get-tuple-element.20), channel_id=1, source_target_pairs={{0,2},{1,3},{2,0},{3,1},{4,6},{5,7},{6,4},{7,5},{8,10},{9,11},{10,... | collective-permute-start | bytes 393224 | tf_op jit(solution)/shard_map/ppermute | solution.py:17
  31.1 0.1 select_reduce_fusion
  31.2 2.4 %collective-permute-done.10 = bf16[32,2048]{1,0:T(8,128)(2,1)S(1)} collective-permute-done((bf16[32,2048]{1,0:T(8,128)(2,1)S(1)}, bf16[32,2048]{1,0:T(8,128)(2,1)S(1)}, u32[]{:S(2)}, u32[]{:S(2)}) %collective-permute-start.10) | collective-permute-done | bytes 131104 | tf_op jit(solution)/shard_map/ppermute | solution.py:17
  33.6 0.9 %collective-permute-done.9 = bf16[32,2048]{1,0:T(8,128)(2,1)S(1)} collective-permute-done((bf16[32,2048]{1,0:T(8,128)(2,1)S(1)}, bf16[32,2048]{1,0:T(8,128)(2,1)S(1)}, u32[]{:S(2)}, u32[]{:S(2)}) %collective-permute-start.9) | collective-permute-done | bytes 131104 | tf_op jit(solution)/shard_map/ppermute | solution.py:17
  34.4 0.1 collective-permute-done.8
  34.6 0.1 fusion.5
  34.6 0.6 %collective-permute-start.13 = (bf16[8,2048]{1,0:T(8,128)(2,1)S(1)}, bf16[8,2048]{1,0:T(8,128)(2,1)S(1)}, u32[]{:S(2)}, u32[]{:S(2)}) collective-permute-start(bf16[8,2048]{1,0:T(8,128)(2,1)S(1)} %get-tuple-element.26), channel_id=1, source_target_pairs={{0,24},{1,25},{2,26},{3,27},{4,28},{5,29},{6,30},{7,31},{8,16},{9,... | collective-permute-start | bytes 98312 | tf_op jit(solution)/shard_map/ppermute | solution.py:17
  35.2 0.0 collective-permute-start.12
  35.2 3.9 %collective-permute-start.11 = (bf16[8,2048]{1,0:T(8,128)(2,1)S(1)}, bf16[8,2048]{1,0:T(8,128)(2,1)S(1)}, u32[]{:S(2)}, u32[]{:S(2)}) collective-permute-start(bf16[8,2048]{1,0:T(8,128)(2,1)S(1)} %get-tuple-element.25), channel_id=1, source_target_pairs={{0,8},{1,9},{2,10},{3,11},{4,12},{5,13},{6,14},{7,15},{8,0},{9,1},... | collective-permute-start | bytes 98312 | tf_op jit(solution)/shard_map/ppermute | solution.py:17
  39.1 1.3 %collective-permute-done.13 = bf16[8,2048]{1,0:T(8,128)(2,1)S(1)} collective-permute-done((bf16[8,2048]{1,0:T(8,128)(2,1)S(1)}, bf16[8,2048]{1,0:T(8,128)(2,1)S(1)}, u32[]{:S(2)}, u32[]{:S(2)}) %collective-permute-start.13) | collective-permute-done | bytes 32800 | tf_op jit(solution)/shard_map/ppermute | solution.py:17
  40.4 0.6 %collective-permute-done.11 = bf16[8,2048]{1,0:T(8,128)(2,1)S(1)} collective-permute-done((bf16[8,2048]{1,0:T(8,128)(2,1)S(1)}, bf16[8,2048]{1,0:T(8,128)(2,1)S(1)}, u32[]{:S(2)}, u32[]{:S(2)}) %collective-permute-start.11) | collective-permute-done | bytes 32800 | tf_op jit(solution)/shard_map/ppermute | solution.py:17
  41.0 0.7 %fusion.4 = bf16[8,2048]{1,0:T(8,128)(2,1)} fusion(f32[8,2048]{1,0:T(8,128)S(1)} %get-tuple-element.15, f32[32,2048]{1,0:T(8,128)S(1)} %get-tuple-element.24, bf16[8,2048]{1,0:T(8,128)(2,1)S(1)} %collective-permute-done.13, bf16[8,2048]{1,0:T(8,128)(2,1)S(1)} %collective-permute-done.12, bf16[8,2048]{1,0:T(8,128)(2,1)S(1)} %collective-permute-done.11, ...), kind=kLoop, calls=%fused_computation.6 | loop fusion | flops 196608 | bytes 262272 | tf_op jit(solution)/shard_map/convert_element_type | solution.py:268
  (13 shorter events, 0.0 us)
Async XLA Ops:
  3.6 22.6 %collective-permute-start.6 = (bf16[2048,512]{1,0:T(8,128)(2,1)S(1)}, bf16[2048,512]{1,0:T(8,128)(2,1)S(1)}, u32[]{:S(2)}, u32[]{:S(2)}) collective-permute-start(bf16[2048,512]{1,0:T(8,128)(2,1)S(1)} %get-tuple-element.18.refs_4_), channel_id=1, source_target_pairs={{0,1},{1,0},{2,3},{3,2},{4,5},{5,4},{6,7},{7,6},{8,9},{9,8},{10,11... | collective-permute-start | bytes 6291464 | tf_op jit(solution)/shard_map/ppermute | solution.py:17
  5.7 20.4 %collective-permute-start.7 = (bf16[512,2048]{1,0:T(8,128)(2,1)S(1)}, bf16[512,2048]{1,0:T(8,128)(2,1)S(1)}, u32[]{:S(2)}, u32[]{:S(2)}) collective-permute-start(bf16[512,2048]{1,0:T(8,128)(2,1)S(1)} %shard_map.101.refs_5_), channel_id=1, source_target_pairs={{0,1},{1,0},{2,3},{3,2},{4,5},{5,4},{6,7},{7,6},{8,9},{9,8},{10,11... | collective-permute-start | bytes 6291464 | tf_op jit(solution)/shard_map/ppermute | solution.py:17
  5.8 5.7 %collective-permute-start = (bf16[8,2048]{1,0:T(8,128)(2,1)S(1)}, bf16[8,2048]{1,0:T(8,128)(2,1)S(1)}, u32[]{:S(2)}, u32[]{:S(2)}) collective-permute-start(bf16[8,2048]{1,0:T(8,128)(2,1)S(1)} %get-tuple-element.17), channel_id=1, source_target_pairs={{0,8},{1,9},{2,10},{3,11},{4,12},{5,13},{6,14},{7,15},{8,0},{9,1},... | collective-permute-start | bytes 98312 | tf_op jit(solution)/shard_map/ppermute | solution.py:17
  8.9 5.4 %collective-permute-start.1 = (bf16[8,2048]{1,0:T(8,128)(2,1)S(1)}, bf16[8,2048]{1,0:T(8,128)(2,1)S(1)}, u32[]{:S(2)}, u32[]{:S(2)}) collective-permute-start(bf16[8,2048]{1,0:T(8,128)(2,1)S(1)} %get-tuple-element.17), channel_id=1, source_target_pairs={{0,16},{1,17},{2,18},{3,19},{4,20},{5,21},{6,22},{7,23},{8,24},{9,... | collective-permute-start | bytes 98312 | tf_op jit(solution)/shard_map/ppermute | solution.py:17
  11.5 5.7 %collective-permute-start.2 = (bf16[8,2048]{1,0:T(8,128)(2,1)S(1)}, bf16[8,2048]{1,0:T(8,128)(2,1)S(1)}, u32[]{:S(2)}, u32[]{:S(2)}) collective-permute-start(bf16[8,2048]{1,0:T(8,128)(2,1)S(1)} %get-tuple-element.17), channel_id=1, source_target_pairs={{0,24},{1,25},{2,26},{3,27},{4,28},{5,29},{6,30},{7,31},{8,16},{9,... | collective-permute-start | bytes 98312 | tf_op jit(solution)/shard_map/ppermute | solution.py:17
  17.2 13.9 %copy-start = (f32[8,2]{0,1:T(2,128)S(1)}, f32[8,2]{0,1:T(2,128)}, u32[]{:S(2)}) copy-start(f32[8,2]{0,1:T(2,128)} %param.19) | copy-start | bytes 196
  17.2 13.9 %copy-start.1 = (s32[8,2]{0,1:T(2,128)S(1)}, s32[8,2]{0,1:T(2,128)}, u32[]{:S(2)}) copy-start(s32[8,2]{0,1:T(2,128)} %param.18) | copy-start | bytes 196
  17.2 6.2 %collective-permute-start.3 = (bf16[32,2048]{1,0:T(8,128)(2,1)S(1)}, bf16[32,2048]{1,0:T(8,128)(2,1)S(1)}, u32[]{:S(2)}, u32[]{:S(2)}) collective-permute-start(bf16[32,2048]{1,0:T(8,128)(2,1)S(1)} %constant_dynamic-update-slice_fusion.refs_0_), channel_id=1, source_target_pairs={{0,2},{1,3},{2,0},{3,1},{4,6},{5,7},{6,4},{7,5},{8,10},{9,11},{10,... | collective-permute-start | bytes 393224 | tf_op jit(solution)/shard_map/ppermute | solution.py:17
  18.7 5.9 %collective-permute-start.4 = (bf16[32,2048]{1,0:T(8,128)(2,1)S(1)}, bf16[32,2048]{1,0:T(8,128)(2,1)S(1)}, u32[]{:S(2)}, u32[]{:S(2)}) collective-permute-start(bf16[32,2048]{1,0:T(8,128)(2,1)S(1)} %constant_dynamic-update-slice_fusion.refs_0_), channel_id=1, source_target_pairs={{0,4},{1,5},{2,6},{3,7},{4,0},{5,1},{6,2},{7,3},{8,12},{9,13},{10,... | collective-permute-start | bytes 393224 | tf_op jit(solution)/shard_map/ppermute | solution.py:17
  20.3 5.9 %collective-permute-start.5 = (bf16[32,2048]{1,0:T(8,128)(2,1)S(1)}, bf16[32,2048]{1,0:T(8,128)(2,1)S(1)}, u32[]{:S(2)}, u32[]{:S(2)}) collective-permute-start(bf16[32,2048]{1,0:T(8,128)(2,1)S(1)} %constant_dynamic-update-slice_fusion.refs_0_), channel_id=1, source_target_pairs={{0,6},{1,7},{2,4},{3,5},{4,2},{5,3},{6,0},{7,1},{8,14},{9,15},{10,... | collective-permute-start | bytes 393224 | tf_op jit(solution)/shard_map/ppermute | solution.py:17
  27.5 6.0 %collective-permute-start.10 = (bf16[32,2048]{1,0:T(8,128)(2,1)S(1)}, bf16[32,2048]{1,0:T(8,128)(2,1)S(1)}, u32[]{:S(2)}, u32[]{:S(2)}) collective-permute-start(bf16[32,2048]{1,0:T(8,128)(2,1)S(1)} %get-tuple-element.22), channel_id=1, source_target_pairs={{0,6},{1,7},{2,4},{3,5},{4,2},{5,3},{6,0},{7,1},{8,14},{9,15},{10,... | collective-permute-start | bytes 393224 | tf_op jit(solution)/shard_map/ppermute | solution.py:17
  28.1 6.4 %collective-permute-start.9 = (bf16[32,2048]{1,0:T(8,128)(2,1)S(1)}, bf16[32,2048]{1,0:T(8,128)(2,1)S(1)}, u32[]{:S(2)}, u32[]{:S(2)}) collective-permute-start(bf16[32,2048]{1,0:T(8,128)(2,1)S(1)} %get-tuple-element.21), channel_id=1, source_target_pairs={{0,4},{1,5},{2,6},{3,7},{4,0},{5,1},{6,2},{7,3},{8,12},{9,13},{10,... | collective-permute-start | bytes 393224 | tf_op jit(solution)/shard_map/ppermute | solution.py:17
  29.6 5.0 %collective-permute-start.8 = (bf16[32,2048]{1,0:T(8,128)(2,1)S(1)}, bf16[32,2048]{1,0:T(8,128)(2,1)S(1)}, u32[]{:S(2)}, u32[]{:S(2)}) collective-permute-start(bf16[32,2048]{1,0:T(8,128)(2,1)S(1)} %get-tuple-element.20), channel_id=1, source_target_pairs={{0,2},{1,3},{2,0},{3,1},{4,6},{5,7},{6,4},{7,5},{8,10},{9,11},{10,... | collective-permute-start | bytes 393224 | tf_op jit(solution)/shard_map/ppermute | solution.py:17
  34.6 5.8 %collective-permute-start.13 = (bf16[8,2048]{1,0:T(8,128)(2,1)S(1)}, bf16[8,2048]{1,0:T(8,128)(2,1)S(1)}, u32[]{:S(2)}, u32[]{:S(2)}) collective-permute-start(bf16[8,2048]{1,0:T(8,128)(2,1)S(1)} %get-tuple-element.26), channel_id=1, source_target_pairs={{0,24},{1,25},{2,26},{3,27},{4,28},{5,29},{6,30},{7,31},{8,16},{9,... | collective-permute-start | bytes 98312 | tf_op jit(solution)/shard_map/ppermute | solution.py:17
  35.2 5.2 %collective-permute-start.12 = (bf16[8,2048]{1,0:T(8,128)(2,1)S(1)}, bf16[8,2048]{1,0:T(8,128)(2,1)S(1)}, u32[]{:S(2)}, u32[]{:S(2)}) collective-permute-start(bf16[8,2048]{1,0:T(8,128)(2,1)S(1)} %get-tuple-element.27), channel_id=1, source_target_pairs={{0,16},{1,17},{2,18},{3,19},{4,20},{5,21},{6,22},{7,23},{8,24},{9,... | collective-permute-start | bytes 98312 | tf_op jit(solution)/shard_map/ppermute | solution.py:17
  35.2 5.8 %collective-permute-start.11 = (bf16[8,2048]{1,0:T(8,128)(2,1)S(1)}, bf16[8,2048]{1,0:T(8,128)(2,1)S(1)}, u32[]{:S(2)}, u32[]{:S(2)}) collective-permute-start(bf16[8,2048]{1,0:T(8,128)(2,1)S(1)} %get-tuple-element.25), channel_id=1, source_target_pairs={{0,8},{1,9},{2,10},{3,11},{4,12},{5,13},{6,14},{7,15},{8,0},{9,1},... | collective-permute-start | bytes 98312 | tf_op jit(solution)/shard_map/ppermute | solution.py:17

commit v7 on v6

--- a/solution.py
+++ b/solution.py
@@ -8,7 +8,6 @@
 HEADS = 16
 SPLIT = 8
 CORES = 2
-PIECES = 4
 VMEM_LIMIT = 16 * 1024 * 1024
 
 
@@ -37,27 +36,24 @@
     streams, width = hidden.shape
     span = key_buf.shape[1]
     head_size = width // HEADS
-    group = key_buf.shape[0] // PIECES
     small = [
         pltpu.make_async_copy(query_in, query, small_sem.at[0]),
         pltpu.make_async_copy(lengths_in, lengths, small_sem.at[1]),
         pltpu.make_async_copy(hidden_in, hidden, small_sem.at[2]),
         pltpu.make_async_copy(gain_in, gain, small_sem.at[3]),
     ]
-    pieces = [pl.ds(piece * group, group) for piece in range(PIECES)]
-    key_copies = [pltpu.make_async_copy(keys.at[p], key_buf.at[p], key_sem.at[i]) for i, p in enumerate(pieces)]
-    value_copies = [pltpu.make_async_copy(values.at[p], value_buf.at[p], value_sem.at[i]) for i, p in enumerate(pieces)]
+    key_copy = pltpu.make_async_copy(keys, key_buf, key_sem)
+    value_copy = pltpu.make_async_copy(values, value_buf, value_sem)
     weight_copy = pltpu.make_async_copy(w_in_from, w_in, small_sem.at[4])
-    for copy in small + key_copies + value_copies + [weight_copy]:
+    for copy in small + [key_copy, value_copy, weight_copy]:
         copy.start()
     owner = lax.broadcasted_iota(jnp.int32, (HEADS, width), 1) // head_size
     own = owner == lax.broadcasted_iota(jnp.int32, (HEADS, width), 0)
     position = lax.broadcasted_iota(jnp.int32, (HEADS, span), 1)
     small[0].wait()
     small[1].wait()
+    key_copy.wait()
     for b in range(streams):
-        if b % group == 0:
-            key_copies[b // group].wait()
         spread = jnp.where(own, query[b : b + 1, :].astype(jnp.float32), 0.0).astype(jnp.bfloat16)
         scores = lax.dot_general(spread, key_buf[b], (((1,), (1,)), ((), ())), preferred_element_type=jnp.float32)
         scores = scores / jnp.sqrt(jnp.float32(head_size))
@@ -65,9 +61,8 @@
     scores = score_buf[...]
     expo = jnp.exp(scores - jnp.max(scores, axis=-1, keepdims=True))
     score_buf[...] = expo / jnp.sum(expo, axis=-1, keepdims=True)
+    value_copy.wait()
     for b in range(streams):
-        if b % group == 0:
-            value_copies[b // group].wait()
         probabilities = score_buf[b * HEADS : (b + 1) * HEADS, :].astype(jnp.bfloat16)
         every = jnp.dot(probabilities, value_buf[b], preferred_element_type=jnp.float32)
         for h in range(HEADS):
@@ -123,8 +118,8 @@
             pltpu.VMEM((streams, span, width), source_values.dtype),
             pltpu.VMEM((streams * HEADS, span), jnp.float32),
             pltpu.SemaphoreType.DMA((5,)),
-            pltpu.SemaphoreType.DMA((PIECES,)),
-            pltpu.SemaphoreType.DMA((PIECES,)),
+            pltpu.SemaphoreType.DMA(()),
+            pltpu.SemaphoreType.DMA(()),
         ],
         compiler_params=pltpu.CompilerParams(vmem_limit_bytes=VMEM_LIMIT),
     )(*[pltpu.with_memory_space_constraint(array, pltpu.HBM) for array in arrays])

time: 41.8 us -> 41.4 us (level)
  no operation moved by 1% of the time
where the time goes in v7:
time: 41.4 us; the launch traced here: 41.3 us
  starting transfers between devices  17.8 us (43%)
  waiting for transfers between devices  16.4 us (40%)
  Pallas kernels  6.13 us (15%)
  other arithmetic  0.85 us (2%)
    ppermute x14, starting transfers between devices, swap(): return lax.ppermute(value, 'expert', pairs)  17.8 us
    ppermute x14, waiting for transfers between devices, swap(): return lax.ppermute(value, 'expert', pairs)  16.4 us
    pallas_call x1, Pallas kernels, attend(): pl.pallas_call(attend_kernel, out_shape=(pltpu.VMEM((streams, width), jnp...  3.16 us
    pallas_call x1, Pallas kernels, bring(): pl.pallas_call(kernel, out_shape=pltpu.VMEM(array.shape, array.dtype), in...  1.6 us
    pallas_call x1, Pallas kernels, feed_forward(): pl.pallas_call(kernel, out_shape=[jax.ShapeDtypeStruct((height, width), k...  1.38 us
  transfers between devices with their start and end apart: 14, of which 10 were waited for; matrix products, arithmetic and copies ran while one was open for 0% of the time, Pallas kernels for 4%

profile of v7, /device:TPU:0, one launch (start us, length us, event | category | flops | bytes accessed | tf_op | source)
XLA Modules:
  0.0 41.3 jit_solution(9671049654167488565)
XLA Ops:
  0.0 3.2 %shard_map.100 = (f32[8,2048]{1,0:T(8,128)S(1)}, bf16[8,2048]{1,0:T(8,128)(2,1)S(1)}, bf16[2048,512]{1,0:T(8,128)(2,1)S(1)}) custom-call(s32[8]{0:T(128)} %lengths_in, bf16[8,2048]{1,0:T(8,128)(2,1)} %hidden_in.1, bf16[8,2048]{1,0:T(8,128)(2,1)} %query_in.1, bf16[8,64,2048]{2,1,0:T(8,128)(2,1)} %keys.1, bf16[8,64,2048]{2,1,0:T(8,128)(2,1)} %values.1, ...), custom_call_target="tpu_custom_call" | custom-call | tf_op jit(solution)/shard_map/pallas_call | solution.py:103
  3.2 0.6 %collective-permute-start.6 = (bf16[2048,512]{1,0:T(8,128)(2,1)S(1)}, bf16[2048,512]{1,0:T(8,128)(2,1)S(1)}, u32[]{:S(2)}, u32[]{:S(2)}) collective-permute-start(bf16[2048,512]{1,0:T(8,128)(2,1)S(1)} %get-tuple-element.18.refs_4_), channel_id=1, source_target_pairs={{0,1},{1,0},{2,3},{3,2},{4,5},{5,4},{6,7},{7,6},{8,9},{9,8},{10,11... | collective-permute-start | bytes 6291464 | tf_op jit(solution)/shard_map/ppermute | solution.py:16
  3.7 1.6 %shard_map.101.refs_5_ = bf16[512,2048]{1,0:T(8,128)(2,1)S(1)} custom-call(bf16[512,2048]{1,0:T(8,128)(2,1)} %source.1), custom_call_target="tpu_custom_call" | custom-call | tf_op jit(solution)/shard_map/pallas_call | solution.py:134
  5.3 0.1 collective-permute-start.7
  5.4 3.1 %collective-permute-start = (bf16[8,2048]{1,0:T(8,128)(2,1)S(1)}, bf16[8,2048]{1,0:T(8,128)(2,1)S(1)}, u32[]{:S(2)}, u32[]{:S(2)}) collective-permute-start(bf16[8,2048]{1,0:T(8,128)(2,1)S(1)} %get-tuple-element.17), channel_id=1, source_target_pairs={{0,8},{1,9},{2,10},{3,11},{4,12},{5,13},{6,14},{7,15},{8,0},{9,1},... | collective-permute-start | bytes 98312 | tf_op jit(solution)/shard_map/ppermute | solution.py:16
  8.5 2.6 %collective-permute-start.1 = (bf16[8,2048]{1,0:T(8,128)(2,1)S(1)}, bf16[8,2048]{1,0:T(8,128)(2,1)S(1)}, u32[]{:S(2)}, u32[]{:S(2)}) collective-permute-start(bf16[8,2048]{1,0:T(8,128)(2,1)S(1)} %get-tuple-element.17), channel_id=1, source_target_pairs={{0,16},{1,17},{2,18},{3,19},{4,20},{5,21},{6,22},{7,23},{8,24},{9,... | collective-permute-start | bytes 98312 | tf_op jit(solution)/shard_map/ppermute | solution.py:16
  11.1 0.0 collective-permute-start.2
  11.1 0.0 collective-permute-done
  11.1 2.8 %collective-permute-done.1 = bf16[8,2048]{1,0:T(8,128)(2,1)S(1)} collective-permute-done((bf16[8,2048]{1,0:T(8,128)(2,1)S(1)}, bf16[8,2048]{1,0:T(8,128)(2,1)S(1)}, u32[]{:S(2)}, u32[]{:S(2)}) %collective-permute-start.1) | collective-permute-done | bytes 32800 | tf_op jit(solution)/shard_map/ppermute | solution.py:16
  13.9 2.9 %collective-permute-done.2 = bf16[8,2048]{1,0:T(8,128)(2,1)S(1)} collective-permute-done((bf16[8,2048]{1,0:T(8,128)(2,1)S(1)}, bf16[8,2048]{1,0:T(8,128)(2,1)S(1)}, u32[]{:S(2)}, u32[]{:S(2)}) %collective-permute-start.2) | collective-permute-done | bytes 32800 | tf_op jit(solution)/shard_map/ppermute | solution.py:16
  16.8 1.6 %collective-permute-start.3 = (bf16[32,2048]{1,0:T(8,128)(2,1)S(1)}, bf16[32,2048]{1,0:T(8,128)(2,1)S(1)}, u32[]{:S(2)}, u32[]{:S(2)}) collective-permute-start(bf16[32,2048]{1,0:T(8,128)(2,1)S(1)} %constant_dynamic-update-slice_fusion.refs_0_), channel_id=1, source_target_pairs={{0,2},{1,3},{2,0},{3,1},{4,6},{5,7},{6,4},{7,5},{8,10},{9,11},{10,... | collective-permute-start | bytes 393224 | tf_op jit(solution)/shard_map/ppermute | solution.py:16
  18.3 1.5 %collective-permute-start.4 = (bf16[32,2048]{1,0:T(8,128)(2,1)S(1)}, bf16[32,2048]{1,0:T(8,128)(2,1)S(1)}, u32[]{:S(2)}, u32[]{:S(2)}) collective-permute-start(bf16[32,2048]{1,0:T(8,128)(2,1)S(1)} %constant_dynamic-update-slice_fusion.refs_0_), channel_id=1, source_target_pairs={{0,4},{1,5},{2,6},{3,7},{4,0},{5,1},{6,2},{7,3},{8,12},{9,13},{10,... | collective-permute-start | bytes 393224 | tf_op jit(solution)/shard_map/ppermute | solution.py:16
  19.9 0.5 %collective-permute-start.5 = (bf16[32,2048]{1,0:T(8,128)(2,1)S(1)}, bf16[32,2048]{1,0:T(8,128)(2,1)S(1)}, u32[]{:S(2)}, u32[]{:S(2)}) collective-permute-start(bf16[32,2048]{1,0:T(8,128)(2,1)S(1)} %constant_dynamic-update-slice_fusion.refs_0_), channel_id=1, source_target_pairs={{0,6},{1,7},{2,4},{3,5},{4,2},{5,3},{6,0},{7,1},{8,14},{9,15},{10,... | collective-permute-start | bytes 393224 | tf_op jit(solution)/shard_map/ppermute | solution.py:16
  20.3 2.7 %collective-permute-done.3.refs_1_ = bf16[32,2048]{1,0:T(8,128)(2,1)S(1)} collective-permute-done((bf16[32,2048]{1,0:T(8,128)(2,1)S(1)}, bf16[32,2048]{1,0:T(8,128)(2,1)S(1)}, u32[]{:S(2)}, u32[]{:S(2)}) %collective-permute-start.3) | collective-permute-done | bytes 131104 | tf_op jit(solution)/shard_map/ppermute | solution.py:16
  23.0 1.2 %collective-permute-done.4.refs_2_ = bf16[32,2048]{1,0:T(8,128)(2,1)S(1)} collective-permute-done((bf16[32,2048]{1,0:T(8,128)(2,1)S(1)}, bf16[32,2048]{1,0:T(8,128)(2,1)S(1)}, u32[]{:S(2)}, u32[]{:S(2)}) %collective-permute-start.4) | collective-permute-done | bytes 131104 | tf_op jit(solution)/shard_map/ppermute | solution.py:16
  24.2 1.5 %collective-permute-done.5.refs_3_ = bf16[32,2048]{1,0:T(8,128)(2,1)S(1)} collective-permute-done((bf16[32,2048]{1,0:T(8,128)(2,1)S(1)}, bf16[32,2048]{1,0:T(8,128)(2,1)S(1)}, u32[]{:S(2)}, u32[]{:S(2)}) %collective-permute-start.5) | collective-permute-done | bytes 131104 | tf_op jit(solution)/shard_map/ppermute | solution.py:16
  25.7 0.0 collective-permute-done.6.refs_6_
  25.7 0.0 collective-permute-done.7.refs_7_
  25.7 1.4 %shard_map.102 = (f32[32,2048]{1,0:T(8,128)S(1)}, bf16[32,2048]{1,0:T(8,128)(2,1)S(1)}, bf16[32,2048]{1,0:T(8,128)(2,1)S(1)}, bf16[32,2048]{1,0:T(8,128)(2,1)S(1)}) custom-call(bf16[32,2048]{1,0:T(8,128)(2,1)S(1)} %constant_dynamic-update-slice_fusion.refs_0_, bf16[32,2048]{1,0:T(8,128)(2,1)S(1)} %collective-permute-done.3.refs_1_, ...), custom_call_target="tpu_custom_call" | custom-call | flops 1073741824 | bytes 8388608 | tf_op jit(solution)/shard_map/pallas_call | solution.py:165
  27.1 0.5 %collective-permute-start.10 = (bf16[32,2048]{1,0:T(8,128)(2,1)S(1)}, bf16[32,2048]{1,0:T(8,128)(2,1)S(1)}, u32[]{:S(2)}, u32[]{:S(2)}) collective-permute-start(bf16[32,2048]{1,0:T(8,128)(2,1)S(1)} %get-tuple-element.22), channel_id=1, source_target_pairs={{0,6},{1,7},{2,4},{3,5},{4,2},{5,3},{6,0},{7,1},{8,14},{9,15},{10,... | collective-permute-start | bytes 393224 | tf_op jit(solution)/shard_map/ppermute | solution.py:16
  27.7 1.5 %collective-permute-start.9 = (bf16[32,2048]{1,0:T(8,128)(2,1)S(1)}, bf16[32,2048]{1,0:T(8,128)(2,1)S(1)}, u32[]{:S(2)}, u32[]{:S(2)}) collective-permute-start(bf16[32,2048]{1,0:T(8,128)(2,1)S(1)} %get-tuple-element.21), channel_id=1, source_target_pairs={{0,4},{1,5},{2,6},{3,7},{4,0},{5,1},{6,2},{7,3},{8,12},{9,13},{10,... | collective-permute-start | bytes 393224 | tf_op jit(solution)/shard_map/ppermute | solution.py:16
  29.2 1.5 %collective-permute-start.8 = (bf16[32,2048]{1,0:T(8,128)(2,1)S(1)}, bf16[32,2048]{1,0:T(8,128)(2,1)S(1)}, u32[]{:S(2)}, u32[]{:S(2)}) collective-permute-start(bf16[32,2048]{1,0:T(8,128)(2,1)S(1)} %get-tuple-element.20), channel_id=1, source_target_pairs={{0,2},{1,3},{2,0},{3,1},{4,6},{5,7},{6,4},{7,5},{8,10},{9,11},{10,... | collective-permute-start | bytes 393224 | tf_op jit(solution)/shard_map/ppermute | solution.py:16
  30.7 0.1 select_reduce_fusion
  30.8 2.4 %collective-permute-done.10 = bf16[32,2048]{1,0:T(8,128)(2,1)S(1)} collective-permute-done((bf16[32,2048]{1,0:T(8,128)(2,1)S(1)}, bf16[32,2048]{1,0:T(8,128)(2,1)S(1)}, u32[]{:S(2)}, u32[]{:S(2)}) %collective-permute-start.10) | collective-permute-done | bytes 131104 | tf_op jit(solution)/shard_map/ppermute | solution.py:16
  33.1 0.9 %collective-permute-done.9 = bf16[32,2048]{1,0:T(8,128)(2,1)S(1)} collective-permute-done((bf16[32,2048]{1,0:T(8,128)(2,1)S(1)}, bf16[32,2048]{1,0:T(8,128)(2,1)S(1)}, u32[]{:S(2)}, u32[]{:S(2)}) %collective-permute-start.9) | collective-permute-done | bytes 131104 | tf_op jit(solution)/shard_map/ppermute | solution.py:16
  34.0 0.1 collective-permute-done.8
  34.1 0.1 fusion.5
  34.2 0.6 %collective-permute-start.13 = (bf16[8,2048]{1,0:T(8,128)(2,1)S(1)}, bf16[8,2048]{1,0:T(8,128)(2,1)S(1)}, u32[]{:S(2)}, u32[]{:S(2)}) collective-permute-start(bf16[8,2048]{1,0:T(8,128)(2,1)S(1)} %get-tuple-element.26), channel_id=1, source_target_pairs={{0,24},{1,25},{2,26},{3,27},{4,28},{5,29},{6,30},{7,31},{8,16},{9,... | collective-permute-start | bytes 98312 | tf_op jit(solution)/shard_map/ppermute | solution.py:16
  34.8 3.9 %collective-permute-start.11 = (bf16[8,2048]{1,0:T(8,128)(2,1)S(1)}, bf16[8,2048]{1,0:T(8,128)(2,1)S(1)}, u32[]{:S(2)}, u32[]{:S(2)}) collective-permute-start(bf16[8,2048]{1,0:T(8,128)(2,1)S(1)} %get-tuple-element.25), channel_id=1, source_target_pairs={{0,8},{1,9},{2,10},{3,11},{4,12},{5,13},{6,14},{7,15},{8,0},{9,1},... | collective-permute-start | bytes 98312 | tf_op jit(solution)/shard_map/ppermute | solution.py:16
  38.7 1.3 %collective-permute-done.13 = bf16[8,2048]{1,0:T(8,128)(2,1)S(1)} collective-permute-done((bf16[8,2048]{1,0:T(8,128)(2,1)S(1)}, bf16[8,2048]{1,0:T(8,128)(2,1)S(1)}, u32[]{:S(2)}, u32[]{:S(2)}) %collective-permute-start.13) | collective-permute-done | bytes 32800 | tf_op jit(solution)/shard_map/ppermute | solution.py:16
  40.0 0.6 %collective-permute-done.11 = bf16[8,2048]{1,0:T(8,128)(2,1)S(1)} collective-permute-done((bf16[8,2048]{1,0:T(8,128)(2,1)S(1)}, bf16[8,2048]{1,0:T(8,128)(2,1)S(1)}, u32[]{:S(2)}, u32[]{:S(2)}) %collective-permute-start.11) | collective-permute-done | bytes 32800 | tf_op jit(solution)/shard_map/ppermute | solution.py:16
  40.6 0.7 %fusion.4 = bf16[8,2048]{1,0:T(8,128)(2,1)} fusion(f32[8,2048]{1,0:T(8,128)S(1)} %get-tuple-element.15, f32[32,2048]{1,0:T(8,128)S(1)} %get-tuple-element.24, bf16[8,2048]{1,0:T(8,128)(2,1)S(1)} %collective-permute-done.13, bf16[8,2048]{1,0:T(8,128)(2,1)S(1)} %collective-permute-done.12, bf16[8,2048]{1,0:T(8,128)(2,1)S(1)} %collective-permute-done.11, ...), kind=kLoop, calls=%fused_computation.6 | loop fusion | flops 196608 | bytes 262272 | tf_op jit(solution)/shard_map/convert_element_type | solution.py:263
  (13 shorter events, 0.0 us)
Async XLA Ops:
  3.2 22.6 %collective-permute-start.6 = (bf16[2048,512]{1,0:T(8,128)(2,1)S(1)}, bf16[2048,512]{1,0:T(8,128)(2,1)S(1)}, u32[]{:S(2)}, u32[]{:S(2)}) collective-permute-start(bf16[2048,512]{1,0:T(8,128)(2,1)S(1)} %get-tuple-element.18.refs_4_), channel_id=1, source_target_pairs={{0,1},{1,0},{2,3},{3,2},{4,5},{5,4},{6,7},{7,6},{8,9},{9,8},{10,11... | collective-permute-start | bytes 6291464 | tf_op jit(solution)/shard_map/ppermute | solution.py:16
  5.3 20.4 %collective-permute-start.7 = (bf16[512,2048]{1,0:T(8,128)(2,1)S(1)}, bf16[512,2048]{1,0:T(8,128)(2,1)S(1)}, u32[]{:S(2)}, u32[]{:S(2)}) collective-permute-start(bf16[512,2048]{1,0:T(8,128)(2,1)S(1)} %shard_map.101.refs_5_), channel_id=1, source_target_pairs={{0,1},{1,0},{2,3},{3,2},{4,5},{5,4},{6,7},{7,6},{8,9},{9,8},{10,11... | collective-permute-start | bytes 6291464 | tf_op jit(solution)/shard_map/ppermute | solution.py:16
  5.4 5.7 %collective-permute-start = (bf16[8,2048]{1,0:T(8,128)(2,1)S(1)}, bf16[8,2048]{1,0:T(8,128)(2,1)S(1)}, u32[]{:S(2)}, u32[]{:S(2)}) collective-permute-start(bf16[8,2048]{1,0:T(8,128)(2,1)S(1)} %get-tuple-element.17), channel_id=1, source_target_pairs={{0,8},{1,9},{2,10},{3,11},{4,12},{5,13},{6,14},{7,15},{8,0},{9,1},... | collective-permute-start | bytes 98312 | tf_op jit(solution)/shard_map/ppermute | solution.py:16
  8.5 5.4 %collective-permute-start.1 = (bf16[8,2048]{1,0:T(8,128)(2,1)S(1)}, bf16[8,2048]{1,0:T(8,128)(2,1)S(1)}, u32[]{:S(2)}, u32[]{:S(2)}) collective-permute-start(bf16[8,2048]{1,0:T(8,128)(2,1)S(1)} %get-tuple-element.17), channel_id=1, source_target_pairs={{0,16},{1,17},{2,18},{3,19},{4,20},{5,21},{6,22},{7,23},{8,24},{9,... | collective-permute-start | bytes 98312 | tf_op jit(solution)/shard_map/ppermute | solution.py:16
  11.1 5.7 %collective-permute-start.2 = (bf16[8,2048]{1,0:T(8,128)(2,1)S(1)}, bf16[8,2048]{1,0:T(8,128)(2,1)S(1)}, u32[]{:S(2)}, u32[]{:S(2)}) collective-permute-start(bf16[8,2048]{1,0:T(8,128)(2,1)S(1)} %get-tuple-element.17), channel_id=1, source_target_pairs={{0,24},{1,25},{2,26},{3,27},{4,28},{5,29},{6,30},{7,31},{8,16},{9,... | collective-permute-start | bytes 98312 | tf_op jit(solution)/shard_map/ppermute | solution.py:16
  16.8 13.9 %copy-start = (f32[8,2]{0,1:T(2,128)S(1)}, f32[8,2]{0,1:T(2,128)}, u32[]{:S(2)}) copy-start(f32[8,2]{0,1:T(2,128)} %param.19) | copy-start | bytes 196
  16.8 13.9 %copy-start.1 = (s32[8,2]{0,1:T(2,128)S(1)}, s32[8,2]{0,1:T(2,128)}, u32[]{:S(2)}) copy-start(s32[8,2]{0,1:T(2,128)} %param.18) | copy-start | bytes 196
  16.8 6.2 %collective-permute-start.3 = (bf16[32,2048]{1,0:T(8,128)(2,1)S(1)}, bf16[32,2048]{1,0:T(8,128)(2,1)S(1)}, u32[]{:S(2)}, u32[]{:S(2)}) collective-permute-start(bf16[32,2048]{1,0:T(8,128)(2,1)S(1)} %constant_dynamic-update-slice_fusion.refs_0_), channel_id=1, source_target_pairs={{0,2},{1,3},{2,0},{3,1},{4,6},{5,7},{6,4},{7,5},{8,10},{9,11},{10,... | collective-permute-start | bytes 393224 | tf_op jit(solution)/shard_map/ppermute | solution.py:16
  18.3 5.9 %collective-permute-start.4 = (bf16[32,2048]{1,0:T(8,128)(2,1)S(1)}, bf16[32,2048]{1,0:T(8,128)(2,1)S(1)}, u32[]{:S(2)}, u32[]{:S(2)}) collective-permute-start(bf16[32,2048]{1,0:T(8,128)(2,1)S(1)} %constant_dynamic-update-slice_fusion.refs_0_), channel_id=1, source_target_pairs={{0,4},{1,5},{2,6},{3,7},{4,0},{5,1},{6,2},{7,3},{8,12},{9,13},{10,... | collective-permute-start | bytes 393224 | tf_op jit(solution)/shard_map/ppermute | solution.py:16
  19.9 5.9 %collective-permute-start.5 = (bf16[32,2048]{1,0:T(8,128)(2,1)S(1)}, bf16[32,2048]{1,0:T(8,128)(2,1)S(1)}, u32[]{:S(2)}, u32[]{:S(2)}) collective-permute-start(bf16[32,2048]{1,0:T(8,128)(2,1)S(1)} %constant_dynamic-update-slice_fusion.refs_0_), channel_id=1, source_target_pairs={{0,6},{1,7},{2,4},{3,5},{4,2},{5,3},{6,0},{7,1},{8,14},{9,15},{10,... | collective-permute-start | bytes 393224 | tf_op jit(solution)/shard_map/ppermute | solution.py:16
  27.1 6.0 %collective-permute-start.10 = (bf16[32,2048]{1,0:T(8,128)(2,1)S(1)}, bf16[32,2048]{1,0:T(8,128)(2,1)S(1)}, u32[]{:S(2)}, u32[]{:S(2)}) collective-permute-start(bf16[32,2048]{1,0:T(8,128)(2,1)S(1)} %get-tuple-element.22), channel_id=1, source_target_pairs={{0,6},{1,7},{2,4},{3,5},{4,2},{5,3},{6,0},{7,1},{8,14},{9,15},{10,... | collective-permute-start | bytes 393224 | tf_op jit(solution)/shard_map/ppermute | solution.py:16
  27.7 6.4 %collective-permute-start.9 = (bf16[32,2048]{1,0:T(8,128)(2,1)S(1)}, bf16[32,2048]{1,0:T(8,128)(2,1)S(1)}, u32[]{:S(2)}, u32[]{:S(2)}) collective-permute-start(bf16[32,2048]{1,0:T(8,128)(2,1)S(1)} %get-tuple-element.21), channel_id=1, source_target_pairs={{0,4},{1,5},{2,6},{3,7},{4,0},{5,1},{6,2},{7,3},{8,12},{9,13},{10,... | collective-permute-start | bytes 393224 | tf_op jit(solution)/shard_map/ppermute | solution.py:16
  29.2 5.0 %collective-permute-start.8 = (bf16[32,2048]{1,0:T(8,128)(2,1)S(1)}, bf16[32,2048]{1,0:T(8,128)(2,1)S(1)}, u32[]{:S(2)}, u32[]{:S(2)}) collective-permute-start(bf16[32,2048]{1,0:T(8,128)(2,1)S(1)} %get-tuple-element.20), channel_id=1, source_target_pairs={{0,2},{1,3},{2,0},{3,1},{4,6},{5,7},{6,4},{7,5},{8,10},{9,11},{10,... | collective-permute-start | bytes 393224 | tf_op jit(solution)/shard_map/ppermute | solution.py:16
  34.2 5.8 %collective-permute-start.13 = (bf16[8,2048]{1,0:T(8,128)(2,1)S(1)}, bf16[8,2048]{1,0:T(8,128)(2,1)S(1)}, u32[]{:S(2)}, u32[]{:S(2)}) collective-permute-start(bf16[8,2048]{1,0:T(8,128)(2,1)S(1)} %get-tuple-element.26), channel_id=1, source_target_pairs={{0,24},{1,25},{2,26},{3,27},{4,28},{5,29},{6,30},{7,31},{8,16},{9,... | collective-permute-start | bytes 98312 | tf_op jit(solution)/shard_map/ppermute | solution.py:16
  34.8 5.2 %collective-permute-start.12 = (bf16[8,2048]{1,0:T(8,128)(2,1)S(1)}, bf16[8,2048]{1,0:T(8,128)(2,1)S(1)}, u32[]{:S(2)}, u32[]{:S(2)}) collective-permute-start(bf16[8,2048]{1,0:T(8,128)(2,1)S(1)} %get-tuple-element.27), channel_id=1, source_target_pairs={{0,16},{1,17},{2,18},{3,19},{4,20},{5,21},{6,22},{7,23},{8,24},{9,... | collective-permute-start | bytes 98312 | tf_op jit(solution)/shard_map/ppermute | solution.py:16
  34.8 5.7 %collective-permute-start.11 = (bf16[8,2048]{1,0:T(8,128)(2,1)S(1)}, bf16[8,2048]{1,0:T(8,128)(2,1)S(1)}, u32[]{:S(2)}, u32[]{:S(2)}) collective-permute-start(bf16[8,2048]{1,0:T(8,128)(2,1)S(1)} %get-tuple-element.25), channel_id=1, source_target_pairs={{0,8},{1,9},{2,10},{3,11},{4,12},{5,13},{6,14},{7,15},{8,0},{9,1},... | collective-permute-start | bytes 98312 | tf_op jit(solution)/shard_map/ppermute | solution.py:16

commit v8 on v5

--- a/solution.py
+++ b/solution.py
@@ -8,13 +8,26 @@
 HEADS = 16
 SPLIT = 8
 CORES = 2
-PIECES = 4
 VMEM_LIMIT = 16 * 1024 * 1024
 
 
 def swap(value, distance, devices):
     pairs = [(source, source ^ distance) for source in range(devices)]
     return lax.ppermute(value, "expert", pairs)
+
+
+def chip_swap(value, step, devices):
+    orders = [chip_order(core) for core in range(CORES)]
+    pairs = [
+        (source, source ^ (CORES * orders[source % CORES][step - 1])) for source in range(devices)
+    ]
+    return lax.ppermute(value, "expert", pairs)
+
+
+def chip_order(core):
+    chips = SPLIT // CORES
+    nearer = list(range(1, chips - 1))
+    return [chips - 1] + (nearer if core == 0 else nearer[::-1])
 
 
 def outer_exchange(blocks, devices):
@@ -37,27 +50,24 @@
     streams, width = hidden.shape
     span = key_buf.shape[1]
     head_size = width // HEADS
-    group = key_buf.shape[0] // PIECES
     small = [
         pltpu.make_async_copy(query_in, query, small_sem.at[0]),
         pltpu.make_async_copy(lengths_in, lengths, small_sem.at[1]),
         pltpu.make_async_copy(hidden_in, hidden, small_sem.at[2]),
         pltpu.make_async_copy(gain_in, gain, small_sem.at[3]),
     ]
-    pieces = [pl.ds(piece * group, group) for piece in range(PIECES)]
-    key_copies = [pltpu.make_async_copy(keys.at[p], key_buf.at[p], key_sem.at[i]) for i, p in enumerate(pieces)]
-    value_copies = [pltpu.make_async_copy(values.at[p], value_buf.at[p], value_sem.at[i]) for i, p in enumerate(pieces)]
+    key_copy = pltpu.make_async_copy(keys, key_buf, key_sem)
+    value_copy = pltpu.make_async_copy(values, value_buf, value_sem)
     weight_copy = pltpu.make_async_copy(w_in_from, w_in, small_sem.at[4])
-    for copy in small + key_copies + value_copies + [weight_copy]:
+    for copy in small + [key_copy, value_copy, weight_copy]:
         copy.start()
     owner = lax.broadcasted_iota(jnp.int32, (HEADS, width), 1) // head_size
     own = owner == lax.broadcasted_iota(jnp.int32, (HEADS, width), 0)
     position = lax.broadcasted_iota(jnp.int32, (HEADS, span), 1)
     small[0].wait()
     small[1].wait()
+    key_copy.wait()
     for b in range(streams):
-        if b % group == 0:
-            key_copies[b // group].wait()
         spread = jnp.where(own, query[b : b + 1, :].astype(jnp.float32), 0.0).astype(jnp.bfloat16)
         scores = lax.dot_general(spread, key_buf[b], (((1,), (1,)), ((), ())), preferred_element_type=jnp.float32)
         scores = scores / jnp.sqrt(jnp.float32(head_size))
@@ -65,9 +75,8 @@
     scores = score_buf[...]
     expo = jnp.exp(scores - jnp.max(scores, axis=-1, keepdims=True))
     score_buf[...] = expo / jnp.sum(expo, axis=-1, keepdims=True)
+    value_copy.wait()
     for b in range(streams):
-        if b % group == 0:
-            value_copies[b // group].wait()
         probabilities = score_buf[b * HEADS : (b + 1) * HEADS, :].astype(jnp.bfloat16)
         every = jnp.dot(probabilities, value_buf[b], preferred_element_type=jnp.float32)
         for h in range(HEADS):
@@ -123,8 +132,8 @@
             pltpu.VMEM((streams, span, width), source_values.dtype),
             pltpu.VMEM((streams * HEADS, span), jnp.float32),
             pltpu.SemaphoreType.DMA((5,)),
-            pltpu.SemaphoreType.DMA((PIECES,)),
-            pltpu.SemaphoreType.DMA((PIECES,)),
+            pltpu.SemaphoreType.DMA(()),
+            pltpu.SemaphoreType.DMA(()),
         ],
         compiler_params=pltpu.CompilerParams(vmem_limit_bytes=VMEM_LIMIT),
     )(*[pltpu.with_memory_space_constraint(array, pltpu.HBM) for array in arrays])
@@ -239,7 +248,7 @@
         column = outer_exchange(blocks, devices)
     near = {0: jnp.concatenate(column, axis=0)}
     for step in range(1, chips):
-        near[step] = swap(near[0], CORES * step, devices)
+        near[step] = chip_swap(near[0], step, devices)
     other_in = swap(w_in, 1, devices)
     w_out = bring(w_out)
     other_out = swap(w_out, 1, devices)
@@ -256,7 +265,7 @@
     for place, (name, _, _) in enumerate(cuts):
         sums[name] = parts[0][place]
         for step in range(1, chips):
-            given = swap(parts[step][place], CORES * step, devices)
+            given = chip_swap(parts[step][place], step, devices)
             sums[name] = sums[name] + given.astype(jnp.float32)
     total = sums["reduce_chip"].reshape(-1, capacity, width)
     result = mixed

time: 42.5 us -> 41.9 us (0.986)
    ppermute x0 -> x9, starting transfers between devices: none -> 10.7 us  [chip_swap(): return lax.ppermute(value, 'expert', pairs)]
    ppermute x17 -> x8, starting transfers between devices: 21.2 us -> 10.7 us  [swap(): return lax.ppermute(value, 'expert', pairs)]
    ppermute x17 -> x8, waiting for transfers between devices: 13.6 us -> 8.35 us  [swap(): return lax.ppermute(value, 'expert', pairs)]
    ppermute x0 -> x9, waiting for transfers between devices: none -> 4.88 us  [chip_swap(): return lax.ppermute(value, 'expert', pairs)]
where the time goes in v8:
time: 41.9 us; the launch traced here: 41.7 us
  starting transfers between devices  21.4 us (51%)
  waiting for transfers between devices  13.2 us (32%)
  Pallas kernels  6.13 us (15%)
  other arithmetic  0.84 us (2%)
    ppermute x8, starting transfers between devices, swap(): return lax.ppermute(value, 'expert', pairs)  10.7 us
    ppermute x9, starting transfers between devices, chip_swap(): return lax.ppermute(value, 'expert', pairs)  10.7 us
    ppermute x8, waiting for transfers between devices, swap(): return lax.ppermute(value, 'expert', pairs)  8.35 us
    ppermute x9, waiting for transfers between devices, chip_swap(): return lax.ppermute(value, 'expert', pairs)  4.88 us
    pallas_call x1, Pallas kernels, attend(): pl.pallas_call(attend_kernel, out_shape=(pltpu.VMEM((streams, width), jnp...  3.16 us
    pallas_call x1, Pallas kernels, bring(): pl.pallas_call(kernel, out_shape=pltpu.VMEM(array.shape, array.dtype), in...  1.6 us
    pallas_call x1, Pallas kernels, feed_forward(): pl.pallas_call(kernel, out_shape=[jax.ShapeDtypeStruct((end - start, widt...  1.37 us
  transfers between devices with their start and end apart: 17, of which 8 were waited for; matrix products, arithmetic and copies ran while one was open for 0% of the time, Pallas kernels for 4%

profile of v8, /device:TPU:0, one launch (start us, length us, event | category | flops | bytes accessed | tf_op | source)
XLA Modules:
  0.0 41.7 jit_solution(13144892925578483139)
XLA Ops:
  0.0 3.2 %shard_map.100 = (f32[8,2048]{1,0:T(8,128)S(1)}, bf16[8,2048]{1,0:T(8,128)(2,1)S(1)}, bf16[2048,512]{1,0:T(8,128)(2,1)S(1)}) custom-call(s32[8]{0:T(128)} %lengths_in, bf16[8,2048]{1,0:T(8,128)(2,1)} %hidden_in.1, bf16[8,2048]{1,0:T(8,128)(2,1)} %query_in.1, bf16[8,64,2048]{2,1,0:T(8,128)(2,1)} %keys.1, bf16[8,64,2048]{2,1,0:T(8,128)(2,1)} %values.1, ...), custom_call_target="tpu_custom_call" | custom-call | tf_op jit(solution)/shard_map/pallas_call | solution.py:117
  3.2 0.6 %collective-permute-start.6 = (bf16[2048,512]{1,0:T(8,128)(2,1)S(1)}, bf16[2048,512]{1,0:T(8,128)(2,1)S(1)}, u32[]{:S(2)}, u32[]{:S(2)}) collective-permute-start(bf16[2048,512]{1,0:T(8,128)(2,1)S(1)} %get-tuple-element.22.refs_4_), channel_id=1, source_target_pairs={{0,1},{1,0},{2,3},{3,2},{4,5},{5,4},{6,7},{7,6},{8,9},{9,8},{10,11... | collective-permute-start | bytes 6291464 | tf_op jit(solution)/shard_map/ppermute | solution.py:16
  3.7 1.6 %shard_map.101.refs_5_ = bf16[512,2048]{1,0:T(8,128)(2,1)S(1)} custom-call(bf16[512,2048]{1,0:T(8,128)(2,1)} %source.1), custom_call_target="tpu_custom_call" | custom-call | tf_op jit(solution)/shard_map/pallas_call | solution.py:148
  5.3 0.1 collective-permute-start.7
  5.4 3.1 %collective-permute-start = (bf16[8,2048]{1,0:T(8,128)(2,1)S(1)}, bf16[8,2048]{1,0:T(8,128)(2,1)S(1)}, u32[]{:S(2)}, u32[]{:S(2)}) collective-permute-start(bf16[8,2048]{1,0:T(8,128)(2,1)S(1)} %get-tuple-element.21), channel_id=1, source_target_pairs={{0,8},{1,9},{2,10},{3,11},{4,12},{5,13},{6,14},{7,15},{8,0},{9,1},... | collective-permute-start | bytes 98312 | tf_op jit(solution)/shard_map/ppermute | solution.py:16
  8.5 2.6 %collective-permute-start.1 = (bf16[8,2048]{1,0:T(8,128)(2,1)S(1)}, bf16[8,2048]{1,0:T(8,128)(2,1)S(1)}, u32[]{:S(2)}, u32[]{:S(2)}) collective-permute-start(bf16[8,2048]{1,0:T(8,128)(2,1)S(1)} %get-tuple-element.21), channel_id=1, source_target_pairs={{0,16},{1,17},{2,18},{3,19},{4,20},{5,21},{6,22},{7,23},{8,24},{9,... | collective-permute-start | bytes 98312 | tf_op jit(solution)/shard_map/ppermute | solution.py:16
  11.1 0.0 collective-permute-start.2
  11.1 2.8 %collective-permute-done.1 = bf16[8,2048]{1,0:T(8,128)(2,1)S(1)} collective-permute-done((bf16[8,2048]{1,0:T(8,128)(2,1)S(1)}, bf16[8,2048]{1,0:T(8,128)(2,1)S(1)}, u32[]{:S(2)}, u32[]{:S(2)}) %collective-permute-start.1) | collective-permute-done | bytes 32800 | tf_op jit(solution)/shard_map/ppermute | solution.py:16
  13.9 2.9 %collective-permute-done.2 = bf16[8,2048]{1,0:T(8,128)(2,1)S(1)} collective-permute-done((bf16[8,2048]{1,0:T(8,128)(2,1)S(1)}, bf16[8,2048]{1,0:T(8,128)(2,1)S(1)}, u32[]{:S(2)}, u32[]{:S(2)}) %collective-permute-start.2) | collective-permute-done | bytes 32800 | tf_op jit(solution)/shard_map/ppermute | solution.py:16
  16.8 2.4 %collective-permute-start.3 = (bf16[32,2048]{1,0:T(8,128)(2,1)S(1)}, bf16[32,2048]{1,0:T(8,128)(2,1)S(1)}, u32[]{:S(2)}, u32[]{:S(2)}) collective-permute-start(bf16[32,2048]{1,0:T(8,128)(2,1)S(1)} %constant_dynamic-update-slice_fusion.refs_0_), channel_id=1, source_target_pairs={{0,6},{1,7},{2,4},{3,5},{4,2},{5,3},{6,0},{7,1},{8,14},{9,15},{10,... | collective-permute-start | bytes 393224 | tf_op jit(solution)/shard_map/ppermute | solution.py:24
  19.2 0.5 %collective-permute-start.4 = (bf16[32,2048]{1,0:T(8,128)(2,1)S(1)}, bf16[32,2048]{1,0:T(8,128)(2,1)S(1)}, u32[]{:S(2)}, u32[]{:S(2)}) collective-permute-start(bf16[32,2048]{1,0:T(8,128)(2,1)S(1)} %constant_dynamic-update-slice_fusion.refs_0_), channel_id=1, source_target_pairs={{0,2},{1,5},{2,0},{3,7},{4,6},{5,1},{6,4},{7,3},{8,10},{9,13},{10,... | collective-permute-start | bytes 393224 | tf_op jit(solution)/shard_map/ppermute | solution.py:24
  19.8 0.5 %collective-permute-start.5 = (bf16[32,2048]{1,0:T(8,128)(2,1)S(1)}, bf16[32,2048]{1,0:T(8,128)(2,1)S(1)}, u32[]{:S(2)}, u32[]{:S(2)}) collective-permute-start(bf16[32,2048]{1,0:T(8,128)(2,1)S(1)} %constant_dynamic-update-slice_fusion.refs_0_), channel_id=1, source_target_pairs={{0,4},{1,3},{2,6},{3,1},{4,0},{5,7},{6,2},{7,5},{8,12},{9,11},{10,... | collective-permute-start | bytes 393224 | tf_op jit(solution)/shard_map/ppermute | solution.py:24
  20.3 3.7 %collective-permute-done.3.refs_1_ = bf16[32,2048]{1,0:T(8,128)(2,1)S(1)} collective-permute-done((bf16[32,2048]{1,0:T(8,128)(2,1)S(1)}, bf16[32,2048]{1,0:T(8,128)(2,1)S(1)}, u32[]{:S(2)}, u32[]{:S(2)}) %collective-permute-start.3) | collective-permute-done | bytes 131104 | tf_op jit(solution)/shard_map/ppermute | solution.py:24
  24.0 0.3 collective-permute-done.4.refs_2_
  24.3 0.7 %collective-permute-done.5.refs_3_ = bf16[32,2048]{1,0:T(8,128)(2,1)S(1)} collective-permute-done((bf16[32,2048]{1,0:T(8,128)(2,1)S(1)}, bf16[32,2048]{1,0:T(8,128)(2,1)S(1)}, u32[]{:S(2)}, u32[]{:S(2)}) %collective-permute-start.5) | collective-permute-done | bytes 131104 | tf_op jit(solution)/shard_map/ppermute | solution.py:24
  25.1 0.0 collective-permute-done.6.refs_6_
  25.1 1.4 %shard_map.102 = (f32[24,2048]{1,0:T(8,128)S(1)}, f32[8,2048]{1,0:T(8,128)S(1)}, bf16[24,2048]{1,0:T(8,128)(2,1)S(1)}, bf16[8,2048]{1,0:T(8,128)(2,1)S(1)}, bf16...) custom-call(bf16[32,2048]{1,0:T(8,128)(2,1)S(1)} %constant_dynamic-u, ...), custom_call_target="tpu_custom_call" | custom-call | flops 1073741824 | bytes 8388608 | tf_op jit(solution)/shard_map/pallas_call | solution.py:180
  26.5 1.7 %collective-permute-start.11 = (bf16[24,2048]{1,0:T(8,128)(2,1)S(1)}, bf16[24,2048]{1,0:T(8,128)(2,1)S(1)}, u32[]{:S(2)}, u32[]{:S(2)}) collective-permute-start(bf16[24,2048]{1,0:T(8,128)(2,1)S(1)} %get-tuple-element.28), channel_id=1, source_target_pairs={{0,6},{1,7},{2,4},{3,5},{4,2},{5,3},{6,0},{7,1},{8,14},{9,15},{10,... | collective-permute-start | bytes 294920 | tf_op jit(solution)/shard_map/ppermute | solution.py:24
  28.2 0.6 %collective-permute-start.12 = (bf16[24,2048]{1,0:T(8,128)(2,1)S(1)}, bf16[24,2048]{1,0:T(8,128)(2,1)S(1)}, u32[]{:S(2)}, u32[]{:S(2)}) collective-permute-start(bf16[24,2048]{1,0:T(8,128)(2,1)S(1)} %get-tuple-element.29), channel_id=1, source_target_pairs={{0,2},{1,5},{2,0},{3,7},{4,6},{5,1},{6,4},{7,3},{8,10},{9,13},{10,... | collective-permute-start | bytes 294920 | tf_op jit(solution)/shard_map/ppermute | solution.py:24
  28.8 1.2 %collective-permute-start.13 = (bf16[24,2048]{1,0:T(8,128)(2,1)S(1)}, bf16[24,2048]{1,0:T(8,128)(2,1)S(1)}, u32[]{:S(2)}, u32[]{:S(2)}) collective-permute-start(bf16[24,2048]{1,0:T(8,128)(2,1)S(1)} %get-tuple-element.30), channel_id=1, source_target_pairs={{0,4},{1,3},{2,6},{3,1},{4,0},{5,7},{6,2},{7,5},{8,12},{9,11},{10,... | collective-permute-start | bytes 294920 | tf_op jit(solution)/shard_map/ppermute | solution.py:24
  30.0 0.1 select_reduce_fusion
  30.1 0.8 %collective-permute-start.10 = (bf16[8,2048]{1,0:T(8,128)(2,1)S(1)}, bf16[8,2048]{1,0:T(8,128)(2,1)S(1)}, u32[]{:S(2)}, u32[]{:S(2)}) collective-permute-start(bf16[8,2048]{1,0:T(8,128)(2,1)S(1)} %get-tuple-element.26), channel_id=1, source_target_pairs={{0,4},{1,3},{2,6},{3,1},{4,0},{5,7},{6,2},{7,5},{8,12},{9,11},{10,... | collective-permute-start | bytes 98312 | tf_op jit(solution)/shard_map/ppermute | solution.py:24
  30.9 1.8 %collective-permute-start.8 = (bf16[8,2048]{1,0:T(8,128)(2,1)S(1)}, bf16[8,2048]{1,0:T(8,128)(2,1)S(1)}, u32[]{:S(2)}, u32[]{:S(2)}) collective-permute-start(bf16[8,2048]{1,0:T(8,128)(2,1)S(1)} %get-tuple-element.24), channel_id=1, source_target_pairs={{0,6},{1,7},{2,4},{3,5},{4,2},{5,3},{6,0},{7,1},{8,14},{9,15},{10,... | collective-permute-start | bytes 98312 | tf_op jit(solution)/shard_map/ppermute | solution.py:24
  32.7 1.0 %collective-permute-start.9 = (bf16[8,2048]{1,0:T(8,128)(2,1)S(1)}, bf16[8,2048]{1,0:T(8,128)(2,1)S(1)}, u32[]{:S(2)}, u32[]{:S(2)}) collective-permute-start(bf16[8,2048]{1,0:T(8,128)(2,1)S(1)} %get-tuple-element.25), channel_id=1, source_target_pairs={{0,2},{1,5},{2,0},{3,7},{4,6},{5,1},{6,4},{7,3},{8,10},{9,13},{10,... | collective-permute-start | bytes 98312 | tf_op jit(solution)/shard_map/ppermute | solution.py:24
  33.7 0.0 collective-permute-done.12
  33.7 0.1 collective-permute-done.13
  33.9 0.1 collective-permute-start.14
  33.9 1.3 %collective-permute-start.15 = (bf16[8,2048]{1,0:T(8,128)(2,1)S(1)}, bf16[8,2048]{1,0:T(8,128)(2,1)S(1)}, u32[]{:S(2)}, u32[]{:S(2)}) collective-permute-start(bf16[8,2048]{1,0:T(8,128)(2,1)S(1)} %get-tuple-element.33), channel_id=1, source_target_pairs={{0,16},{1,17},{2,18},{3,19},{4,20},{5,21},{6,22},{7,23},{8,24},{9,... | collective-permute-start | bytes 98312 | tf_op jit(solution)/shard_map/ppermute | solution.py:16
  35.3 3.0 %collective-permute-start.16 = (bf16[8,2048]{1,0:T(8,128)(2,1)S(1)}, bf16[8,2048]{1,0:T(8,128)(2,1)S(1)}, u32[]{:S(2)}, u32[]{:S(2)}) collective-permute-start(bf16[8,2048]{1,0:T(8,128)(2,1)S(1)} %get-tuple-element.32), channel_id=1, source_target_pairs={{0,24},{1,25},{2,26},{3,27},{4,28},{5,29},{6,30},{7,31},{8,16},{9,... | collective-permute-start | bytes 98312 | tf_op jit(solution)/shard_map/ppermute | solution.py:16
  38.3 0.5 %collective-permute-done.15 = bf16[8,2048]{1,0:T(8,128)(2,1)S(1)} collective-permute-done((bf16[8,2048]{1,0:T(8,128)(2,1)S(1)}, bf16[8,2048]{1,0:T(8,128)(2,1)S(1)}, u32[]{:S(2)}, u32[]{:S(2)}) %collective-permute-start.15) | collective-permute-done | bytes 32800 | tf_op jit(solution)/shard_map/ppermute | solution.py:16
  38.8 2.2 %collective-permute-done.16 = bf16[8,2048]{1,0:T(8,128)(2,1)S(1)} collective-permute-done((bf16[8,2048]{1,0:T(8,128)(2,1)S(1)}, bf16[8,2048]{1,0:T(8,128)(2,1)S(1)}, u32[]{:S(2)}, u32[]{:S(2)}) %collective-permute-start.16) | collective-permute-done | bytes 32800 | tf_op jit(solution)/shard_map/ppermute | solution.py:16
  41.0 0.7 %add_convert_fusion.1 = bf16[8,2048]{1,0:T(8,128)(2,1)} fusion(bf16[8,2048]{1,0:T(8,128)(2,1)S(1)} %collective-permute-done.16, bf16[8,2048]{1,0:T(8,128)(2,1)S(1)} %collective-permute-done.15, bf16[8,2048]{1,0:T(8,128)(2,1)S(1)} %collective-permute-done.14, f32[8,2048]{1,0:T(8,128)S(1)} %get-tuple-element.19, ...), kind=kLoop, calls=%fused_computation.1 | loop fusion | flops 294912 | bytes 360576 | tf_op jit(solution)/shard_map/convert_element_type | solution.py:290
  (19 shorter events, 0.1 us)
Async XLA Ops:
  3.2 21.9 %collective-permute-start.6 = (bf16[2048,512]{1,0:T(8,128)(2,1)S(1)}, bf16[2048,512]{1,0:T(8,128)(2,1)S(1)}, u32[]{:S(2)}, u32[]{:S(2)}) collective-permute-start(bf16[2048,512]{1,0:T(8,128)(2,1)S(1)} %get-tuple-element.22.refs_4_), channel_id=1, source_target_pairs={{0,1},{1,0},{2,3},{3,2},{4,5},{5,4},{6,7},{7,6},{8,9},{9,8},{10,11... | collective-permute-start | bytes 6291464 | tf_op jit(solution)/shard_map/ppermute | solution.py:16
  5.3 19.8 %collective-permute-start.7 = (bf16[512,2048]{1,0:T(8,128)(2,1)S(1)}, bf16[512,2048]{1,0:T(8,128)(2,1)S(1)}, u32[]{:S(2)}, u32[]{:S(2)}) collective-permute-start(bf16[512,2048]{1,0:T(8,128)(2,1)S(1)} %shard_map.101.refs_5_), channel_id=1, source_target_pairs={{0,1},{1,0},{2,3},{3,2},{4,5},{5,4},{6,7},{7,6},{8,9},{9,8},{10,11... | collective-permute-start | bytes 6291464 | tf_op jit(solution)/shard_map/ppermute | solution.py:16
  5.4 5.7 %collective-permute-start = (bf16[8,2048]{1,0:T(8,128)(2,1)S(1)}, bf16[8,2048]{1,0:T(8,128)(2,1)S(1)}, u32[]{:S(2)}, u32[]{:S(2)}) collective-permute-start(bf16[8,2048]{1,0:T(8,128)(2,1)S(1)} %get-tuple-element.21), channel_id=1, source_target_pairs={{0,8},{1,9},{2,10},{3,11},{4,12},{5,13},{6,14},{7,15},{8,0},{9,1},... | collective-permute-start | bytes 98312 | tf_op jit(solution)/shard_map/ppermute | solution.py:16
  8.5 5.4 %collective-permute-start.1 = (bf16[8,2048]{1,0:T(8,128)(2,1)S(1)}, bf16[8,2048]{1,0:T(8,128)(2,1)S(1)}, u32[]{:S(2)}, u32[]{:S(2)}) collective-permute-start(bf16[8,2048]{1,0:T(8,128)(2,1)S(1)} %get-tuple-element.21), channel_id=1, source_target_pairs={{0,16},{1,17},{2,18},{3,19},{4,20},{5,21},{6,22},{7,23},{8,24},{9,... | collective-permute-start | bytes 98312 | tf_op jit(solution)/shard_map/ppermute | solution.py:16
  11.1 5.7 %collective-permute-start.2 = (bf16[8,2048]{1,0:T(8,128)(2,1)S(1)}, bf16[8,2048]{1,0:T(8,128)(2,1)S(1)}, u32[]{:S(2)}, u32[]{:S(2)}) collective-permute-start(bf16[8,2048]{1,0:T(8,128)(2,1)S(1)} %get-tuple-element.21), channel_id=1, source_target_pairs={{0,24},{1,25},{2,26},{3,27},{4,28},{5,29},{6,30},{7,31},{8,16},{9,... | collective-permute-start | bytes 98312 | tf_op jit(solution)/shard_map/ppermute | solution.py:16
  16.8 7.2 %collective-permute-start.3 = (bf16[32,2048]{1,0:T(8,128)(2,1)S(1)}, bf16[32,2048]{1,0:T(8,128)(2,1)S(1)}, u32[]{:S(2)}, u32[]{:S(2)}) collective-permute-start(bf16[32,2048]{1,0:T(8,128)(2,1)S(1)} %constant_dynamic-update-slice_fusion.refs_0_), channel_id=1, source_target_pairs={{0,6},{1,7},{2,4},{3,5},{4,2},{5,3},{6,0},{7,1},{8,14},{9,15},{10,... | collective-permute-start | bytes 393224 | tf_op jit(solution)/shard_map/ppermute | solution.py:24
  19.2 5.1 %collective-permute-start.4 = (bf16[32,2048]{1,0:T(8,128)(2,1)S(1)}, bf16[32,2048]{1,0:T(8,128)(2,1)S(1)}, u32[]{:S(2)}, u32[]{:S(2)}) collective-permute-start(bf16[32,2048]{1,0:T(8,128)(2,1)S(1)} %constant_dynamic-update-slice_fusion.refs_0_), channel_id=1, source_target_pairs={{0,2},{1,5},{2,0},{3,7},{4,6},{5,1},{6,4},{7,3},{8,10},{9,13},{10,... | collective-permute-start | bytes 393224 | tf_op jit(solution)/shard_map/ppermute | solution.py:24
  19.8 5.3 %collective-permute-start.5 = (bf16[32,2048]{1,0:T(8,128)(2,1)S(1)}, bf16[32,2048]{1,0:T(8,128)(2,1)S(1)}, u32[]{:S(2)}, u32[]{:S(2)}) collective-permute-start(bf16[32,2048]{1,0:T(8,128)(2,1)S(1)} %constant_dynamic-update-slice_fusion.refs_0_), channel_id=1, source_target_pairs={{0,4},{1,3},{2,6},{3,1},{4,0},{5,7},{6,2},{7,5},{8,12},{9,11},{10,... | collective-permute-start | bytes 393224 | tf_op jit(solution)/shard_map/ppermute | solution.py:24
  20.3 9.8 %copy-start = (f32[8,2]{0,1:T(2,128)S(1)}, f32[8,2]{0,1:T(2,128)}, u32[]{:S(2)}) copy-start(f32[8,2]{0,1:T(2,128)} %param.19) | copy-start | bytes 196
  20.3 9.8 %copy-start.1 = (s32[8,2]{0,1:T(2,128)S(1)}, s32[8,2]{0,1:T(2,128)}, u32[]{:S(2)}) copy-start(s32[8,2]{0,1:T(2,128)} %param.18) | copy-start | bytes 196
  26.5 6.2 %collective-permute-start.11 = (bf16[24,2048]{1,0:T(8,128)(2,1)S(1)}, bf16[24,2048]{1,0:T(8,128)(2,1)S(1)}, u32[]{:S(2)}, u32[]{:S(2)}) collective-permute-start(bf16[24,2048]{1,0:T(8,128)(2,1)S(1)} %get-tuple-element.28), channel_id=1, source_target_pairs={{0,6},{1,7},{2,4},{3,5},{4,2},{5,3},{6,0},{7,1},{8,14},{9,15},{10,... | collective-permute-start | bytes 294920 | tf_op jit(solution)/shard_map/ppermute | solution.py:24
  28.2 5.5 %collective-permute-start.12 = (bf16[24,2048]{1,0:T(8,128)(2,1)S(1)}, bf16[24,2048]{1,0:T(8,128)(2,1)S(1)}, u32[]{:S(2)}, u32[]{:S(2)}) collective-permute-start(bf16[24,2048]{1,0:T(8,128)(2,1)S(1)} %get-tuple-element.29), channel_id=1, source_target_pairs={{0,2},{1,5},{2,0},{3,7},{4,6},{5,1},{6,4},{7,3},{8,10},{9,13},{10,... | collective-permute-start | bytes 294920 | tf_op jit(solution)/shard_map/ppermute | solution.py:24
  28.8 5.0 %collective-permute-start.13 = (bf16[24,2048]{1,0:T(8,128)(2,1)S(1)}, bf16[24,2048]{1,0:T(8,128)(2,1)S(1)}, u32[]{:S(2)}, u32[]{:S(2)}) collective-permute-start(bf16[24,2048]{1,0:T(8,128)(2,1)S(1)} %get-tuple-element.30), channel_id=1, source_target_pairs={{0,4},{1,3},{2,6},{3,1},{4,0},{5,7},{6,2},{7,5},{8,12},{9,11},{10,... | collective-permute-start | bytes 294920 | tf_op jit(solution)/shard_map/ppermute | solution.py:24
  30.1 5.2 %collective-permute-start.10 = (bf16[8,2048]{1,0:T(8,128)(2,1)S(1)}, bf16[8,2048]{1,0:T(8,128)(2,1)S(1)}, u32[]{:S(2)}, u32[]{:S(2)}) collective-permute-start(bf16[8,2048]{1,0:T(8,128)(2,1)S(1)} %get-tuple-element.26), channel_id=1, source_target_pairs={{0,4},{1,3},{2,6},{3,1},{4,0},{5,7},{6,2},{7,5},{8,12},{9,11},{10,... | collective-permute-start | bytes 98312 | tf_op jit(solution)/shard_map/ppermute | solution.py:24
  30.9 7.4 %collective-permute-start.8 = (bf16[8,2048]{1,0:T(8,128)(2,1)S(1)}, bf16[8,2048]{1,0:T(8,128)(2,1)S(1)}, u32[]{:S(2)}, u32[]{:S(2)}) collective-permute-start(bf16[8,2048]{1,0:T(8,128)(2,1)S(1)} %get-tuple-element.24), channel_id=1, source_target_pairs={{0,6},{1,7},{2,4},{3,5},{4,2},{5,3},{6,0},{7,1},{8,14},{9,15},{10,... | collective-permute-start | bytes 98312 | tf_op jit(solution)/shard_map/ppermute | solution.py:24
  32.7 5.6 %collective-permute-start.9 = (bf16[8,2048]{1,0:T(8,128)(2,1)S(1)}, bf16[8,2048]{1,0:T(8,128)(2,1)S(1)}, u32[]{:S(2)}, u32[]{:S(2)}) collective-permute-start(bf16[8,2048]{1,0:T(8,128)(2,1)S(1)} %get-tuple-element.25), channel_id=1, source_target_pairs={{0,2},{1,5},{2,0},{3,7},{4,6},{5,1},{6,4},{7,3},{8,10},{9,13},{10,... | collective-permute-start | bytes 98312 | tf_op jit(solution)/shard_map/ppermute | solution.py:24
  33.9 4.5 %collective-permute-start.14 = (bf16[8,2048]{1,0:T(8,128)(2,1)S(1)}, bf16[8,2048]{1,0:T(8,128)(2,1)S(1)}, u32[]{:S(2)}, u32[]{:S(2)}) collective-permute-start(bf16[8,2048]{1,0:T(8,128)(2,1)S(1)} %get-tuple-element.31), channel_id=1, source_target_pairs={{0,8},{1,9},{2,10},{3,11},{4,12},{5,13},{6,14},{7,15},{8,0},{9,1},... | collective-permute-start | bytes 98312 | tf_op jit(solution)/shard_map/ppermute | solution.py:16
  33.9 4.9 %collective-permute-start.15 = (bf16[8,2048]{1,0:T(8,128)(2,1)S(1)}, bf16[8,2048]{1,0:T(8,128)(2,1)S(1)}, u32[]{:S(2)}, u32[]{:S(2)}) collective-permute-start(bf16[8,2048]{1,0:T(8,128)(2,1)S(1)} %get-tuple-element.33), channel_id=1, source_target_pairs={{0,16},{1,17},{2,18},{3,19},{4,20},{5,21},{6,22},{7,23},{8,24},{9,... | collective-permute-start | bytes 98312 | tf_op jit(solution)/shard_map/ppermute | solution.py:16
  35.3 5.7 %collective-permute-start.16 = (bf16[8,2048]{1,0:T(8,128)(2,1)S(1)}, bf16[8,2048]{1,0:T(8,128)(2,1)S(1)}, u32[]{:S(2)}, u32[]{:S(2)}) collective-permute-start(bf16[8,2048]{1,0:T(8,128)(2,1)S(1)} %get-tuple-element.32), channel_id=1, source_target_pairs={{0,24},{1,25},{2,26},{3,27},{4,28},{5,29},{6,30},{7,31},{8,16},{9,... | collective-permute-start | bytes 98312 | tf_op jit(solution)/shard_map/ppermute | solution.py:16

commit v9 on v8

--- a/solution.py
+++ b/solution.py
@@ -253,9 +253,11 @@
     w_out = bring(w_out)
     other_out = swap(w_out, 1, devices)
     height = near[0].shape[0]
+    nearer = experts_count // 2
     cuts = [("reduce_chip", 0, height)]
     if direct:
-        cuts = [("reduce_chip", capacity, height), ("reduce_own", 0, capacity)]
+        split = nearer * capacity
+        cuts = [("reduce_chip", split, height), ("reduce_own", 0, split)]
     parts = feed_forward(
         [near[step] for step in range(chips)],
         [(w_in, w_out), (other_in, other_out)],
@@ -267,15 +269,15 @@
         for step in range(1, chips):
             given = chip_swap(parts[step][place], step, devices)
             sums[name] = sums[name] + given.astype(jnp.float32)
-    total = sums["reduce_chip"].reshape(-1, capacity, width)
+    total = [sums[name].reshape(-1, capacity, width) for name, _, _ in cuts[::-1]]
+    total = [rows[k] for rows in total for k in range(rows.shape[0])]
+    sent = [rows.astype(jnp.bfloat16) for rows in total]
     result = mixed
-    sent = total.astype(jnp.bfloat16)
     if direct:
-        back = {k: swap(sent[k - 1], k * SPLIT, devices) for k in distances}
-        parts = [sums["reduce_own"]]
-        parts += [back[k].astype(jnp.float32) for k in range(1, experts_count)]
+        back = {k: swap(sent[k], k * SPLIT, devices) for k in distances}
+        parts = [total[0]] + [back[k].astype(jnp.float32) for k in range(1, experts_count)]
     else:
-        back = outer_exchange([sent[k] for k in range(experts_count)], devices)
+        back = outer_exchange(sent, devices)
         parts = [part.astype(jnp.float32) for part in back]
     for k, part in enumerate(parts):
         if capacity < streams:

time: 41.9 us -> 42.4 us (1.012)
  waiting for transfers between devices: 13.2 us -> 16.5 us
  starting transfers between devices: 21.4 us -> 18.6 us
    ppermute x9, waiting for transfers between devices: 4.88 us -> 7.92 us  [chip_swap(): return lax.ppermute(value, 'expert', pairs)]
    ppermute x8, starting transfers between devices: 10.7 us -> 8.06 us  [swap(): return lax.ppermute(value, 'expert', pairs)]
  transfers between devices with their start and end apart: 17 -> 17, of which waited for: 8 -> 11; matrix products, arithmetic and copies ran while one was open for 0% -> 0% of each run, Pallas kernels for 4% -> 4%
where the time goes in v9:
time: 42.4 us; the launch traced here: 42.2 us
  starting transfers between devices  18.6 us (44%)
  waiting for transfers between devices  16.5 us (39%)
  Pallas kernels  6.13 us (14%)
  other arithmetic  0.85 us (2%)
    ppermute x9, starting transfers between devices, chip_swap(): return lax.ppermute(value, 'expert', pairs)  10.5 us
    ppermute x8, waiting for transfers between devices, swap(): return lax.ppermute(value, 'expert', pairs)  8.63 us
    ppermute x8, starting transfers between devices, swap(): return lax.ppermute(value, 'expert', pairs)  8.06 us
    ppermute x9, waiting for transfers between devices, chip_swap(): return lax.ppermute(value, 'expert', pairs)  7.92 us
    pallas_call x1, Pallas kernels, attend(): pl.pallas_call(attend_kernel, out_shape=(pltpu.VMEM((streams, width), jnp...  3.16 us
    pallas_call x1, Pallas kernels, bring(): pl.pallas_call(kernel, out_shape=pltpu.VMEM(array.shape, array.dtype), in...  1.6 us
    pallas_call x1, Pallas kernels, feed_forward(): pl.pallas_call(kernel, out_shape=[jax.ShapeDtypeStruct((end - start, widt...  1.37 us
  transfers between devices with their start and end apart: 17, of which 11 were waited for; matrix products, arithmetic and copies ran while one was open for 0% of the time, Pallas kernels for 4%

profile of v9, /device:TPU:0, one launch (start us, length us, event | category | flops | bytes accessed | tf_op | source)
XLA Modules:
  0.0 42.2 jit_solution(14541212159906130569)
XLA Ops:
  0.0 3.2 %shard_map.100 = (f32[8,2048]{1,0:T(8,128)S(1)}, bf16[8,2048]{1,0:T(8,128)(2,1)S(1)}, bf16[2048,512]{1,0:T(8,128)(2,1)S(1)}) custom-call(s32[8]{0:T(128)} %lengths_in, bf16[8,2048]{1,0:T(8,128)(2,1)} %hidden_in.1, bf16[8,2048]{1,0:T(8,128)(2,1)} %query_in.1, bf16[8,64,2048]{2,1,0:T(8,128)(2,1)} %keys.1, bf16[8,64,2048]{2,1,0:T(8,128)(2,1)} %values.1, ...), custom_call_target="tpu_custom_call" | custom-call | tf_op jit(solution)/shard_map/pallas_call | solution.py:117
  3.2 0.6 %collective-permute-start.6 = (bf16[2048,512]{1,0:T(8,128)(2,1)S(1)}, bf16[2048,512]{1,0:T(8,128)(2,1)S(1)}, u32[]{:S(2)}, u32[]{:S(2)}) collective-permute-start(bf16[2048,512]{1,0:T(8,128)(2,1)S(1)} %get-tuple-element.22.refs_4_), channel_id=1, source_target_pairs={{0,1},{1,0},{2,3},{3,2},{4,5},{5,4},{6,7},{7,6},{8,9},{9,8},{10,11... | collective-permute-start | bytes 6291464 | tf_op jit(solution)/shard_map/ppermute | solution.py:16
  3.7 1.6 %shard_map.101.refs_5_ = bf16[512,2048]{1,0:T(8,128)(2,1)S(1)} custom-call(bf16[512,2048]{1,0:T(8,128)(2,1)} %source.1), custom_call_target="tpu_custom_call" | custom-call | tf_op jit(solution)/shard_map/pallas_call | solution.py:148
  5.3 0.1 collective-permute-start.7
  5.4 3.1 %collective-permute-start = (bf16[8,2048]{1,0:T(8,128)(2,1)S(1)}, bf16[8,2048]{1,0:T(8,128)(2,1)S(1)}, u32[]{:S(2)}, u32[]{:S(2)}) collective-permute-start(bf16[8,2048]{1,0:T(8,128)(2,1)S(1)} %get-tuple-element.21), channel_id=1, source_target_pairs={{0,8},{1,9},{2,10},{3,11},{4,12},{5,13},{6,14},{7,15},{8,0},{9,1},... | collective-permute-start | bytes 98312 | tf_op jit(solution)/shard_map/ppermute | solution.py:16
  8.5 2.6 %collective-permute-start.1 = (bf16[8,2048]{1,0:T(8,128)(2,1)S(1)}, bf16[8,2048]{1,0:T(8,128)(2,1)S(1)}, u32[]{:S(2)}, u32[]{:S(2)}) collective-permute-start(bf16[8,2048]{1,0:T(8,128)(2,1)S(1)} %get-tuple-element.21), channel_id=1, source_target_pairs={{0,16},{1,17},{2,18},{3,19},{4,20},{5,21},{6,22},{7,23},{8,24},{9,... | collective-permute-start | bytes 98312 | tf_op jit(solution)/shard_map/ppermute | solution.py:16
  11.1 2.8 %collective-permute-done.1 = bf16[8,2048]{1,0:T(8,128)(2,1)S(1)} collective-permute-done((bf16[8,2048]{1,0:T(8,128)(2,1)S(1)}, bf16[8,2048]{1,0:T(8,128)(2,1)S(1)}, u32[]{:S(2)}, u32[]{:S(2)}) %collective-permute-start.1) | collective-permute-done | bytes 32800 | tf_op jit(solution)/shard_map/ppermute | solution.py:16
  13.9 2.9 %collective-permute-done.2 = bf16[8,2048]{1,0:T(8,128)(2,1)S(1)} collective-permute-done((bf16[8,2048]{1,0:T(8,128)(2,1)S(1)}, bf16[8,2048]{1,0:T(8,128)(2,1)S(1)}, u32[]{:S(2)}, u32[]{:S(2)}) %collective-permute-start.2) | collective-permute-done | bytes 32800 | tf_op jit(solution)/shard_map/ppermute | solution.py:16
  16.8 2.4 %collective-permute-start.3 = (bf16[32,2048]{1,0:T(8,128)(2,1)S(1)}, bf16[32,2048]{1,0:T(8,128)(2,1)S(1)}, u32[]{:S(2)}, u32[]{:S(2)}) collective-permute-start(bf16[32,2048]{1,0:T(8,128)(2,1)S(1)} %constant_dynamic-update-slice_fusion.refs_0_), channel_id=1, source_target_pairs={{0,6},{1,7},{2,4},{3,5},{4,2},{5,3},{6,0},{7,1},{8,14},{9,15},{10,... | collective-permute-start | bytes 393224 | tf_op jit(solution)/shard_map/ppermute | solution.py:24
  19.2 0.5 %collective-permute-start.4 = (bf16[32,2048]{1,0:T(8,128)(2,1)S(1)}, bf16[32,2048]{1,0:T(8,128)(2,1)S(1)}, u32[]{:S(2)}, u32[]{:S(2)}) collective-permute-start(bf16[32,2048]{1,0:T(8,128)(2,1)S(1)} %constant_dynamic-update-slice_fusion.refs_0_), channel_id=1, source_target_pairs={{0,2},{1,5},{2,0},{3,7},{4,6},{5,1},{6,4},{7,3},{8,10},{9,13},{10,... | collective-permute-start | bytes 393224 | tf_op jit(solution)/shard_map/ppermute | solution.py:24
  19.8 0.5 %collective-permute-start.5 = (bf16[32,2048]{1,0:T(8,128)(2,1)S(1)}, bf16[32,2048]{1,0:T(8,128)(2,1)S(1)}, u32[]{:S(2)}, u32[]{:S(2)}) collective-permute-start(bf16[32,2048]{1,0:T(8,128)(2,1)S(1)} %constant_dynamic-update-slice_fusion.refs_0_), channel_id=1, source_target_pairs={{0,4},{1,3},{2,6},{3,1},{4,0},{5,7},{6,2},{7,5},{8,12},{9,11},{10,... | collective-permute-start | bytes 393224 | tf_op jit(solution)/shard_map/ppermute | solution.py:24
  20.3 3.7 %collective-permute-done.3.refs_1_ = bf16[32,2048]{1,0:T(8,128)(2,1)S(1)} collective-permute-done((bf16[32,2048]{1,0:T(8,128)(2,1)S(1)}, bf16[32,2048]{1,0:T(8,128)(2,1)S(1)}, u32[]{:S(2)}, u32[]{:S(2)}) %collective-permute-start.3) | collective-permute-done | bytes 131104 | tf_op jit(solution)/shard_map/ppermute | solution.py:24
  24.0 0.3 collective-permute-done.4.refs_2_
  24.3 0.7 %collective-permute-done.5.refs_3_ = bf16[32,2048]{1,0:T(8,128)(2,1)S(1)} collective-permute-done((bf16[32,2048]{1,0:T(8,128)(2,1)S(1)}, bf16[32,2048]{1,0:T(8,128)(2,1)S(1)}, u32[]{:S(2)}, u32[]{:S(2)}) %collective-permute-start.5) | collective-permute-done | bytes 131104 | tf_op jit(solution)/shard_map/ppermute | solution.py:24
  25.1 0.0 collective-permute-done.6.refs_6_
  25.1 1.4 %shard_map.102 = (f32[16,2048]{1,0:T(8,128)S(1)}, f32[16,2048]{1,0:T(8,128)S(1)}, bf16[16,2048]{1,0:T(8,128)(2,1)S(1)}, bf16[16,2048]{1,0:T(8,128)(2,1)S(1)}, bf...) custom-call(bf16[32,2048]{1,0:T(8,128)(2,1)S(1)} %constant_dynamic-u, ...), custom_call_target="tpu_custom_call" | custom-call | flops 1073741824 | bytes 8388608 | tf_op jit(solution)/shard_map/pallas_call | solution.py:180
  26.5 0.9 %collective-permute-start.14 = (bf16[16,2048]{1,0:T(8,128)(2,1)S(1)}, bf16[16,2048]{1,0:T(8,128)(2,1)S(1)}, u32[]{:S(2)}, u32[]{:S(2)}) collective-permute-start(bf16[16,2048]{1,0:T(8,128)(2,1)S(1)} %get-tuple-element.30), channel_id=1, source_target_pairs={{0,4},{1,3},{2,6},{3,1},{4,0},{5,7},{6,2},{7,5},{8,12},{9,11},{10,... | collective-permute-start | bytes 196616 | tf_op jit(solution)/shard_map/ppermute | solution.py:24
  27.3 1.4 %collective-permute-start.13 = (bf16[16,2048]{1,0:T(8,128)(2,1)S(1)}, bf16[16,2048]{1,0:T(8,128)(2,1)S(1)}, u32[]{:S(2)}, u32[]{:S(2)}) collective-permute-start(bf16[16,2048]{1,0:T(8,128)(2,1)S(1)} %get-tuple-element.29), channel_id=1, source_target_pairs={{0,2},{1,5},{2,0},{3,7},{4,6},{5,1},{6,4},{7,3},{8,10},{9,13},{10,... | collective-permute-start | bytes 196616 | tf_op jit(solution)/shard_map/ppermute | solution.py:24
  28.8 1.3 %collective-permute-start.12 = (bf16[16,2048]{1,0:T(8,128)(2,1)S(1)}, bf16[16,2048]{1,0:T(8,128)(2,1)S(1)}, u32[]{:S(2)}, u32[]{:S(2)}) collective-permute-start(bf16[16,2048]{1,0:T(8,128)(2,1)S(1)} %get-tuple-element.28), channel_id=1, source_target_pairs={{0,6},{1,7},{2,4},{3,5},{4,2},{5,3},{6,0},{7,1},{8,14},{9,15},{10,... | collective-permute-start | bytes 196616 | tf_op jit(solution)/shard_map/ppermute | solution.py:24
  30.0 0.1 select_reduce_fusion
  30.1 0.8 %collective-permute-start.10 = (bf16[16,2048]{1,0:T(8,128)(2,1)S(1)}, bf16[16,2048]{1,0:T(8,128)(2,1)S(1)}, u32[]{:S(2)}, u32[]{:S(2)}) collective-permute-start(bf16[16,2048]{1,0:T(8,128)(2,1)S(1)} %get-tuple-element.26), channel_id=1, source_target_pairs={{0,4},{1,3},{2,6},{3,1},{4,0},{5,7},{6,2},{7,5},{8,12},{9,11},{10,... | collective-permute-start | bytes 196616 | tf_op jit(solution)/shard_map/ppermute | solution.py:24
  30.9 1.4 %collective-permute-start.9 = (bf16[16,2048]{1,0:T(8,128)(2,1)S(1)}, bf16[16,2048]{1,0:T(8,128)(2,1)S(1)}, u32[]{:S(2)}, u32[]{:S(2)}) collective-permute-start(bf16[16,2048]{1,0:T(8,128)(2,1)S(1)} %get-tuple-element.25), channel_id=1, source_target_pairs={{0,2},{1,5},{2,0},{3,7},{4,6},{5,1},{6,4},{7,3},{8,10},{9,13},{10,... | collective-permute-start | bytes 196616 | tf_op jit(solution)/shard_map/ppermute | solution.py:24
  32.3 1.3 %collective-permute-start.8 = (bf16[16,2048]{1,0:T(8,128)(2,1)S(1)}, bf16[16,2048]{1,0:T(8,128)(2,1)S(1)}, u32[]{:S(2)}, u32[]{:S(2)}) collective-permute-start(bf16[16,2048]{1,0:T(8,128)(2,1)S(1)} %get-tuple-element.24), channel_id=1, source_target_pairs={{0,6},{1,7},{2,4},{3,5},{4,2},{5,3},{6,0},{7,1},{8,14},{9,15},{10,... | collective-permute-start | bytes 196616 | tf_op jit(solution)/shard_map/ppermute | solution.py:24
  33.6 0.3 collective-permute-done.12
  34.0 0.7 %collective-permute-start.16 = (bf16[8,2048]{1,0:T(8,128)(2,1)S(1)}, bf16[8,2048]{1,0:T(8,128)(2,1)S(1)}, u32[]{:S(2)}, u32[]{:S(2)}) collective-permute-start(bf16[8,2048]{1,0:T(8,128)(2,1)S(1)} %get-tuple-element.32), channel_id=1, source_target_pairs={{0,24},{1,25},{2,26},{3,27},{4,28},{5,29},{6,30},{7,31},{8,16},{9,... | collective-permute-start | bytes 98312 | tf_op jit(solution)/shard_map/ppermute | solution.py:16
  34.8 0.4 collective-permute-done.9
  35.2 2.3 %collective-permute-done.8 = bf16[16,2048]{1,0:T(8,128)(2,1)S(1)} collective-permute-done((bf16[16,2048]{1,0:T(8,128)(2,1)S(1)}, bf16[16,2048]{1,0:T(8,128)(2,1)S(1)}, u32[]{:S(2)}, u32[]{:S(2)}) %collective-permute-start.8) | collective-permute-done | bytes 65568 | tf_op jit(solution)/shard_map/ppermute | solution.py:24
  37.6 1.0 %collective-permute-start.11 = (bf16[8,2048]{1,0:T(8,128)(2,1)S(1)}, bf16[8,2048]{1,0:T(8,128)(2,1)S(1)}, u32[]{:S(2)}, u32[]{:S(2)}) collective-permute-start(bf16[8,2048]{1,0:T(8,128)(2,1)S(1)} %slice.59), channel_id=1, source_target_pairs={{0,8},{1,9},{2,10},{3,11},{4,12},{5,13},{6,14},{7,15},{8,0},{9,1},... | collective-permute-start | bytes 98312 | tf_op jit(solution)/shard_map/ppermute | solution.py:16
  38.6 1.3 %collective-permute-done.16 = bf16[8,2048]{1,0:T(8,128)(2,1)S(1)} collective-permute-done((bf16[8,2048]{1,0:T(8,128)(2,1)S(1)}, bf16[8,2048]{1,0:T(8,128)(2,1)S(1)}, u32[]{:S(2)}, u32[]{:S(2)}) %collective-permute-start.16) | collective-permute-done | bytes 32800 | tf_op jit(solution)/shard_map/ppermute | solution.py:16
  39.9 0.4 collective-permute-done.15
  40.3 1.3 %collective-permute-done.11 = bf16[8,2048]{1,0:T(8,128)(2,1)S(1)} collective-permute-done((bf16[8,2048]{1,0:T(8,128)(2,1)S(1)}, bf16[8,2048]{1,0:T(8,128)(2,1)S(1)}, u32[]{:S(2)}, u32[]{:S(2)}) %collective-permute-start.11) | collective-permute-done | bytes 32800 | tf_op jit(solution)/shard_map/ppermute | solution.py:16
  41.5 0.7 %fusion.4 = bf16[8,2048]{1,0:T(8,128)(2,1)} fusion(f32[8,2048]{1,0:T(8,128)S(1)} %get-tuple-element.19, f32[16,2048]{1,0:T(8,128)S(1)} %convert_add_fusion, bf16[8,2048]{1,0:T(8,128)(2,1)S(1)} %collective-permute-done.16, bf16[8,2048]{1,0:T(8,128)(2,1)S(1)} %collective-permute-done.15, bf16[8,2048]{1,0:T(8,128)(2,1)S(1)} %collective-permute-done.11, ...), kind=kLoop, calls=%fused_computation.8 | loop fusion | flops 196608 | bytes 262272 | tf_op jit(solution)/shard_map/convert_element_type | solution.py:292
  (21 shorter events, 0.1 us)
Async XLA Ops:
  3.2 21.9 %collective-permute-start.6 = (bf16[2048,512]{1,0:T(8,128)(2,1)S(1)}, bf16[2048,512]{1,0:T(8,128)(2,1)S(1)}, u32[]{:S(2)}, u32[]{:S(2)}) collective-permute-start(bf16[2048,512]{1,0:T(8,128)(2,1)S(1)} %get-tuple-element.22.refs_4_), channel_id=1, source_target_pairs={{0,1},{1,0},{2,3},{3,2},{4,5},{5,4},{6,7},{7,6},{8,9},{9,8},{10,11... | collective-permute-start | bytes 6291464 | tf_op jit(solution)/shard_map/ppermute | solution.py:16
  5.3 19.8 %collective-permute-start.7 = (bf16[512,2048]{1,0:T(8,128)(2,1)S(1)}, bf16[512,2048]{1,0:T(8,128)(2,1)S(1)}, u32[]{:S(2)}, u32[]{:S(2)}) collective-permute-start(bf16[512,2048]{1,0:T(8,128)(2,1)S(1)} %shard_map.101.refs_5_), channel_id=1, source_target_pairs={{0,1},{1,0},{2,3},{3,2},{4,5},{5,4},{6,7},{7,6},{8,9},{9,8},{10,11... | collective-permute-start | bytes 6291464 | tf_op jit(solution)/shard_map/ppermute | solution.py:16
  5.4 5.7 %collective-permute-start = (bf16[8,2048]{1,0:T(8,128)(2,1)S(1)}, bf16[8,2048]{1,0:T(8,128)(2,1)S(1)}, u32[]{:S(2)}, u32[]{:S(2)}) collective-permute-start(bf16[8,2048]{1,0:T(8,128)(2,1)S(1)} %get-tuple-element.21), channel_id=1, source_target_pairs={{0,8},{1,9},{2,10},{3,11},{4,12},{5,13},{6,14},{7,15},{8,0},{9,1},... | collective-permute-start | bytes 98312 | tf_op jit(solution)/shard_map/ppermute | solution.py:16
  8.5 5.4 %collective-permute-start.1 = (bf16[8,2048]{1,0:T(8,128)(2,1)S(1)}, bf16[8,2048]{1,0:T(8,128)(2,1)S(1)}, u32[]{:S(2)}, u32[]{:S(2)}) collective-permute-start(bf16[8,2048]{1,0:T(8,128)(2,1)S(1)} %get-tuple-element.21), channel_id=1, source_target_pairs={{0,16},{1,17},{2,18},{3,19},{4,20},{5,21},{6,22},{7,23},{8,24},{9,... | collective-permute-start | bytes 98312 | tf_op jit(solution)/shard_map/ppermute | solution.py:16
  11.1 5.7 %collective-permute-start.2 = (bf16[8,2048]{1,0:T(8,128)(2,1)S(1)}, bf16[8,2048]{1,0:T(8,128)(2,1)S(1)}, u32[]{:S(2)}, u32[]{:S(2)}) collective-permute-start(bf16[8,2048]{1,0:T(8,128)(2,1)S(1)} %get-tuple-element.21), channel_id=1, source_target_pairs={{0,24},{1,25},{2,26},{3,27},{4,28},{5,29},{6,30},{7,31},{8,16},{9,... | collective-permute-start | bytes 98312 | tf_op jit(solution)/shard_map/ppermute | solution.py:16
  16.8 7.2 %collective-permute-start.3 = (bf16[32,2048]{1,0:T(8,128)(2,1)S(1)}, bf16[32,2048]{1,0:T(8,128)(2,1)S(1)}, u32[]{:S(2)}, u32[]{:S(2)}) collective-permute-start(bf16[32,2048]{1,0:T(8,128)(2,1)S(1)} %constant_dynamic-update-slice_fusion.refs_0_), channel_id=1, source_target_pairs={{0,6},{1,7},{2,4},{3,5},{4,2},{5,3},{6,0},{7,1},{8,14},{9,15},{10,... | collective-permute-start | bytes 393224 | tf_op jit(solution)/shard_map/ppermute | solution.py:24
  19.2 5.1 %collective-permute-start.4 = (bf16[32,2048]{1,0:T(8,128)(2,1)S(1)}, bf16[32,2048]{1,0:T(8,128)(2,1)S(1)}, u32[]{:S(2)}, u32[]{:S(2)}) collective-permute-start(bf16[32,2048]{1,0:T(8,128)(2,1)S(1)} %constant_dynamic-update-slice_fusion.refs_0_), channel_id=1, source_target_pairs={{0,2},{1,5},{2,0},{3,7},{4,6},{5,1},{6,4},{7,3},{8,10},{9,13},{10,... | collective-permute-start | bytes 393224 | tf_op jit(solution)/shard_map/ppermute | solution.py:24
  19.8 5.3 %collective-permute-start.5 = (bf16[32,2048]{1,0:T(8,128)(2,1)S(1)}, bf16[32,2048]{1,0:T(8,128)(2,1)S(1)}, u32[]{:S(2)}, u32[]{:S(2)}) collective-permute-start(bf16[32,2048]{1,0:T(8,128)(2,1)S(1)} %constant_dynamic-update-slice_fusion.refs_0_), channel_id=1, source_target_pairs={{0,4},{1,3},{2,6},{3,1},{4,0},{5,7},{6,2},{7,5},{8,12},{9,11},{10,... | collective-permute-start | bytes 393224 | tf_op jit(solution)/shard_map/ppermute | solution.py:24
  20.3 9.8 %copy-start = (f32[8,2]{0,1:T(2,128)S(1)}, f32[8,2]{0,1:T(2,128)}, u32[]{:S(2)}) copy-start(f32[8,2]{0,1:T(2,128)} %param.19) | copy-start | bytes 196
  20.3 9.8 %copy-start.1 = (s32[8,2]{0,1:T(2,128)S(1)}, s32[8,2]{0,1:T(2,128)}, u32[]{:S(2)}) copy-start(s32[8,2]{0,1:T(2,128)} %param.18) | copy-start | bytes 196
  26.5 5.9 %collective-permute-start.14 = (bf16[16,2048]{1,0:T(8,128)(2,1)S(1)}, bf16[16,2048]{1,0:T(8,128)(2,1)S(1)}, u32[]{:S(2)}, u32[]{:S(2)}) collective-permute-start(bf16[16,2048]{1,0:T(8,128)(2,1)S(1)} %get-tuple-element.30), channel_id=1, source_target_pairs={{0,4},{1,3},{2,6},{3,1},{4,0},{5,7},{6,2},{7,5},{8,12},{9,11},{10,... | collective-permute-start | bytes 196616 | tf_op jit(solution)/shard_map/ppermute | solution.py:24
  27.3 6.3 %collective-permute-start.13 = (bf16[16,2048]{1,0:T(8,128)(2,1)S(1)}, bf16[16,2048]{1,0:T(8,128)(2,1)S(1)}, u32[]{:S(2)}, u32[]{:S(2)}) collective-permute-start(bf16[16,2048]{1,0:T(8,128)(2,1)S(1)} %get-tuple-element.29), channel_id=1, source_target_pairs={{0,2},{1,5},{2,0},{3,7},{4,6},{5,1},{6,4},{7,3},{8,10},{9,13},{10,... | collective-permute-start | bytes 196616 | tf_op jit(solution)/shard_map/ppermute | solution.py:24
  28.8 5.2 %collective-permute-start.12 = (bf16[16,2048]{1,0:T(8,128)(2,1)S(1)}, bf16[16,2048]{1,0:T(8,128)(2,1)S(1)}, u32[]{:S(2)}, u32[]{:S(2)}) collective-permute-start(bf16[16,2048]{1,0:T(8,128)(2,1)S(1)} %get-tuple-element.28), channel_id=1, source_target_pairs={{0,6},{1,7},{2,4},{3,5},{4,2},{5,3},{6,0},{7,1},{8,14},{9,15},{10,... | collective-permute-start | bytes 196616 | tf_op jit(solution)/shard_map/ppermute | solution.py:24
  30.1 4.6 %collective-permute-start.10 = (bf16[16,2048]{1,0:T(8,128)(2,1)S(1)}, bf16[16,2048]{1,0:T(8,128)(2,1)S(1)}, u32[]{:S(2)}, u32[]{:S(2)}) collective-permute-start(bf16[16,2048]{1,0:T(8,128)(2,1)S(1)} %get-tuple-element.26), channel_id=1, source_target_pairs={{0,4},{1,3},{2,6},{3,1},{4,0},{5,7},{6,2},{7,5},{8,12},{9,11},{10,... | collective-permute-start | bytes 196616 | tf_op jit(solution)/shard_map/ppermute | solution.py:24
  30.9 4.3 %collective-permute-start.9 = (bf16[16,2048]{1,0:T(8,128)(2,1)S(1)}, bf16[16,2048]{1,0:T(8,128)(2,1)S(1)}, u32[]{:S(2)}, u32[]{:S(2)}) collective-permute-start(bf16[16,2048]{1,0:T(8,128)(2,1)S(1)} %get-tuple-element.25), channel_id=1, source_target_pairs={{0,2},{1,5},{2,0},{3,7},{4,6},{5,1},{6,4},{7,3},{8,10},{9,13},{10,... | collective-permute-start | bytes 196616 | tf_op jit(solution)/shard_map/ppermute | solution.py:24
  32.3 5.2 %collective-permute-start.8 = (bf16[16,2048]{1,0:T(8,128)(2,1)S(1)}, bf16[16,2048]{1,0:T(8,128)(2,1)S(1)}, u32[]{:S(2)}, u32[]{:S(2)}) collective-permute-start(bf16[16,2048]{1,0:T(8,128)(2,1)S(1)} %get-tuple-element.24), channel_id=1, source_target_pairs={{0,6},{1,7},{2,4},{3,5},{4,2},{5,3},{6,0},{7,1},{8,14},{9,15},{10,... | collective-permute-start | bytes 196616 | tf_op jit(solution)/shard_map/ppermute | solution.py:24
  34.0 5.9 %collective-permute-start.16 = (bf16[8,2048]{1,0:T(8,128)(2,1)S(1)}, bf16[8,2048]{1,0:T(8,128)(2,1)S(1)}, u32[]{:S(2)}, u32[]{:S(2)}) collective-permute-start(bf16[8,2048]{1,0:T(8,128)(2,1)S(1)} %get-tuple-element.32), channel_id=1, source_target_pairs={{0,24},{1,25},{2,26},{3,27},{4,28},{5,29},{6,30},{7,31},{8,16},{9,... | collective-permute-start | bytes 98312 | tf_op jit(solution)/shard_map/ppermute | solution.py:16
  34.7 5.5 %collective-permute-start.15 = (bf16[8,2048]{1,0:T(8,128)(2,1)S(1)}, bf16[8,2048]{1,0:T(8,128)(2,1)S(1)}, u32[]{:S(2)}, u32[]{:S(2)}) collective-permute-start(bf16[8,2048]{1,0:T(8,128)(2,1)S(1)} %get-tuple-element.31), channel_id=1, source_target_pairs={{0,16},{1,17},{2,18},{3,19},{4,20},{5,21},{6,22},{7,23},{8,24},{9,... | collective-permute-start | bytes 98312 | tf_op jit(solution)/shard_map/ppermute | solution.py:16
  37.6 4.0 %collective-permute-start.11 = (bf16[8,2048]{1,0:T(8,128)(2,1)S(1)}, bf16[8,2048]{1,0:T(8,128)(2,1)S(1)}, u32[]{:S(2)}, u32[]{:S(2)}) collective-permute-start(bf16[8,2048]{1,0:T(8,128)(2,1)S(1)} %slice.59), channel_id=1, source_target_pairs={{0,8},{1,9},{2,10},{3,11},{4,12},{5,13},{6,14},{7,15},{8,0},{9,1},... | collective-permute-start | bytes 98312 | tf_op jit(solution)/shard_map/ppermute | solution.py:16
